TPU v7x, 32 devices: a whole 2x2x4 slice. The times are simulated.
32 devices in a mesh: dp: 16 (over z, x, core), fsdp: 2 (over y).
Axes of the slice: x: 2, y: 2, z: 4, core: 2. Of those that a mesh axis runs over, the one named last changes fastest.
Arguments:
- x_prompt: bfloat16 [2, 16, 960, 768], P(None, 'dp', 'fsdp'), may hold values from -6 to 6
- x_cont: bfloat16 [2, 16, 2, 64, 768], P(None, 'dp', 'fsdp'), may hold values from -6 to 6
- dy_prompt: bfloat16 [2, 16, 960, 768], P(None, 'dp', 'fsdp'), may hold values from -6 to 6
- dy_cont: bfloat16 [2, 16, 2, 64, 768], P(None, 'dp', 'fsdp'), may hold values from -6 to 6
- ln1_gain: bfloat16 [768], P(('dp', 'fsdp')), may hold values from 0.5 to 1.5
- ln1_bias: bfloat16 [768], P(('dp', 'fsdp')), may hold values from -3 to 3
- w_qkv: bfloat16 [768, 2304], P(('dp', 'fsdp')), may hold values from -0.21875 to 0.21875
- b_qv: bfloat16 [1536], P(('dp', 'fsdp')), may hold values from -1.5 to 1.5
- w_out: bfloat16 [768, 768], P(('dp', 'fsdp')), may hold values from -1.25 to 1.25
- b_out: bfloat16 [768], P(('dp', 'fsdp')), may hold values from -3 to 3
- ln2_gain: bfloat16 [768], P(('dp', 'fsdp')), may hold values from 0.5 to 1.5
- ln2_bias: bfloat16 [768], P(('dp', 'fsdp')), may hold values from -3 to 3
- w_up: bfloat16 [768, 3072], P(('dp', 'fsdp')), may hold values from -0.21875 to 0.21875
- b_up: bfloat16 [3072], P(('dp', 'fsdp')), may hold values from -4 to 4
- w_down: bfloat16 [3072, 768], P(('dp', 'fsdp')), may hold values from -0.109375 to 0.109375
- b_down: bfloat16 [768], P(('dp', 'fsdp')), may hold values from -3 to 3
Outputs:
- y_prompt: bfloat16 [2, 16, 960, 768], P(None, 'dp', 'fsdp')
- y_cont: bfloat16 [2, 16, 2, 64, 768], P(None, 'dp', 'fsdp')
- dx_prompt: float32 [2, 16, 960, 768], P(None, 'dp', 'fsdp')
- dx_cont: float32 [2, 16, 2, 64, 768], P(None, 'dp', 'fsdp')
- grad_ln1_gain: float32 [768], P(('dp', 'fsdp'))
- grad_ln1_bias: float32 [768], P(('dp', 'fsdp'))
- grad_w_qkv: float32 [768, 2304], P(('dp', 'fsdp'))
- grad_b_qv: float32 [1536], P(('dp', 'fsdp'))
- grad_w_out: float32 [768, 768], P(('dp', 'fsdp'))
- grad_b_out: float32 [768], P(('dp', 'fsdp'))
- grad_ln2_gain: float32 [768], P(('dp', 'fsdp'))
- grad_ln2_bias: float32 [768], P(('dp', 'fsdp'))
- grad_w_up: float32 [768, 3072], P(('dp', 'fsdp'))
- grad_b_up: float32 [3072], P(('dp', 'fsdp'))
- grad_w_down: float32 [3072, 768], P(('dp', 'fsdp'))
- grad_b_down: float32 [768], P(('dp', 'fsdp'))
All inputs are finite; a program needn't handle non-finite values.
Results may differ from a plain program's by a relative error of at most 0.012.
Values may be sent and summed in bfloat16 or wider, within the bound.
No kernel may reach another device: no remote copies, remote signals or barrier semaphores. Data moves between devices by JAX's collectives and lax.ppermute only.
A program may use at most 248 MiB of HBM per device.

v0:
```python
from functools import partial

import jax
import jax.numpy as jnp
from jax import lax
from jax.experimental import pallas as pl
from jax.experimental.pallas import tpu as pltpu
from jax.sharding import PartitionSpec as P


D = 768
HEADS = 12
HEAD_DIM = 64
PROMPT = 960
CONT = 64
MICRO = 2


EPS = 1e-05
NEG = -1e30


def normalize(values, gain, shift):
    center = values - jnp.mean(values, -1, keepdims=True)
    spread = jnp.mean(center * center, -1, keepdims=True)
    return center * lax.rsqrt(spread + EPS) * gain + shift


def later_sum(values):
    return jnp.flip(jnp.cumsum(jnp.flip(values, 1), 1), 1) - values


def attend_group(inputs_g, causal, score_scale):
    query_g, key_g, value_g, penalty_g = inputs_g
    rows_here = query_g.shape[0]
    heads_q = query_g.reshape(rows_here, HEADS, HEAD_DIM)
    heads_k = key_g.reshape(-1, HEADS, HEAD_DIM)
    heads_v = value_g.reshape(-1, HEADS, HEAD_DIM)
    scores = (
        jnp.einsum("rhd,khd->hrk", heads_q, heads_k, preferred_element_type=jnp.float32)
        * score_scale
    )
    logits = jnp.where(causal[None], scores - penalty_g[None], NEG)
    highest = jnp.max(logits, -1, keepdims=True)
    raised = jnp.exp(logits - highest)
    totals = jnp.sum(raised, -1, keepdims=True)
    weights_b = (raised / totals).astype(jnp.bfloat16)
    mixture = jnp.einsum("hrk,khd->rhd", weights_b, heads_v, preferred_element_type=jnp.float32)
    return (
        mixture.reshape(rows_here, -1).astype(jnp.bfloat16),
        (highest + jnp.log(totals))[..., 0],
    )


def attend_back(inputs_g, causal, score_scale):
    query_g, key_g, value_g, penalty_g, grad_mix, log_totals = inputs_g
    rows_here = query_g.shape[0]
    heads_q = query_g.reshape(rows_here, HEADS, HEAD_DIM)
    heads_k = key_g.reshape(-1, HEADS, HEAD_DIM)
    heads_v = value_g.reshape(-1, HEADS, HEAD_DIM)
    heads_g = grad_mix.reshape(rows_here, HEADS, HEAD_DIM)
    scores = (
        jnp.einsum("rhd,khd->hrk", heads_q, heads_k, preferred_element_type=jnp.float32)
        * score_scale
    )
    logits = jnp.where(causal[None], scores - penalty_g[None], NEG)
    softmax_w = jnp.exp(logits - log_totals[..., None])
    grad_soft = jnp.einsum("rhd,khd->hrk", heads_g, heads_v, preferred_element_type=jnp.float32)
    inner_sum = jnp.sum(softmax_w * grad_soft, -1, keepdims=True)
    grad_logit = softmax_w * (grad_soft - inner_sum)
    grad_value = jnp.einsum(
        "hrk,rhd->khd", softmax_w.astype(jnp.bfloat16), heads_g, preferred_element_type=jnp.float32
    )
    grad_penalty = -jnp.sum(grad_logit, 0)
    rest_b = grad_logit[1:].astype(jnp.bfloat16)
    grad_query = (
        jnp.einsum("hrk,khd->rhd", rest_b, heads_k[:, 1:], preferred_element_type=jnp.float32)
        * score_scale
    )
    grad_key = (
        jnp.einsum("hrk,rhd->khd", rest_b, heads_q[:, 1:], preferred_element_type=jnp.float32)
        * score_scale
    )
    return (
        grad_value.reshape(-1, D),
        grad_query.reshape(rows_here, -1),
        grad_key.reshape(grad_key.shape[0], -1),
        grad_logit[0],
        grad_penalty,
    )


def spread_layer(
    x_prompt,
    x_cont,
    dy_prompt,
    dy_cont,
    ln1_gain,
    ln1_bias,
    w_qkv,
    b_qv,
    w_out,
    b_out,
    ln2_gain,
    ln2_bias,
    w_up,
    b_up,
    w_down,
    b_down,
):
    shards = (
        ln1_gain,
        ln1_bias,
        w_qkv,
        b_qv,
        w_out,
        b_out,
        ln2_gain,
        ln2_bias,
        w_up,
        b_up,
        w_down,
        b_down,
    )
    groups_here = x_prompt.shape[1]
    prompt_rows = x_prompt.shape[2]
    fsdp_count = lax.axis_size("fsdp")
    fsdp_place = lax.axis_index("fsdp")
    key_count = PROMPT + CONT
    score_scale = HEAD_DIM ** (-0.5)
    select_gain = 4.0 / (PROMPT + CONT)
    query_pos = jnp.concatenate(
        [
            fsdp_place * prompt_rows + jnp.arange(prompt_rows, dtype=jnp.int32),
            PROMPT + jnp.arange(CONT, dtype=jnp.int32),
        ]
    )
    key_pos = jnp.arange(key_count, dtype=jnp.int32)
    causal = key_pos[None, :] <= query_pos[:, None]
    chosen = (key_pos[None, :] < query_pos[:, None]) & (key_pos[None, :] > 0)
    lower_mask = (jnp.arange(fsdp_count, dtype=jnp.int32) < fsdp_place).astype(jnp.float32)
    pad_zeros = jnp.zeros((groups_here, CONT), jnp.float32)
    forward_attend = partial(attend_group, causal=causal, score_scale=score_scale)
    backward_attend = partial(attend_back, causal=causal, score_scale=score_scale)
    totals = tuple(
        (
            jnp.zeros(
                (single.shape[0] * lax.axis_size(("dp", "fsdp")),) + single.shape[1:], jnp.float32
            )
            for single in shards
        )
    )
    outputs_yp, outputs_yc, outputs_dxp, outputs_dxc = ([], [], [], [])
    for batch_index in range(MICRO):
        gathered = (
            lax.all_gather(shards[0], ("dp", "fsdp"), axis=0, tiled=True),
            lax.all_gather(shards[1], ("dp", "fsdp"), axis=0, tiled=True),
            lax.all_gather(shards[2], ("dp", "fsdp"), axis=0, tiled=True),
            lax.all_gather(shards[3], ("dp", "fsdp"), axis=0, tiled=True),
            lax.all_gather(shards[4], ("dp", "fsdp"), axis=0, tiled=True),
            lax.all_gather(shards[5], ("dp", "fsdp"), axis=0, tiled=True),
            lax.all_gather(shards[6], ("dp", "fsdp"), axis=0, tiled=True),
            lax.all_gather(shards[7], ("dp", "fsdp"), axis=0, tiled=True),
            lax.all_gather(shards[8], ("dp", "fsdp"), axis=0, tiled=True),
            lax.all_gather(shards[9], ("dp", "fsdp"), axis=0, tiled=True),
            lax.all_gather(shards[10], ("dp", "fsdp"), axis=0, tiled=True),
            lax.all_gather(shards[11], ("dp", "fsdp"), axis=0, tiled=True),
        )
        inputs_x = jnp.concatenate([x_prompt[batch_index], x_cont[batch_index][:, 0]], 1).astype(
            jnp.float32
        )
        local_rows = inputs_x.shape[1]
        flat_x = inputs_x.reshape(-1, D)
        normed_one = normalize(
            flat_x, gathered[0].astype(jnp.float32), gathered[1].astype(jnp.float32)
        ).astype(jnp.bfloat16)
        joined = jnp.dot(normed_one, gathered[2], preferred_element_type=jnp.float32)
        bias_qv = gathered[3].astype(jnp.float32)
        queries = (
            (joined[:, :D] + bias_qv[:D]).astype(jnp.bfloat16).reshape(groups_here, local_rows, D)
        )
        keys_own = joined[:, D : 2 * D].astype(jnp.bfloat16).reshape(groups_here, local_rows, D)
        values_own = (
            (joined[:, 2 * D :] + bias_qv[D:])
            .astype(jnp.bfloat16)
            .reshape(groups_here, local_rows, D)
        )
        prompt_pair = jnp.concatenate([keys_own[:, :prompt_rows], values_own[:, :prompt_rows]], 2)
        whole_kv = lax.all_gather(prompt_pair, "fsdp", axis=1, tiled=True)
        keys_all = jnp.concatenate([whole_kv[..., :D], keys_own[:, prompt_rows:]], 1)
        values_all = jnp.concatenate([whole_kv[..., D:], values_own[:, prompt_rows:]], 1)
        score_zero = (
            jnp.einsum(
                "grd,gkd->grk",
                queries[..., :HEAD_DIM],
                keys_all[..., :HEAD_DIM],
                preferred_element_type=jnp.float32,
            )
            * score_scale
        )
        select = jnp.where(chosen[None], jnp.maximum(score_zero, 0.0), 0.0)
        own_part = jnp.sum(select[:, :prompt_rows, :PROMPT], 1)
        all_parts = lax.all_gather(own_part[None], "fsdp", axis=0, tiled=True)
        prefix = jnp.sum(all_parts * lower_mask[:, None, None], 0)
        whole_sum = jnp.sum(all_parts, 0)
        select_p = select[:, :prompt_rows]
        select_c = select[:, prompt_rows:]
        penalty = select_gain * jnp.concatenate(
            [
                jnp.concatenate([prefix, pad_zeros], 1)[:, None]
                + (jnp.cumsum(select_p, 1) - select_p),
                jnp.concatenate([whole_sum, pad_zeros], 1)[:, None]
                + (jnp.cumsum(select_c, 1) - select_c),
            ],
            1,
        )
        mixture, log_totals = lax.map(forward_attend, (queries, keys_all, values_all, penalty))
        mixed_flat = mixture.reshape(-1, D)
        residual = flat_x + (
            jnp.dot(mixed_flat, gathered[4], preferred_element_type=jnp.float32)
            + gathered[5].astype(jnp.float32)
        )
        normed_two = normalize(
            residual, gathered[6].astype(jnp.float32), gathered[7].astype(jnp.float32)
        ).astype(jnp.bfloat16)
        upward = jnp.dot(normed_two, gathered[8], preferred_element_type=jnp.float32) + gathered[
            9
        ].astype(jnp.float32)
        active, gelu_back = jax.vjp(partial(jax.nn.gelu, approximate=True), upward)
        active_b = active.astype(jnp.bfloat16)
        output = residual + (
            jnp.dot(active_b, gathered[10], preferred_element_type=jnp.float32)
            + gathered[11].astype(jnp.float32)
        )
        output_b = output.astype(jnp.bfloat16).reshape(groups_here, local_rows, D)
        outputs_yp.append(output_b[:, :prompt_rows])
        outputs_yc.append(output_b[:, prompt_rows:][:, None])
        back_set = (
            lax.all_gather(shards[0], ("dp", "fsdp"), axis=0, tiled=True),
            lax.all_gather(shards[1], ("dp", "fsdp"), axis=0, tiled=True),
            lax.all_gather(shards[2], ("dp", "fsdp"), axis=0, tiled=True),
            lax.all_gather(shards[3], ("dp", "fsdp"), axis=0, tiled=True),
            lax.all_gather(shards[4], ("dp", "fsdp"), axis=0, tiled=True),
            lax.all_gather(shards[5], ("dp", "fsdp"), axis=0, tiled=True),
            lax.all_gather(shards[6], ("dp", "fsdp"), axis=0, tiled=True),
            lax.all_gather(shards[7], ("dp", "fsdp"), axis=0, tiled=True),
            lax.all_gather(shards[8], ("dp", "fsdp"), axis=0, tiled=True),
            lax.all_gather(shards[9], ("dp", "fsdp"), axis=0, tiled=True),
            lax.all_gather(shards[10], ("dp", "fsdp"), axis=0, tiled=True),
            lax.all_gather(shards[11], ("dp", "fsdp"), axis=0, tiled=True),
        )
        grad_out_y = jnp.concatenate(
            [dy_prompt[batch_index], dy_cont[batch_index][:, 0]], 1
        ).reshape(-1, D)
        grad_down = jnp.einsum(
            "rf,rd->fd", active_b, grad_out_y, preferred_element_type=jnp.float32
        )
        grad_bdown = jnp.sum(grad_out_y.astype(jnp.float32), 0)
        grad_active = jnp.einsum(
            "rd,fd->rf", grad_out_y, back_set[10], preferred_element_type=jnp.float32
        )
        grad_upward = gelu_back(grad_active)[0].astype(jnp.bfloat16)
        grad_up = jnp.einsum(
            "rd,rf->df", normed_two, grad_upward, preferred_element_type=jnp.float32
        )
        grad_bup = jnp.sum(grad_upward.astype(jnp.float32), 0)
        grad_normed = jnp.einsum(
            "rf,df->rd", grad_upward, back_set[8], preferred_element_type=jnp.float32
        )
        _, norm_back = jax.vjp(
            normalize, residual, back_set[6].astype(jnp.float32), back_set[7].astype(jnp.float32)
        )
        grad_resid, grad_gain_two, grad_shift_two = norm_back(grad_normed)
        grad_resid = grad_out_y.astype(jnp.float32) + grad_resid
        grad_branch = grad_resid.astype(jnp.bfloat16)
        grad_wout = jnp.einsum(
            "rd,re->de", mixed_flat, grad_branch, preferred_element_type=jnp.float32
        )
        grad_bout = jnp.sum(grad_branch.astype(jnp.float32), 0)
        grad_mixed = jnp.einsum(
            "re,de->rd", grad_branch, back_set[4], preferred_element_type=jnp.float32
        )
        grad_mixed = grad_mixed.astype(jnp.bfloat16).reshape(groups_here, local_rows, D)
        back_values, back_queries, back_keys, back_zero, back_penalty = lax.map(
            backward_attend, (queries, keys_all, values_all, penalty, grad_mixed, log_totals)
        )
        prefix_grad = select_gain * jnp.sum(back_penalty[:, :prompt_rows, :PROMPT], 1)
        whole_grad = select_gain * jnp.sum(back_penalty[:, prompt_rows:, :PROMPT], 1)
        spread_back = prefix_grad[None] * lower_mask[:, None, None] + whole_grad[None]
        part_grad = lax.psum_scatter(spread_back, "fsdp", scatter_dimension=0, tiled=True)[0]
        select_back = jnp.concatenate(
            [
                select_gain * later_sum(back_penalty[:, :prompt_rows])
                + jnp.concatenate([part_grad, pad_zeros], 1)[:, None],
                select_gain * later_sum(back_penalty[:, prompt_rows:]),
            ],
            1,
        )
        grad_zero = (
            back_zero + jnp.where(chosen[None] & (score_zero > 0), select_back, 0.0)
        ).astype(jnp.bfloat16)
        query_zero = (
            jnp.einsum(
                "grk,gkd->grd",
                grad_zero,
                keys_all[..., :HEAD_DIM],
                preferred_element_type=jnp.float32,
            )
            * score_scale
        )
        key_zero = (
            jnp.einsum(
                "grk,grd->gkd",
                grad_zero,
                queries[..., :HEAD_DIM],
                preferred_element_type=jnp.float32,
            )
            * score_scale
        )
        grad_queries = jnp.concatenate([query_zero, back_queries], 2)
        grad_keys = jnp.concatenate([key_zero, back_keys], 2)
        prompt_back = jnp.concatenate([grad_keys[:, :PROMPT], back_values[:, :PROMPT]], 2)
        own_back = lax.psum_scatter(
            prompt_back.astype(jnp.bfloat16), "fsdp", scatter_dimension=1, tiled=True
        ).astype(jnp.float32)
        keys_back = jnp.concatenate([own_back[..., :D], grad_keys[:, PROMPT:]], 1)
        values_back = jnp.concatenate([own_back[..., D:], back_values[:, PROMPT:]], 1)
        grad_joined = (
            jnp.concatenate([grad_queries, keys_back, values_back], 2)
            .astype(jnp.bfloat16)
            .reshape(-1, 3 * D)
        )
        grad_wqkv = jnp.einsum(
            "rd,re->de", normed_one, grad_joined, preferred_element_type=jnp.float32
        )
        grad_bqv = jnp.concatenate(
            [
                jnp.sum(grad_joined[:, :D].astype(jnp.float32), 0),
                jnp.sum(grad_joined[:, 2 * D :].astype(jnp.float32), 0),
            ]
        )
        grad_normed_one = jnp.einsum(
            "re,de->rd", grad_joined, back_set[2], preferred_element_type=jnp.float32
        )
        _, norm_back_one = jax.vjp(
            normalize, flat_x, back_set[0].astype(jnp.float32), back_set[1].astype(jnp.float32)
        )
        grad_input, grad_gain_one, grad_shift_one = norm_back_one(grad_normed_one)
        grad_input = (grad_resid + grad_input).reshape(groups_here, local_rows, D)
        outputs_dxp.append(grad_input[:, :prompt_rows])
        outputs_dxc.append(grad_input[:, prompt_rows:][:, None])
        micro_grads = (
            grad_gain_one,
            grad_shift_one,
            grad_wqkv,
            grad_bqv,
            grad_wout,
            grad_bout,
            grad_gain_two,
            grad_shift_two,
            grad_up,
            grad_bup,
            grad_down,
            grad_bdown,
        )
        totals = tuple((first + second for first, second in zip(totals, micro_grads)))
    results = (
        lax.psum_scatter(totals[0], ("dp", "fsdp"), scatter_dimension=0, tiled=True),
        lax.psum_scatter(totals[1], ("dp", "fsdp"), scatter_dimension=0, tiled=True),
        lax.psum_scatter(totals[2], ("dp", "fsdp"), scatter_dimension=0, tiled=True),
        lax.psum_scatter(totals[3], ("dp", "fsdp"), scatter_dimension=0, tiled=True),
        lax.psum_scatter(totals[4], ("dp", "fsdp"), scatter_dimension=0, tiled=True),
        lax.psum_scatter(totals[5], ("dp", "fsdp"), scatter_dimension=0, tiled=True),
        lax.psum_scatter(totals[6], ("dp", "fsdp"), scatter_dimension=0, tiled=True),
        lax.psum_scatter(totals[7], ("dp", "fsdp"), scatter_dimension=0, tiled=True),
        lax.psum_scatter(totals[8], ("dp", "fsdp"), scatter_dimension=0, tiled=True),
        lax.psum_scatter(totals[9], ("dp", "fsdp"), scatter_dimension=0, tiled=True),
        lax.psum_scatter(totals[10], ("dp", "fsdp"), scatter_dimension=0, tiled=True),
        lax.psum_scatter(totals[11], ("dp", "fsdp"), scatter_dimension=0, tiled=True),
    )
    return (
        jnp.stack(outputs_yp),
        jnp.stack(outputs_yc),
        jnp.stack(outputs_dxp),
        jnp.stack(outputs_dxc),
        results[0],
        results[1],
        results[2],
        results[3],
        results[4],
        results[5],
        results[6],
        results[7],
        results[8],
        results[9],
        results[10],
        results[11],
    )


NCONT = 2
ROWS = PROMPT + NCONT * CONT
SEQ = PROMPT + CONT
SCALE = HEAD_DIM ** (-0.5)
SELECT_GAIN = 4.0 / SEQ
PAIR = 2 * HEAD_DIM
BLOCKS = ((0, 256, 256), (256, 256, 512), (512, 256, 768), (768, 256, 1024), (1024, 64, ROWS))
TAIL = PROMPT - 768
F32 = jnp.float32
B16 = jnp.bfloat16


def mm(a, b):
    return lax.dot_general(a, b, (((1,), (0,)), ((), ())), preferred_element_type=F32)


def mm_nt(a, b):
    return lax.dot_general(a, b, (((1,), (1,)), ((), ())), preferred_element_type=F32)


def masked_half(values, half):
    lane = lax.broadcasted_iota(jnp.int32, values.shape, 1)
    return jnp.where(lane // HEAD_DIM == half, values, 0.0).astype(B16)


def block_masks(place):
    first, rows, keys = BLOCKS[place]
    key_id = lax.broadcasted_iota(jnp.int32, (keys, rows), 0)
    row_id = first + lax.broadcasted_iota(jnp.int32, (keys, rows), 1)
    visible = key_id <= row_id
    if first >= SEQ:
        visible = visible & ((key_id < PROMPT) | (key_id >= SEQ))
    chosen = visible & (key_id < row_id) & (key_id > 0)
    return visible, chosen


def split_mm(values, ones):
    high = values.astype(B16)
    low = (values - high.astype(F32)).astype(B16)
    return mm(high, ones) + mm(low, ones)


def triangle(rows, later):
    a = lax.broadcasted_iota(jnp.int32, (rows, rows), 0)
    b = lax.broadcasted_iota(jnp.int32, (rows, rows), 1)
    return jnp.where((a > b) if later else (a < b), 1.0, 0.0).astype(B16)


def forward_kernel(q_ref, k_ref, v_ref, o_ref, lse_ref, b0, b1, b2, b3, b4, vt_ref, ot_ref):
    bias_refs = (b0, b1, b2, b3, b4)
    head = pl.program_id(0)
    half = head % 2
    queries = masked_half(q_ref[...].astype(F32) * SCALE, half)

    @pl.when(head == 0)
    def _():
        carry = None
        for place, (first, rows, keys) in enumerate(BLOCKS):
            scores = mm_nt(k_ref[:keys], queries[first : first + rows])
            visible, chosen = block_masks(place)
            select = jnp.where(chosen, jnp.maximum(scores, 0.0), 0.0)
            penalty = split_mm(select, triangle(rows, False))
            if carry is not None:
                grown = jnp.zeros((keys - carry.shape[0], 1), F32)
                penalty = penalty + jnp.concatenate([carry, grown], 0)
            bias_refs[place][...] = jnp.where(visible, -SELECT_GAIN * penalty, NEG)
            if first + rows == SEQ:
                lane = lax.broadcasted_iota(jnp.int32, select.shape, 1)
                select = jnp.where(lane < TAIL, select, 0.0)
            if place + 1 < len(BLOCKS):
                total = jnp.sum(select, 1, keepdims=True)
                if carry is not None:
                    total = total + jnp.concatenate([carry, grown], 0)
                carry = total

    @pl.when(half == 0)
    def _():
        vt_ref[...] = v_ref[...].astype(F32).T.astype(B16)

    own = pl.ds(pl.multiple_of(half * HEAD_DIM, HEAD_DIM), HEAD_DIM)
    for place, (first, rows, keys) in enumerate(BLOCKS):
        logits = mm_nt(k_ref[:keys], queries[first : first + rows]) + bias_refs[place][...]
        highest = jnp.max(logits, 0, keepdims=True)
        raised = jnp.exp(logits - highest)
        total = jnp.sum(raised, 0, keepdims=True)
        mixed = mm(vt_ref[own, :keys], raised.astype(B16))
        ot_ref[own, first : first + rows] = mixed * (1.0 / total)
        lse_ref[0, :, first : first + rows] = highest + jnp.log(total)

    @pl.when(half == 1)
    def _():
        o_ref[...] = ot_ref[...].T.astype(B16)


def backward_kernel(
    q_ref, k_ref, v_ref, g_ref, lse_ref, b0, b1, b2, b3, b4,
    dq_ref, dk_ref, dv_ref,
    kt_ref, dqt_ref, dk_acc, dv_acc, p0, p1, p2, p3, p4,
):
    bias_refs = (b0, b1, b2, b3, b4)
    pen_refs = (p0, p1, p2, p3, p4)
    head = HEADS - 1 - pl.program_id(0)
    half = head % 2
    queries = masked_half(q_ref[...].astype(F32) * SCALE, half)
    grads = masked_half(g_ref[...].astype(F32), half)
    own = pl.ds(pl.multiple_of(half * HEAD_DIM, HEAD_DIM), HEAD_DIM)

    @pl.when(head == HEADS - 1)
    def _():
        for pen in pen_refs:
            pen[...] = jnp.zeros_like(pen)

    @pl.when(half == 1)
    def _():
        kt_ref[...] = k_ref[...].astype(F32).T.astype(B16)
        dk_acc[...] = jnp.zeros_like(dk_acc)
        dv_acc[...] = jnp.zeros_like(dv_acc)

    def softmax_grad(place):
        first, rows, keys = BLOCKS[place]
        scores = mm_nt(k_ref[:keys], queries[first : first + rows])
        shares = jnp.exp(scores + bias_refs[place][...] - lse_ref[0, :, first : first + rows])
        back = mm_nt(v_ref[:keys], grads[first : first + rows])
        inner = jnp.sum(shares * back, 0, keepdims=True)
        dv_acc[:keys] += mm(shares.astype(B16), grads[first : first + rows])
        return scores, shares * (back - inner)

    def score_grad(place, grad):
        first, rows, keys = BLOCKS[place]
        grad = grad.astype(B16)
        dqt_ref[own, first : first + rows] = mm(kt_ref[own, :keys], grad)
        dk_acc[:keys] += mm(grad, queries[first : first + rows])

    @pl.when(head != 0)
    def _():
        for place in range(len(BLOCKS)):
            _, grad = softmax_grad(place)
            pen_refs[place][...] += grad
            score_grad(place, grad)

    @pl.when(head == 0)
    def _():
        carry = None
        for place in reversed(range(len(BLOCKS))):
            first, rows, keys = BLOCKS[place]
            scores, grad = softmax_grad(place)
            whole = pen_refs[place][...] + grad
            later = split_mm(whole, triangle(rows, True))
            total = jnp.sum(whole, 1, keepdims=True)
            if carry is not None:
                if first + rows == SEQ:
                    lane = lax.broadcasted_iota(jnp.int32, (keys, rows), 1)
                    later = later + jnp.where(lane < TAIL, carry[:keys], 0.0)
                else:
                    later = later + carry[:keys]
                total = total + carry[:keys]
            carry = total
            _, chosen = block_masks(place)
            grad = grad + jnp.where(chosen & (scores > 0.0), -SELECT_GAIN * later, 0.0)
            score_grad(place, grad)

    @pl.when(half == 0)
    def _():
        dq_ref[...] = (dqt_ref[...].T * SCALE).astype(B16)
        dk_ref[...] = dk_acc[...].astype(B16)
        dv_ref[...] = dv_acc[...].astype(B16)


def pair_spec(index):
    return pl.BlockSpec((ROWS, PAIR), index)


def whole_specs():
    return [pl.BlockSpec((keys, rows), lambda i: (0, 0)) for _, rows, keys in BLOCKS]


PAIRS = HEADS // 2


def attend_forward(joined):
    return pl.pallas_call(
        forward_kernel,
        grid=(HEADS,),
        in_specs=[
            pair_spec(lambda i: (0, i // 2)),
            pair_spec(lambda i: (0, PAIRS + i // 2)),
            pair_spec(lambda i: (0, 2 * PAIRS + i // 2)),
        ],
        out_specs=[
            pair_spec(lambda i: (0, i // 2)),
            pl.BlockSpec((1, 1, ROWS), lambda i: (i, 0, 0)),
            *whole_specs(),
        ],
        out_shape=[
            jax.ShapeDtypeStruct((ROWS, D), B16),
            jax.ShapeDtypeStruct((HEADS, 1, ROWS), F32),
            *(jax.ShapeDtypeStruct((keys, rows), F32) for _, rows, keys in BLOCKS),
        ],
        scratch_shapes=[pltpu.VMEM((PAIR, ROWS), B16), pltpu.VMEM((PAIR, ROWS), F32)],
        name="attend_forward",
    )(joined, joined, joined)


def attend_backward(joined, grad_mixed, lse, biases):
    last = PAIRS - 1
    return pl.pallas_call(
        backward_kernel,
        grid=(HEADS,),
        in_specs=[
            pair_spec(lambda i: (0, last - i // 2)),
            pair_spec(lambda i: (0, PAIRS + last - i // 2)),
            pair_spec(lambda i: (0, 2 * PAIRS + last - i // 2)),
            pair_spec(lambda i: (0, last - i // 2)),
            pl.BlockSpec((1, 1, ROWS), lambda i: (HEADS - 1 - i, 0, 0)),
            *whole_specs(),
        ],
        out_specs=[pair_spec(lambda i: (0, last - i // 2)) for _ in range(3)],
        out_shape=[jax.ShapeDtypeStruct((ROWS, D), B16) for _ in range(3)],
        scratch_shapes=[
            pltpu.VMEM((PAIR, ROWS), B16),
            pltpu.VMEM((PAIR, ROWS), F32),
            pltpu.VMEM((ROWS, PAIR), F32),
            pltpu.VMEM((ROWS, PAIR), F32),
            *(pltpu.VMEM((keys, rows), F32) for _, rows, keys in BLOCKS),
        ],
        name="attend_backward",
    )(joined, joined, joined, grad_mixed, lse, *biases)


EVERY = ("dp", "fsdp")
CORE = 2
PLANE = (0, 1, 4, 5)


def device_count():
    return lax.axis_size("dp") * lax.axis_size("fsdp")


def depth():
    return device_count() // 8


def place_of():
    number = lax.axis_index("dp")
    return number // 4, number // 2 % 2, number % 2, lax.axis_index("fsdp")


def swap(value, mask):
    return lax.ppermute(value, EVERY, [(i, i ^ mask) for i in range(device_count())])


def arrange(pieces, own):
    pieces = list(pieces)
    bit = 1
    while bit < len(pieces):
        odd = (own // bit) % 2 == 1
        pieces = [jnp.where(odd, pieces[k ^ bit], pieces[k]) for k in range(len(pieces))]
        bit *= 2
    return pieces


def gather_steps(shard):
    z, x, core, y = place_of()
    column = [shard] + [swap(shard, 8 * k) for k in range(1, depth())]
    value = jnp.stack(arrange(column, z))
    plane = [value] + [swap(value, mask) for mask in PLANE[1:]]
    plane = arrange(plane, 2 * x + y)
    value = jnp.stack([jnp.stack(plane[:2], 1), jnp.stack(plane[2:], 1)], 1)
    value = jnp.stack(arrange([value, swap(value, CORE)], core), 2)
    return value.reshape(-1, shard.shape[1])


def take(value, index, axis):
    return lax.dynamic_index_in_dim(value, index, axis, keepdims=False)


def add_up(pieces):
    total = pieces[0].astype(F32)
    for piece in pieces[1:]:
        total = total + piece.astype(F32)
    return total


def scatter_steps(grad):
    return scatter_chips(scatter_core(grad))


def scatter_core(grad):
    core = place_of()[2]
    rows = grad.shape[0] // device_count()
    value = grad.reshape(depth(), 2, 2, 2, rows, grad.shape[1])
    other = swap(take(value, 1 - core, 2), CORE)
    return take(value, core, 2) + other


def scatter_chips(value):
    z, x, _, y = place_of()
    plane = [
        take(take(value, x ^ (mask // 4), 1), y ^ (mask % 2), 1) for mask in PLANE
    ]
    others = [swap(piece, mask) for piece, mask in zip(plane[1:], PLANE[1:])]
    value = add_up(plane[:1] + others).astype(B16)
    column = [take(value, z ^ k, 0) for k in range(depth())]
    others = [swap(column[k], 8 * k) for k in range(1, depth())]
    return add_up(column[:1] + others)


def pack_vectors(vectors, kind):
    rows = D // device_count()
    flat = jnp.concatenate([v.reshape(-1, v.shape[0] // vectors[0].shape[0] * rows) for v in vectors], 1)
    flat = flat.astype(kind).reshape(-1, 3, flat.shape[1] // 3)
    flat = jnp.pad(flat, ((0, 0), (0, rows - 3), (0, 128 - flat.shape[2])))
    return flat.reshape(-1, 128)


def unpack_vectors(columns, sizes):
    rows = D // device_count()
    width = sum(sizes) // 3
    flat = columns.reshape(-1, rows, 128)[:, :3, :width].reshape(-1, 3 * width)
    out, start = [], 0
    for size in sizes:
        out.append(flat[:, start : start + size].reshape(-1).astype(F32))
        start += size
    return out


def gelu_pair(upward):
    rate = (2.0 / jnp.pi) ** 0.5
    square = upward * upward
    bend = jnp.tanh(rate * (upward + 0.044715 * (square * upward)))
    gate = 0.5 * (1.0 + bend)
    slope = gate + 0.5 * upward * (1.0 - bend * bend) * (rate * (1.0 + 3 * 0.044715 * square))
    return (upward * gate).astype(B16), slope.astype(B16)


def normalize_back(values, gain, grad):
    center = values - jnp.mean(values, -1, keepdims=True)
    rate = lax.rsqrt(jnp.mean(center * center, -1, keepdims=True) + EPS)
    unit = center * rate
    scaled = grad * gain
    inner = jnp.mean(scaled * unit, -1, keepdims=True)
    back = rate * (scaled - jnp.mean(scaled, -1, keepdims=True) - unit * inner)
    return back, jnp.sum(grad * unit, 0), jnp.sum(grad, 0)


def pick(first, second, when):
    return jnp.where(when, first, second)


def trade_rows(prompt, cont):
    place = lax.axis_index("fsdp")
    low = place == 0
    swap_pairs = [(0, 1), (1, 0)]
    mine = [pick(t[0], t[1], low).reshape(-1, D) for t in (prompt, cont)]
    away = [pick(t[1], t[0], low).reshape(-1, D) for t in (prompt, cont)]
    came = lax.ppermute(jnp.concatenate(away, 0), "fsdp", swap_pairs)
    half = mine[0].shape[0]
    parts = (came[:half], came[half:])
    return jnp.concatenate(
        [
            pick(mine[0], parts[0], low),
            pick(parts[0], mine[0], low),
            pick(mine[1], parts[1], low),
            pick(parts[1], mine[1], low),
        ],
        0,
    )


def return_rows(whole, kind):
    place = lax.axis_index("fsdp")
    low = place == 0
    half = PROMPT // 2
    parts = (
        (whole[:half], whole[PROMPT:SEQ]),
        (whole[half:PROMPT], whole[SEQ:]),
    )
    mine = [pick(parts[0][i], parts[1][i], low) for i in range(2)]
    away = [pick(parts[1][i], parts[0][i], low) for i in range(2)]
    came = lax.ppermute(jnp.concatenate(away, 0).astype(B16), "fsdp", [(0, 1), (1, 0)])
    came = (came[:half], came[half:])
    out = []
    for i in range(2):
        own, other = mine[i].astype(kind), came[i].astype(kind)
        out.append(jnp.stack([pick(own, other, low), pick(other, own, low)]))
    return out[0][:, None], out[1][:, None, None]


def whole_layer(*args):
    return whole_steps(*args)


def whole_steps(
    x_prompt, x_cont, dy_prompt, dy_cont,
    ln1_gain, ln1_bias, w_qkv, b_qv, w_out, b_out,
    ln2_gain, ln2_bias, w_up, b_up, w_down, b_down,
):
    devices = device_count()
    vectors = (ln1_gain, ln1_bias, b_qv, b_out, ln2_gain, ln2_bias, b_up, b_down)
    sizes = [v.shape[0] for v in vectors]
    chunks = w_down.shape[0] // w_qkv.shape[0]
    rows = w_qkv.shape[0]
    full_rest = lax.all_gather(
        jnp.concatenate([w_out, *(w_up[:, i * D : (i + 1) * D] for i in range(chunks)), w_down], 0),
        EVERY,
        axis=0,
    )
    full_first = gather_steps(jnp.concatenate([w_qkv, pack_vectors(vectors, B16)], 1))
    full_qkv = full_first[:, : 3 * D]
    (
        gain_one, shift_one, bias_qv, bias_out, gain_two, shift_two, bias_up, bias_down,
    ) = unpack_vectors(full_first[:, 3 * D :], sizes)
    hidden = w_up.shape[1]
    full_out = full_rest[:, :rows].reshape(D, D)
    full_up = jnp.concatenate(
        [full_rest[:, rows * i : rows * (i + 1)].reshape(D, D) for i in range(1, chunks + 1)], 1
    )
    full_down = full_rest[:, rows * (chunks + 1) :].reshape(hidden, D)

    flat_x = trade_rows(x_prompt, x_cont).astype(F32)
    normed_one = normalize(flat_x, gain_one, shift_one).astype(B16)
    bias_joined = jnp.concatenate([bias_qv[:D], jnp.zeros((D,), F32), bias_qv[D:]])
    joined = (
        jnp.dot(normed_one, full_qkv, preferred_element_type=F32) + bias_joined
    ).astype(B16)
    joined, dy_prompt, dy_cont = lax.optimization_barrier((joined, dy_prompt, dy_cont))
    grad_y = trade_rows(dy_prompt, dy_cont)
    mixed, lse, *biases = attend_forward(joined)
    residual = flat_x + (jnp.dot(mixed, full_out, preferred_element_type=F32) + bias_out)
    normed_two = normalize(residual, gain_two, shift_two).astype(B16)
    upward = jnp.dot(normed_two, full_up, preferred_element_type=F32) + bias_up
    active, slope = lax.optimization_barrier(gelu_pair(upward))

    def weight_grad(left, right):
        return jnp.einsum("rd,re->de", left, right, preferred_element_type=F32).astype(B16)

    def through(grad, weight):
        return jnp.einsum("re,de->rd", grad, weight, preferred_element_type=F32)

    def column_sum(values):
        return jnp.sum(values.astype(F32), 0)

    grad_upward = (through(grad_y, full_down) * slope.astype(F32)).astype(B16)
    grad_down = weight_grad(active, grad_y)
    grad_up = weight_grad(normed_two, grad_upward)
    packed_grads = jnp.concatenate(
        [
            *(grad_up[:, i * D : (i + 1) * D].reshape(devices, rows, D) for i in range(chunks)),
            grad_down.reshape(devices, -1, D),
        ],
        1,
    )
    packed_grads, active, grad_upward = lax.optimization_barrier(
        (packed_grads, active, grad_upward)
    )
    own_hidden = lax.psum_scatter(packed_grads, EVERY, scatter_dimension=0).astype(F32)
    grad_w_up = jnp.concatenate(
        [own_hidden[i * rows : (i + 1) * rows] for i in range(chunks)], 1
    )
    grad_w_down = own_hidden[chunks * rows :]
    output = residual + (jnp.dot(active, full_down, preferred_element_type=F32) + bias_down)
    y_prompt, y_cont = return_rows(output.astype(B16), B16)

    grad_b_down = column_sum(grad_y)
    grad_b_up = column_sum(grad_upward)
    grad_resid, grad_gain_two, grad_shift_two = normalize_back(
        residual, gain_two, through(grad_upward, full_up)
    )
    grad_resid = grad_y.astype(F32) + grad_resid
    grad_branch = grad_resid.astype(B16)
    grad_w_out = scatter_steps(weight_grad(mixed, grad_branch))
    grad_b_out = column_sum(grad_branch)
    grad_mixed = through(grad_branch, full_out).astype(B16)
    grad_joined = jnp.concatenate(attend_backward(joined, grad_mixed, lse, biases), 1)
    grad_qkv = weight_grad(normed_one, grad_joined)
    grad_qkv, grad_joined = lax.optimization_barrier((grad_qkv, grad_joined))
    grad_b_qv = jnp.concatenate(
        [column_sum(grad_joined[:, :D]), column_sum(grad_joined[:, 2 * D :])]
    )
    first = scatter_core(grad_qkv)
    back_one = through(grad_joined, full_qkv)
    first, back_one = lax.optimization_barrier((first, back_one))
    grad_input, grad_gain_one, grad_shift_one = normalize_back(flat_x, gain_one, back_one)
    dx_prompt, dx_cont = return_rows(grad_resid + grad_input, F32)

    small = (
        grad_gain_one, grad_shift_one, grad_b_qv, grad_b_out,
        grad_gain_two, grad_shift_two, grad_b_up, grad_b_down,
    )
    own_first = scatter_chips(first)
    own_vectors = scatter_steps(pack_vectors(small, B16))
    grad_w_qkv = own_first
    pieces = unpack_vectors(own_vectors, sizes)
    return (
        y_prompt, y_cont, dx_prompt, dx_cont,
        pieces[0], pieces[1], grad_w_qkv, pieces[2], grad_w_out, pieces[3],
        pieces[4], pieces[5], grad_w_up, pieces[6], grad_w_down, pieces[7],
    )


def solution(mesh):
    sizes = dict(mesh.shape)
    whole = sizes["fsdp"] == MICRO == NCONT and sizes["dp"] & (sizes["dp"] - 1) == 0
    return jax.shard_map(
        whole_layer if whole else spread_layer,
        mesh=mesh,
        in_specs=(
            P(None, "dp", "fsdp", None),
            P(None, "dp", "fsdp", None, None),
            P(None, "dp", "fsdp", None),
            P(None, "dp", "fsdp", None, None),
            P(("dp", "fsdp")),
            P(("dp", "fsdp")),
            P(("dp", "fsdp"), None),
            P(("dp", "fsdp")),
            P(("dp", "fsdp"), None),
            P(("dp", "fsdp")),
            P(("dp", "fsdp")),
            P(("dp", "fsdp")),
            P(("dp", "fsdp"), None),
            P(("dp", "fsdp")),
            P(("dp", "fsdp"), None),
            P(("dp", "fsdp")),
        ),
        out_specs=(
            P(None, "dp", "fsdp", None),
            P(None, "dp", "fsdp", None, None),
            P(None, "dp", "fsdp", None),
            P(None, "dp", "fsdp", None, None),
            P(("dp", "fsdp")),
            P(("dp", "fsdp")),
            P(("dp", "fsdp"), None),
            P(("dp", "fsdp")),
            P(("dp", "fsdp"), None),
            P(("dp", "fsdp")),
            P(("dp", "fsdp")),
            P(("dp", "fsdp")),
            P(("dp", "fsdp"), None),
            P(("dp", "fsdp")),
            P(("dp", "fsdp"), None),
            P(("dp", "fsdp")),
        ),
        check_vma=False,
    )
```

profile of v0, /device:TPU:0, one launch (start us, length us, event | category | flops | bytes accessed | tf_op | source)
XLA Modules:
  0.0 475.6 jit_solution(8759705581541939116)
XLA Ops:
  14.8 5.1 %collective-permute-start.1 = (bf16[24,2432]{1,0:T(8,128)(2,1)S(1)}, bf16[24,2432]{1,0:T(8,128)(2,1)S(1)}, u32[]{:S(2)}, u32[]{:S(2)}) collective-permute-start(bf16[24,2432]{1,0:T(8,128)(2,1)S(1)} %pad_maximum_fusion.13), channel_id=1, source_target_pairs={{0,24},{1,25},{2,26},{3,27},{4,28},{5,29},{6,30},{7,31},{8,16},{9,... | collective-permute-start | bytes 350216 | tf_op jit(solution)/shard_map/ppermute | solution.py:649
  20.6 3.5 collective-permute-done.1
  24.1 9.1 %collective-permute-done.2 = bf16[24,2432]{1,0:T(8,128)(2,1)S(1)} collective-permute-done((bf16[24,2432]{1,0:T(8,128)(2,1)S(1)}, bf16[24,2432]{1,0:T(8,128)(2,1)S(1)}, u32[]{:S(2)}, u32[]{:S(2)}) %collective-permute-start.2) | collective-permute-done | bytes 116768 | tf_op jit(solution)/shard_map/ppermute | solution.py:649
  40.8 12.2 %collective-permute-done.5 = bf16[4,24,2432]{2,1,0:T(8,128)(2,1)S(1)} collective-permute-done((bf16[4,24,2432]{2,1,0:T(8,128)(2,1)}, bf16[4,24,2432]{2,1,0:T(8,128)(2,1)S(1)}, u32[]{:S(2)}, u32[]{:S(2)}) %collective-permute-start.5) | collective-permute-done | bytes 466976 | tf_op jit(solution)/shard_map/ppermute | solution.py:649
  53.0 12.7 %collective-permute-done.4 = bf16[4,24,2432]{2,1,0:T(8,128)(2,1)S(1)} collective-permute-done((bf16[4,24,2432]{2,1,0:T(8,128)(2,1)}, bf16[4,24,2432]{2,1,0:T(8,128)(2,1)S(1)}, u32[]{:S(2)}, u32[]{:S(2)}) %collective-permute-start.4) | collective-permute-done | bytes 466976 | tf_op jit(solution)/shard_map/ppermute | solution.py:649
  70.9 15.4 %collective-permute-done = bf16[544,768]{1,0:T(8,128)(2,1)} collective-permute-done((bf16[544,768]{1,0:T(8,128)(2,1)S(1)}, bf16[544,768]{1,0:T(8,128)(2,1)}, u32[]{:S(2)}, u32[]{:S(2)}) %collective-permute-start) | collective-permute-done | bytes 835616 | tf_op jit(solution)/shard_map/ppermute | solution.py:756
  95.5 10.4 %fusion.9.q_ref.k_ref.v_ref = bf16[1088,2304]{1,0:T(8,128)(2,1)} fusion(f32[2304]{0:T(1024)S(1)} %pad_maximum_fusion.14, bf16[768,2432]{1,0:T(8,128)(2,1)} %bitcast.237, f32[768]{0:T(1024)S(1)} %reshape.443, f32[768]{0:T(1024)S(1)} %reshape.442, f32[1088]{0:T(1024)S(1)} %add_rsqrt_fusion.1, f32[1088]{0:T(1024)S(1)} %broadcast_multiply_fusion.5, ...), kind=kOutput, calls=%fused_computation.16 | convolution fusion | flops 3866247168 | bytes 10247680 | tf_op jit(solution)/shard_map/dot_general | solution.py:824
  108.1 39.5 %attend_forward.1 = (bf16[1088,768]{1,0:T(8,128)(2,1)}, f32[12,1,1088]{2,1,0:T(1,128)}, f32[256,256]{1,0:T(8,128)}, f32[512,256]{1,0:T(8,128)}, f32[768,256]{1,0...) custom-call(bf16[1088,2304]{1,0:T(8,128)(2,1)} %fusion.9.q_ref.k_ref.v_ref, ...), custom_call_target="tpu_custom_call" | custom-call | tf_op jit(solution)/shard_map/attend_forward/pallas_call | solution.py:581
  154.7 3.1 fusion.65
  157.9 6.8 %slice.320 = bf16[32,96,768]{2,1,0:T(8,128)(2,1)} slice(bf16[32,216,768]{2,1,0:T(8,128)(2,1)} %bitcast.226), slice={[0:32], [120:216], [0:768]} | slice | bytes 9437184 | tf_op jit(solution)/shard_map/slice | solution.py:818
  167.1 17.3 %fusion.8 = (bf16[1088,3072]{1,0:T(8,128)(2,1)}, bf16[1088,3072]{1,0:T(8,128)(2,1)}) fusion(f32[3072]{0:T(1024)S(1)} %copy-done.46, bf16[768,768]{1,0:T(8,128)(2,1)S(1)} %bitcast.244, bf16[768,768]{1,0:T(8,128)(2,1)S(1)} %bitcast.246, bf16[768,768]{1,0:T(8,128)(2,1)S(1)} %bitcast.248, bf16[768,768]{1,0:T(8,128)(2,1)S(1)} %bitcast.242, ...), kind=kOutput, calls=%fused_computation.13 | convolution fusion | flops 5223727104 | bytes 21457408 | tf_op jit(solution)/shard_map/dot_general | solution.py:831
  184.5 11.2 %fusion.10 = bf16[1088,3072]{1,0:T(8,128)(2,1)S(1)} fusion(bf16[1088,3072]{1,0:T(8,128)(2,1)} %get-tuple-element.42, bf16[3072,768]{1,0:T(8,128)(2,1)} %bitcast.233, bf16[64,768]{1,0:T(8,128)(2,1)S(1)} %get-tuple-element.164, bf16[64,768]{1,0:T(8,128)(2,1)S(1)} %get-tuple-element.123, bf16[480,768]{1,0:T(8,128)(2,1)S(1)} %copy-done.15, ...), kind=kOutput, calls=%fused_computation.17 | convolution fusion | flops 5150539776 | bytes 19759104 | tf_op jit(solution)/shard_map/re,de->rd/dot_general | solution.py:838
  195.7 7.8 %convolution_convert_fusion.2 = bf16[768,3072]{1,0:T(8,128)(2,1)S(1)} fusion(bf16[1088,3072]{1,0:T(8,128)(2,1)S(1)} %fusion.10, f32[1088,768]{1,0:T(8,128)S(1)} %get-tuple-element.205, f32[768]{0:T(1024)S(1)} %copy-done.51, f32[768]{0:T(1024)S(1)} %copy-done.45, f32[1088]{0:T(1024)S(1)} %add_rsqrt_fusion, f32[1088]{0:T(1024)S(1)} %broadcast_multiply_fusion.4), kind=kOutput, calls=%fused_computation.20 | convolution fusion | flops 5140365312 | bytes 14760448 | tf_op jit(solution)/shard_map/rd,re->de/dot_general | solution.py:835
  206.8 6.7 %convolution_convert_fusion.1 = bf16[3072,768]{1,0:T(8,128)(2,1)S(1)} fusion(bf16[1088,3072]{1,0:T(8,128)(2,1)S(1)} %copy-done.57, bf16[64,768]{1,0:T(8,128)(2,1)S(1)} %get-tuple-element.164, bf16[64,768]{1,0:T(8,128)(2,1)S(1)} %get-tuple-element.123, bf16[480,768]{1,0:T(8,128)(2,1)S(1)} %copy-done.15, bf16[480,768]{1,0:T(8,128)(2,1)S(1)} %copy-done.14), kind=kOutput, calls=%fused_computation.19 | convolution fusion | flops 5142872064 | bytes 13074432 | tf_op jit(solution)/shard_map/rd,re->de/dot_general | solution.py:835
  219.5 10.0 %fusion.18 = bf16[1088,768]{1,0:T(8,128)(2,1)S(1)} fusion(f32[1088,768]{1,0:T(8,128)} %copy-done.5, bf16[1088,3072]{1,0:T(8,128)(2,1)} %get-tuple-element.44, bf16[3072,768]{1,0:T(8,128)(2,1)} %bitcast.234, f32[768]{0:T(1024)S(1)} %copy-done.50), kind=kOutput, calls=%fused_computation.35 | convolution fusion | flops 5136334848 | bytes 16419840 | tf_op jit(solution)/shard_map/dot_general | solution.py:861
  233.2 9.8 %multiply_reduce_fusion = (bf16[768]{0:T(1024)(128)(2,1)}, f32[1088]{0:T(1024)S(1)}, f32[1088]{0:T(1024)S(1)}, bf16[768]{0:T(1024)(128)(2,1)}, f32[1088,768]{1,0:T(8,128)S(1)}) fusion(f32[1088,768]{1,0:T(8,128)S(1)} %copy-done.6, f32[1088]{0:T(1024)S(1)} %add_rsqrt_fusion, f32[1088]{0:T(1024)S(1)} %broadcast_multiply_fusion.4, f32[768]{0:T(1024)S(1)} %copy-done.45, ...), kind=kOutput, calls=%fused_computation.45 | convolution fusion | flops 5160218624 | bytes 18111488 | tf_op jit(solution)/shard_map/re,de->rd/dot_general | solution.py:838
  243.0 3.4 convert_reduce_fusion.1
  249.2 48.9 %attend_backward.1 = (bf16[1088,768]{1,0:T(8,128)(2,1)}, bf16[1088,768]{1,0:T(8,128)(2,1)}, bf16[1088,768]{1,0:T(8,128)(2,1)}) custom-call(bf16[1088,2304]{1,0:T(8,128)(2,1)} %fusion.9.q_ref.k_ref.v_ref, bf16[1088,2304]{1,0:T(8,128)(2,1)} %fusion.9.q_ref.k_ref.v_ref, bf16[1088,2304]{1,0:T(8,128)(2,1)} %fusion.9.q_ref.k_ref.v_ref, ...), custom_call_target="tpu_custom_call" | custom-call | tf_op jit(solution)/shard_map/attend_backward/pallas_call | solution.py:606
  305.2 8.2 %convolution_convert_fusion = bf16[768,2304]{1,0:T(8,128)(2,1)S(1)} fusion(bf16[1088,2304]{1,0:T(8,128)(2,1)} %constant_dynamic-update-slice_fusion.7, f32[768]{0:T(1024)S(1)} %copy-done.49, f32[768]{0:T(1024)S(1)} %copy-done.37, f32[1088]{0:T(1024)S(1)} %add_rsqrt_fusion.1, f32[1088]{0:T(1024)S(1)} %broadcast_multiply_fusion.5, ...), kind=kOutput, calls=%fused_computation.18 | convolution fusion | flops 3863003136 | bytes 10238464 | tf_op jit(solution)/shard_map/rd,re->de/dot_general | solution.py:835
  319.8 5.8 %fusion.27 = f32[1088,768]{1,0:T(8,128)} fusion(bf16[1088,2304]{1,0:T(8,128)(2,1)S(1)} %bitcast.228, bf16[768,2432]{1,0:T(8,128)(2,1)S(1)} %bitcast.238), kind=kOutput, calls=%fused_computation.51 | convolution fusion | flops 3850371072 | bytes 11894784 | tf_op jit(solution)/shard_map/re,de->rd/dot_general | solution.py:838
  331.5 3.7 collective-permute-done.28
  339.4 3.2 collective-permute-start.31
  346.5 3.9 reduce.3
  360.4 4.0 fusion.25
  365.1 4.9 %fusion.24 = f32[1088,768]{1,0:T(8,128)S(1)} fusion(f32[1088,768]{1,0:T(8,128)} %copy-done.2, f32[1088,768]{1,0:T(8,128)} %fusion.27, f32[1088]{0:T(1024)S(1)} %broadcast_multiply_fusion, f32[1088]{0:T(1024)S(1)} %broadcast_multiply_fusion.1, f32[768]{0:T(1024)} %copy-done.36, f32[1088]{0:T(1024)S(1)} %add_rsqrt_fusion.1, ...), kind=kLoop, calls=%fused_computation.42 | loop fusion | flops 13369344 | bytes 11718656 | tf_op jit(solution)/shard_map/add | solution.py:884
  376.1 3.4 collective-permute-start.18
  386.8 10.9 %collective-permute-done.21 = bf16[4,24,2304]{2,1,0:T(8,128)(2,1)} collective-permute-done((bf16[4,24,2304]{2,1,0:T(8,128)(2,1)}, bf16[4,24,2304]{2,1,0:T(8,128)(2,1)}, u32[]{:S(2)}, u32[]{:S(2)}) %collective-permute-start.21) | collective-permute-done | bytes 442400 | tf_op jit(solution)/shard_map/ppermute | solution.py:649
  397.8 7.8 %collective-permute-done.20 = bf16[4,24,2304]{2,1,0:T(8,128)(2,1)} collective-permute-done((bf16[4,24,2304]{2,1,0:T(8,128)(2,1)}, bf16[4,24,2304]{2,1,0:T(8,128)(2,1)}, u32[]{:S(2)}, u32[]{:S(2)}) %collective-permute-start.20) | collective-permute-done | bytes 442400 | tf_op jit(solution)/shard_map/ppermute | solution.py:649
  405.6 22.1 %collective-permute-done.19 = bf16[4,24,2304]{2,1,0:T(8,128)(2,1)} collective-permute-done((bf16[4,24,2304]{2,1,0:T(8,128)(2,1)}, bf16[4,24,2304]{2,1,0:T(8,128)(2,1)}, u32[]{:S(2)}, u32[]{:S(2)}) %collective-permute-start.19) | collective-permute-done | bytes 442400 | tf_op jit(solution)/shard_map/ppermute | solution.py:649
  434.4 4.7 collective-permute-done.24
  439.1 7.4 %collective-permute-done.23 = bf16[24,2304]{1,0:T(8,128)(2,1)S(1)} collective-permute-done((bf16[24,2304]{1,0:T(8,128)(2,1)S(1)}, bf16[24,2304]{1,0:T(8,128)(2,1)S(1)}, u32[]{:S(2)}, u32[]{:S(2)}) %collective-permute-start.23) | collective-permute-done | bytes 110624 | tf_op jit(solution)/shard_map/ppermute | solution.py:649
  452.1 14.0 %reduce-scatter.2.cloned.1.call-done = bf16[1,192,768]{2,1,0:T(8,128)(2,1)} async-done(((bf16[32,192,768]{2,1,0:T(8,128)(2,1)}), bf16[1,192,768]{2,1,0:T(8,128)(2,1)}) %reduce-scatter.2.cloned.1.call-update) | async-done | bytes 294928 | tf_op jit(solution)/shard_map/reduce_scatter | solution.py:856
  (303 shorter events, 123.5 us)
Async XLA Ops:
  7.2 147.5 %all-gather.3.cloned.1.call-start = ((), (), s32[]{:S(2)}) async-start(), calls=%async_computation.2 | async-start | bytes 10948608 | tf_op jit(solution)/shard_map/all_gather | solution.py:803
  12.9 453.1 %reduce-scatter.2.cloned.1.call-start = ((), (), s32[]{:S(2)}) async-start(), calls=%async_computation.1 | async-start | bytes 9732096 | tf_op jit(solution)/shard_map/reduce_scatter | solution.py:856
  14.8 9.3 %collective-permute-start.1 = (bf16[24,2432]{1,0:T(8,128)(2,1)S(1)}, bf16[24,2432]{1,0:T(8,128)(2,1)S(1)}, u32[]{:S(2)}, u32[]{:S(2)}) collective-permute-start(bf16[24,2432]{1,0:T(8,128)(2,1)S(1)} %pad_maximum_fusion.13), channel_id=1, source_target_pairs={{0,24},{1,25},{2,26},{3,27},{4,28},{5,29},{6,30},{7,31},{8,16},{9,... | collective-permute-start | bytes 350216 | tf_op jit(solution)/shard_map/ppermute | solution.py:649
  20.0 13.2 %collective-permute-start.2 = (bf16[24,2432]{1,0:T(8,128)(2,1)S(1)}, bf16[24,2432]{1,0:T(8,128)(2,1)S(1)}, u32[]{:S(2)}, u32[]{:S(2)}) collective-permute-start(bf16[24,2432]{1,0:T(8,128)(2,1)S(1)} %pad_maximum_fusion.13), channel_id=1, source_target_pairs={{0,16},{1,17},{2,18},{3,19},{4,20},{5,21},{6,22},{7,23},{8,24},{9,... | collective-permute-start | bytes 350216 | tf_op jit(solution)/shard_map/ppermute | solution.py:649
  20.0 13.2 %collective-permute-start.3 = (bf16[24,2432]{1,0:T(8,128)(2,1)S(1)}, bf16[24,2432]{1,0:T(8,128)(2,1)S(1)}, u32[]{:S(2)}, u32[]{:S(2)}) collective-permute-start(bf16[24,2432]{1,0:T(8,128)(2,1)S(1)} %pad_maximum_fusion.13), channel_id=1, source_target_pairs={{0,8},{1,9},{2,10},{3,11},{4,12},{5,13},{6,14},{7,15},{8,0},{9,1},... | collective-permute-start | bytes 350216 | tf_op jit(solution)/shard_map/ppermute | solution.py:649
  35.1 18.0 %collective-permute-start.5 = (bf16[4,24,2432]{2,1,0:T(8,128)(2,1)}, bf16[4,24,2432]{2,1,0:T(8,128)(2,1)S(1)}, u32[]{:S(2)}, u32[]{:S(2)}) collective-permute-start(bf16[4,24,2432]{2,1,0:T(8,128)(2,1)} %pad_maximum_fusion.11), channel_id=1, source_target_pairs={{0,4},{1,5},{2,6},{3,7},{4,0},{5,1},{6,2},{7,3},{8,12},{9,13},{10,... | collective-permute-start | bytes 1400840 | tf_op jit(solution)/shard_map/ppermute | solution.py:649
  36.9 28.8 %collective-permute-start.4 = (bf16[4,24,2432]{2,1,0:T(8,128)(2,1)}, bf16[4,24,2432]{2,1,0:T(8,128)(2,1)S(1)}, u32[]{:S(2)}, u32[]{:S(2)}) collective-permute-start(bf16[4,24,2432]{2,1,0:T(8,128)(2,1)} %pad_maximum_fusion.11), channel_id=1, source_target_pairs={{0,5},{1,4},{2,7},{3,6},{4,1},{5,0},{6,3},{7,2},{8,13},{9,12},{10,... | collective-permute-start | bytes 1400840 | tf_op jit(solution)/shard_map/ppermute | solution.py:649
  38.5 28.4 %collective-permute-start.6 = (bf16[4,24,2432]{2,1,0:T(8,128)(2,1)}, bf16[4,24,2432]{2,1,0:T(8,128)(2,1)S(1)}, u32[]{:S(2)}, u32[]{:S(2)}) collective-permute-start(bf16[4,24,2432]{2,1,0:T(8,128)(2,1)} %pad_maximum_fusion.11), channel_id=1, source_target_pairs={{0,1},{1,0},{2,3},{3,2},{4,5},{5,4},{6,7},{7,6},{8,9},{9,8},{10,11... | collective-permute-start | bytes 1400840 | tf_op jit(solution)/shard_map/ppermute | solution.py:649
  39.3 47.0 %collective-permute-start = (bf16[544,768]{1,0:T(8,128)(2,1)S(1)}, bf16[544,768]{1,0:T(8,128)(2,1)}, u32[]{:S(2)}, u32[]{:S(2)}) collective-permute-start(bf16[544,768]{1,0:T(8,128)(2,1)S(1)} %pad_maximum_fusion.5), channel_id=1, source_target_pairs={{0,1},{1,0},{2,3},{3,2},{4,5},{5,4},{6,7},{7,6},{8,9},{9,8},{10,11... | collective-permute-start | bytes 2506760 | tf_op jit(solution)/shard_map/ppermute | solution.py:756
  70.9 19.0 %collective-permute-start.7 = (bf16[4,2,2,24,2432]{4,3,2,1,0:T(8,128)(2,1)}, bf16[4,2,2,24,2432]{4,3,2,1,0:T(8,128)(2,1)}, u32[]{:S(2)}, u32[]{:S(2)}) collective-permute-start(bf16[4,2,2,24,2432]{4,3,2,1,0:T(8,128)(2,1)} %pad_maximum_fusion.2), channel_id=1, source_target_pairs={{0,2},{1,3},{2,0},{3,1},{4,6},{5,7},{6,4},{7,5},{8,10},{9,11},{10,... | collective-permute-start | bytes 5603336 | tf_op jit(solution)/shard_map/ppermute | solution.py:649
  106.9 43.4 %collective-permute-start.8 = (bf16[544,768]{1,0:T(8,128)(2,1)}, bf16[544,768]{1,0:T(8,128)(2,1)}, u32[]{:S(2)}, u32[]{:S(2)}) collective-permute-start(bf16[544,768]{1,0:T(8,128)(2,1)} %pad_maximum_fusion.6), channel_id=1, source_target_pairs={{0,1},{1,0},{2,3},{3,2},{4,5},{5,4},{6,7},{7,6},{8,9},{9,8},{10,11... | collective-permute-start | bytes 2506760 | tf_op jit(solution)/shard_map/ppermute | solution.py:756
  231.7 120.8 %collective-permute-start.9 = (bf16[544,768]{1,0:T(8,128)(2,1)}, bf16[544,768]{1,0:T(8,128)(2,1)}, u32[]{:S(2)}, u32[]{:S(2)}) collective-permute-start(bf16[544,768]{1,0:T(8,128)(2,1)} %pad_maximum_fusion.7), channel_id=1, source_target_pairs={{0,1},{1,0},{2,3},{3,2},{4,5},{5,4},{6,7},{7,6},{8,9},{9,8},{10,11... | collective-permute-start | bytes 2506760 | tf_op jit(solution)/shard_map/ppermute | solution.py:780
  315.0 42.3 %collective-permute-start.10 = (bf16[4,2,2,24,2304]{4,3,0,2,1:T(8,128)(2,1)}, bf16[4,2,2,24,2304]{4,3,0,2,1:T(8,128)(2,1)}, u32[]{:S(2)}, u32[]{:S(2)}) collective-permute-start(bf16[4,2,2,24,2304]{4,3,0,2,1:T(8,128)(2,1)} %bitcast.223), channel_id=1, source_target_pairs={{0,2},{1,3},{2,0},{3,1},{4,6},{5,7},{6,4},{7,5},{8,10},{9,11},{10,... | collective-permute-start | bytes 5308424 | tf_op jit(solution)/shard_map/ppermute | solution.py:649
  318.7 6.9 %collective-permute-start.25 = (bf16[4,2,2,24,768]{4,3,0,2,1:T(8,128)(2,1)S(1)}, bf16[4,2,2,24,768]{4,3,0,2,1:T(8,128)(2,1)S(1)}, u32[]{:S(2)}, u32[]{:S(2)}) collective-permute-start(bf16[4,2,2,24,768]{4,3,0,2,1:T(8,128)(2,1)S(1)} %bitcast.253), channel_id=1, source_target_pairs={{0,2},{1,3},{2,0},{3,1},{4,6},{5,7},{6,4},{7,5},{8,10},{9,11},{10,... | collective-permute-start | bytes 1769480 | tf_op jit(solution)/shard_map/ppermute | solution.py:649
  327.3 7.9 %collective-permute-start.28 = (bf16[4,24,768]{2,1,0:T(8,128)(2,1)}, bf16[4,24,768]{2,1,0:T(8,128)(2,1)}, u32[]{:S(2)}, u32[]{:S(2)}) collective-permute-start(bf16[4,24,768]{2,1,0:T(8,128)(2,1)} %get-tuple-element.172), channel_id=1, source_target_pairs={{0,5},{1,4},{2,7},{3,6},{4,1},{5,0},{6,3},{7,2},{8,13},{9,12},{10,... | collective-permute-start | bytes 442376 | tf_op jit(solution)/shard_map/ppermute | solution.py:649
  328.9 7.0 %collective-permute-start.27 = (bf16[4,24,768]{2,1,0:T(8,128)(2,1)}, bf16[4,24,768]{2,1,0:T(8,128)(2,1)}, u32[]{:S(2)}, u32[]{:S(2)}) collective-permute-start(bf16[4,24,768]{2,1,0:T(8,128)(2,1)} %get-tuple-element.173), channel_id=1, source_target_pairs={{0,4},{1,5},{2,6},{3,7},{4,0},{5,1},{6,2},{7,3},{8,12},{9,13},{10,... | collective-permute-start | bytes 442376 | tf_op jit(solution)/shard_map/ppermute | solution.py:649
  329.2 7.7 %collective-permute-start.26 = (bf16[4,24,768]{2,1,0:T(8,128)(2,1)}, bf16[4,24,768]{2,1,0:T(8,128)(2,1)}, u32[]{:S(2)}, u32[]{:S(2)}) collective-permute-start(bf16[4,24,768]{2,1,0:T(8,128)(2,1)} %get-tuple-element.171), channel_id=1, source_target_pairs={{0,1},{1,0},{2,3},{3,2},{4,5},{5,4},{6,7},{7,6},{8,9},{9,8},{10,11... | collective-permute-start | bytes 442376 | tf_op jit(solution)/shard_map/ppermute | solution.py:649
  339.4 11.6 %collective-permute-start.31 = (bf16[24,768]{1,0:T(8,128)(2,1)}, bf16[24,768]{1,0:T(8,128)(2,1)S(1)}, u32[]{:S(2)}, u32[]{:S(2)}) collective-permute-start(bf16[24,768]{1,0:T(8,128)(2,1)} %get-tuple-element.182), channel_id=1, source_target_pairs={{0,24},{1,25},{2,26},{3,27},{4,28},{5,29},{6,30},{7,31},{8,16},{9,... | collective-permute-start | bytes 110600 | tf_op jit(solution)/shard_map/ppermute | solution.py:649
  342.6 8.5 %collective-permute-start.30 = (bf16[24,768]{1,0:T(8,128)(2,1)}, bf16[24,768]{1,0:T(8,128)(2,1)}, u32[]{:S(2)}, u32[]{:S(2)}) collective-permute-start(bf16[24,768]{1,0:T(8,128)(2,1)} %get-tuple-element.183), channel_id=1, source_target_pairs={{0,16},{1,17},{2,18},{3,19},{4,20},{5,21},{6,22},{7,23},{8,24},{9,... | collective-permute-start | bytes 110600 | tf_op jit(solution)/shard_map/ppermute | solution.py:649
  342.6 8.5 %collective-permute-start.29 = (bf16[24,768]{1,0:T(8,128)(2,1)S(1)}, bf16[24,768]{1,0:T(8,128)(2,1)}, u32[]{:S(2)}, u32[]{:S(2)}) collective-permute-start(bf16[24,768]{1,0:T(8,128)(2,1)S(1)} %get-tuple-element.181), channel_id=1, source_target_pairs={{0,8},{1,9},{2,10},{3,11},{4,12},{5,13},{6,14},{7,15},{8,0},{9,1},... | collective-permute-start | bytes 110600 | tf_op jit(solution)/shard_map/ppermute | solution.py:649
  365.0 5.2 %collective-permute-start.12 = (bf16[4,2,2,24,128]{4,3,2,1,0:T(8,128)(2,1)S(1)}, bf16[4,2,2,24,128]{4,3,2,1,0:T(8,128)(2,1)S(1)}, u32[]{:S(2)}, u32[]{:S(2)}) collective-permute-start(bf16[4,2,2,24,128]{4,3,2,1,0:T(8,128)(2,1)S(1)} %dynamic-slice_bitcast_fusion.9), channel_id=1, source_target_pairs={{0,2},{1,3},{2,0},{3,1},{4,6},{5,7},{6,4},{7,5},{8,10},{9,11},{10,... | collective-permute-start | bytes 294920 | tf_op jit(solution)/shard_map/ppermute | solution.py:649
  370.2 5.0 %collective-permute-start.15 = (bf16[4,24,128]{2,1,0:T(8,128)(2,1)S(1)}, bf16[4,24,128]{2,1,0:T(8,128)(2,1)S(1)}, u32[]{:S(2)}, u32[]{:S(2)}) collective-permute-start(bf16[4,24,128]{2,1,0:T(8,128)(2,1)S(1)} %get-tuple-element.185), channel_id=1, source_target_pairs={{0,5},{1,4},{2,7},{3,6},{4,1},{5,0},{6,3},{7,2},{8,13},{9,12},{10,... | collective-permute-start | bytes 73736 | tf_op jit(solution)/shard_map/ppermute | solution.py:649
  374.7 72.5 %collective-permute-start.11 = (bf16[544,768]{1,0:T(8,128)(2,1)}, bf16[544,768]{1,0:T(8,128)(2,1)}, u32[]{:S(2)}, u32[]{:S(2)}) collective-permute-start(bf16[544,768]{1,0:T(8,128)(2,1)} %pad_maximum_fusion.8), channel_id=1, source_target_pairs={{0,1},{1,0},{2,3},{3,2},{4,5},{5,4},{6,7},{7,6},{8,9},{9,8},{10,11... | collective-permute-start | bytes 2506760 | tf_op jit(solution)/shard_map/ppermute | solution.py:780
  376.1 8.7 %collective-permute-start.18 = (bf16[24,128]{1,0:T(8,128)(2,1)S(1)}, bf16[24,128]{1,0:T(8,128)(2,1)S(1)}, u32[]{:S(2)}, u32[]{:S(2)}) collective-permute-start(bf16[24,128]{1,0:T(8,128)(2,1)S(1)} %get-tuple-element.188), channel_id=1, source_target_pairs={{0,24},{1,25},{2,26},{3,27},{4,28},{5,29},{6,30},{7,31},{8,16},{9,... | collective-permute-start | bytes 18440 | tf_op jit(solution)/shard_map/ppermute | solution.py:649
  379.5 5.3 %collective-permute-start.17 = (bf16[24,128]{1,0:T(8,128)(2,1)S(1)}, bf16[24,128]{1,0:T(8,128)(2,1)S(1)}, u32[]{:S(2)}, u32[]{:S(2)}) collective-permute-start(bf16[24,128]{1,0:T(8,128)(2,1)S(1)} %get-tuple-element.189), channel_id=1, source_target_pairs={{0,16},{1,17},{2,18},{3,19},{4,20},{5,21},{6,22},{7,23},{8,24},{9,... | collective-permute-start | bytes 18440 | tf_op jit(solution)/shard_map/ppermute | solution.py:649
  379.5 6.1 %collective-permute-start.16 = (bf16[24,128]{1,0:T(8,128)(2,1)S(1)}, bf16[24,128]{1,0:T(8,128)(2,1)S(1)}, u32[]{:S(2)}, u32[]{:S(2)}) collective-permute-start(bf16[24,128]{1,0:T(8,128)(2,1)S(1)} %get-tuple-element.187), channel_id=1, source_target_pairs={{0,8},{1,9},{2,10},{3,11},{4,12},{5,13},{6,14},{7,15},{8,0},{9,1},... | collective-permute-start | bytes 18440 | tf_op jit(solution)/shard_map/ppermute | solution.py:649
  381.8 16.0 %collective-permute-start.21 = (bf16[4,24,2304]{2,1,0:T(8,128)(2,1)}, bf16[4,24,2304]{2,1,0:T(8,128)(2,1)}, u32[]{:S(2)}, u32[]{:S(2)}) collective-permute-start(bf16[4,24,2304]{2,1,0:T(8,128)(2,1)} %get-tuple-element.159), channel_id=1, source_target_pairs={{0,5},{1,4},{2,7},{3,6},{4,1},{5,0},{6,3},{7,2},{8,13},{9,12},{10,... | collective-permute-start | bytes 1327112 | tf_op jit(solution)/shard_map/ppermute | solution.py:649
  384.8 20.8 %collective-permute-start.20 = (bf16[4,24,2304]{2,1,0:T(8,128)(2,1)}, bf16[4,24,2304]{2,1,0:T(8,128)(2,1)}, u32[]{:S(2)}, u32[]{:S(2)}) collective-permute-start(bf16[4,24,2304]{2,1,0:T(8,128)(2,1)} %get-tuple-element.160), channel_id=1, source_target_pairs={{0,4},{1,5},{2,6},{3,7},{4,0},{5,1},{6,2},{7,3},{8,12},{9,13},{10,... | collective-permute-start | bytes 1327112 | tf_op jit(solution)/shard_map/ppermute | solution.py:649
  384.8 42.9 %collective-permute-start.19 = (bf16[4,24,2304]{2,1,0:T(8,128)(2,1)}, bf16[4,24,2304]{2,1,0:T(8,128)(2,1)}, u32[]{:S(2)}, u32[]{:S(2)}) collective-permute-start(bf16[4,24,2304]{2,1,0:T(8,128)(2,1)} %get-tuple-element.158), channel_id=1, source_target_pairs={{0,1},{1,0},{2,3},{3,2},{4,5},{5,4},{6,7},{7,6},{8,9},{9,8},{10,11... | collective-permute-start | bytes 1327112 | tf_op jit(solution)/shard_map/ppermute | solution.py:649
  429.4 9.7 %collective-permute-start.24 = (bf16[24,2304]{1,0:T(8,128)(2,1)S(1)}, bf16[24,2304]{1,0:T(8,128)(2,1)S(1)}, u32[]{:S(2)}, u32[]{:S(2)}) collective-permute-start(bf16[24,2304]{1,0:T(8,128)(2,1)S(1)} %get-tuple-element.179), channel_id=1, source_target_pairs={{0,24},{1,25},{2,26},{3,27},{4,28},{5,29},{6,30},{7,31},{8,16},{9,... | collective-permute-start | bytes 331784 | tf_op jit(solution)/shard_map/ppermute | solution.py:649
  431.9 14.6 %collective-permute-start.23 = (bf16[24,2304]{1,0:T(8,128)(2,1)S(1)}, bf16[24,2304]{1,0:T(8,128)(2,1)S(1)}, u32[]{:S(2)}, u32[]{:S(2)}) collective-permute-start(bf16[24,2304]{1,0:T(8,128)(2,1)S(1)} %get-tuple-element.180), channel_id=1, source_target_pairs={{0,16},{1,17},{2,18},{3,19},{4,20},{5,21},{6,22},{7,23},{8,24},{9,... | collective-permute-start | bytes 331784 | tf_op jit(solution)/shard_map/ppermute | solution.py:649
  431.9 14.6 %collective-permute-start.22 = (bf16[24,2304]{1,0:T(8,128)(2,1)S(1)}, bf16[24,2304]{1,0:T(8,128)(2,1)S(1)}, u32[]{:S(2)}, u32[]{:S(2)}) collective-permute-start(bf16[24,2304]{1,0:T(8,128)(2,1)S(1)} %get-tuple-element.178), channel_id=1, source_target_pairs={{0,8},{1,9},{2,10},{3,11},{4,12},{5,13},{6,14},{7,15},{8,0},{9,1},... | collective-permute-start | bytes 331784 | tf_op jit(solution)/shard_map/ppermute | solution.py:649
  (62 other events, 1015.8 us)
Sparse Core Ops, SparseCore 0:
  13.0 98.5 all-gather.2
  301.0 164.9 reduce-scatter.1
where the time goes:
time: 481 us; the launch traced here: 476 us
  waiting for transfers between devices  127 us (26%)
  matrix products  93.3 us (19%)
  Pallas kernels  88.4 us (18%)
  other arithmetic  56.8 us (12%)
  local copies, waits for them, and re-layouts  56.5 us (12%)
  starting transfers between devices  38.2 us (8%)
  between operations  15.3 us (3%)
    ppermute x28, waiting for transfers between devices, swap(): lax.ppermute(value, EVERY, [(i, i ^ mask) for i in range(device_count())])  97.9 us
    pallas_call x1, Pallas kernels, attend_backward(): pl.pallas_call(backward_kernel, grid=(HEADS,), in_specs=[pair_spec(lambda...  48.9 us
    pallas_call x1, Pallas kernels, attend_forward(): pl.pallas_call(forward_kernel, grid=(HEADS,), in_specs=[pair_spec(lambda...  39.5 us
    ppermute x28, starting transfers between devices, swap(): lax.ppermute(value, EVERY, [(i, i ^ mask) for i in range(device_count())])  34.1 us
    dot_general x4, matrix products, through(): return jnp.einsum('re,de->rd', grad, weight, preferred_element_type=F32)  29.5 us
    unnamed x131, local copies, waits for them, and re-layouts  25.6 us
    dot_general x4, matrix products, weight_grad(): jnp.einsum('rd,re->de', left, right, preferred_element_type=F32).astype(B16)  24.5 us
    dot_general x1, matrix products, whole_steps(): upward = jnp.dot(normed_two, full_up, preferred_element_type=F32) + bias_up  17.3 us
  transfers between devices with their start and end apart: 34, of which 17 were waited for; matrix products, arithmetic and copies ran while one was open for 24% of the time, Pallas kernels for 19%

commit v1 on v0

--- a/solution.py
+++ b/solution.py
@@ -494,8 +494,8 @@
 
 def backward_kernel(
     q_ref, k_ref, v_ref, g_ref, lse_ref, b0, b1, b2, b3, b4,
-    dq_ref, dk_ref, dv_ref,
-    kt_ref, dqt_ref, dk_acc, dv_acc, p0, p1, p2, p3, p4,
+    joined_ref,
+    kt_ref, dqt_ref, dk_acc, dv_acc, p0, p1, p2, p3, p4, stage_ref, sems,
 ):
     bias_refs = (b0, b1, b2, b3, b4)
     pen_refs = (p0, p1, p2, p3, p4)
@@ -559,11 +559,33 @@
             grad = grad + jnp.where(chosen & (scores > 0.0), -SELECT_GAIN * later, 0.0)
             score_grad(place, grad)
 
+    def copies(pair):
+        return [
+            pltpu.make_async_copy(
+                stage_ref.at[part],
+                joined_ref.at[:, pl.ds(pl.multiple_of(part * D + pair * PAIR, PAIR), PAIR)],
+                sems.at[part],
+            )
+            for part in range(3)
+        ]
+
+    @pl.when((half == 0) & (head != HEADS - 2))
+    def _():
+        for copy in copies(head // 2 + 1):
+            copy.wait()
+
     @pl.when(half == 0)
     def _():
-        dq_ref[...] = (dqt_ref[...].T * SCALE).astype(B16)
-        dk_ref[...] = dk_acc[...].astype(B16)
-        dv_ref[...] = dv_acc[...].astype(B16)
+        stage_ref[0] = (dqt_ref[...].T * SCALE).astype(B16)
+        stage_ref[1] = dk_acc[...].astype(B16)
+        stage_ref[2] = dv_acc[...].astype(B16)
+        for copy in copies(head // 2):
+            copy.start()
+
+    @pl.when(head == 0)
+    def _():
+        for copy in copies(0):
+            copy.wait()
 
 
 def pair_spec(index):
@@ -614,14 +636,16 @@
             pl.BlockSpec((1, 1, ROWS), lambda i: (HEADS - 1 - i, 0, 0)),
             *whole_specs(),
         ],
-        out_specs=[pair_spec(lambda i: (0, last - i // 2)) for _ in range(3)],
-        out_shape=[jax.ShapeDtypeStruct((ROWS, D), B16) for _ in range(3)],
+        out_specs=pl.BlockSpec(memory_space=pl.ANY),
+        out_shape=jax.ShapeDtypeStruct((ROWS, 3 * D), B16),
         scratch_shapes=[
             pltpu.VMEM((PAIR, ROWS), B16),
             pltpu.VMEM((PAIR, ROWS), F32),
             pltpu.VMEM((ROWS, PAIR), F32),
             pltpu.VMEM((ROWS, PAIR), F32),
             *(pltpu.VMEM((keys, rows), F32) for _, rows, keys in BLOCKS),
+            pltpu.VMEM((3, ROWS, PAIR), B16),
+            pltpu.SemaphoreType.DMA((3,)),
         ],
         name="attend_backward",
     )(joined, joined, joined, grad_mixed, lse, *biases)
@@ -659,15 +683,16 @@
     return pieces
 
 
-def gather_steps(shard):
+def gather_steps(shard, held):
     z, x, core, y = place_of()
     column = [shard] + [swap(shard, 8 * k) for k in range(1, depth())]
+    *column, held = lax.optimization_barrier((*column, held))
     value = jnp.stack(arrange(column, z))
     plane = [value] + [swap(value, mask) for mask in PLANE[1:]]
     plane = arrange(plane, 2 * x + y)
     value = jnp.stack([jnp.stack(plane[:2], 1), jnp.stack(plane[2:], 1)], 1)
     value = jnp.stack(arrange([value, swap(value, CORE)], core), 2)
-    return value.reshape(-1, shard.shape[1])
+    return value.reshape(-1, shard.shape[1]), held
 
 
 def take(value, index, axis):
@@ -800,12 +825,12 @@
     sizes = [v.shape[0] for v in vectors]
     chunks = w_down.shape[0] // w_qkv.shape[0]
     rows = w_qkv.shape[0]
-    full_rest = lax.all_gather(
-        jnp.concatenate([w_out, *(w_up[:, i * D : (i + 1) * D] for i in range(chunks)), w_down], 0),
-        EVERY,
-        axis=0,
-    )
-    full_first = gather_steps(jnp.concatenate([w_qkv, pack_vectors(vectors, B16)], 1))
+    flat_x = trade_rows(x_prompt, x_cont).astype(F32)
+    rest = jnp.concatenate(
+        [w_out, *(w_up[:, i * D : (i + 1) * D] for i in range(chunks)), w_down], 0
+    )
+    full_first, rest = gather_steps(jnp.concatenate([w_qkv, pack_vectors(vectors, B16)], 1), rest)
+    full_rest = lax.all_gather(rest, EVERY, axis=0)
     full_qkv = full_first[:, : 3 * D]
     (
         gain_one, shift_one, bias_qv, bias_out, gain_two, shift_two, bias_up, bias_down,
@@ -817,7 +842,6 @@
     )
     full_down = full_rest[:, rows * (chunks + 1) :].reshape(hidden, D)
 
-    flat_x = trade_rows(x_prompt, x_cont).astype(F32)
     normed_one = normalize(flat_x, gain_one, shift_one).astype(B16)
     bias_joined = jnp.concatenate([bias_qv[:D], jnp.zeros((D,), F32), bias_qv[D:]])
     joined = (
@@ -871,7 +895,7 @@
     grad_w_out = scatter_steps(weight_grad(mixed, grad_branch))
     grad_b_out = column_sum(grad_branch)
     grad_mixed = through(grad_branch, full_out).astype(B16)
-    grad_joined = jnp.concatenate(attend_backward(joined, grad_mixed, lse, biases), 1)
+    grad_joined = attend_backward(joined, grad_mixed, lse, biases)
     grad_qkv = weight_grad(normed_one, grad_joined)
     grad_qkv, grad_joined = lax.optimization_barrier((grad_qkv, grad_joined))
     grad_b_qv = jnp.concatenate(

time: 481 us -> 437 us (0.909)
  waiting for transfers between devices: 127 us -> 88.3 us
  local copies, waits for them, and re-layouts: 56.5 us -> 49.9 us
    ppermute x28, waiting for transfers between devices: 97.9 us -> 73.4 us  [swap(): lax.ppermute(value, EVERY, [(i, i ^ mask) for i in range(device_count())])]
    reduce_scatter x1, waiting for transfers between devices: 14 us -> 0.01 us  [whole_steps(): lax.psum_scatter(packed_grads, EVERY, scatter_dimension=0).astype(F32)]
    unnamed x131 -> x127, local copies, waits for them, and re-layouts: 25.6 us -> 20.3 us
  transfers between devices with their start and end apart: 34 -> 34, of which waited for: 17 -> 14; matrix products, arithmetic and copies ran while one was open for 24% -> 25% of each run, Pallas kernels for 19% -> 20%
where the time goes in v1:
time: 437 us; the launch traced here: 431 us
  matrix products  93 us (21%)
  waiting for transfers between devices  88.3 us (20%)
  Pallas kernels  88.3 us (20%)
  other arithmetic  55.9 us (13%)
  local copies, waits for them, and re-layouts  49.9 us (11%)
  starting transfers between devices  40.7 us (9%)
  between operations  15.4 us (4%)
    ppermute x28, waiting for transfers between devices, swap(): lax.ppermute(value, EVERY, [(i, i ^ mask) for i in range(device_count())])  73.4 us
    pallas_call x1, Pallas kernels, attend_backward(): pl.pallas_call(backward_kernel, grid=(HEADS,), in_specs=[pair_spec(lambda...  48.8 us
    pallas_call x1, Pallas kernels, attend_forward(): pl.pallas_call(forward_kernel, grid=(HEADS,), in_specs=[pair_spec(lambda...  39.5 us
    ppermute x28, starting transfers between devices, swap(): lax.ppermute(value, EVERY, [(i, i ^ mask) for i in range(device_count())])  35.6 us
    dot_general x4, matrix products, through(): return jnp.einsum('re,de->rd', grad, weight, preferred_element_type=F32)  29.5 us
    dot_general x4, matrix products, weight_grad(): jnp.einsum('rd,re->de', left, right, preferred_element_type=F32).astype(B16)  24.6 us
    unnamed x127, local copies, waits for them, and re-layouts  20.3 us
    dot_general x1, matrix products, whole_steps(): upward = jnp.dot(normed_two, full_up, preferred_element_type=F32) + bias_up  17.5 us
  transfers between devices with their start and end apart: 34, of which 14 were waited for; matrix products, arithmetic and copies ran while one was open for 25% of the time, Pallas kernels for 20%

profile of v1, /device:TPU:0, one launch (start us, length us, event | category | flops | bytes accessed | tf_op | source)
XLA Modules:
  0.0 431.5 jit_solution(7335024930112231654)
XLA Ops:
  9.3 3.1 collective-permute-start.1
  19.8 4.5 %collective-permute-done.2 = bf16[24,2432]{1,0:T(8,128)(2,1)S(1)} collective-permute-done((bf16[24,2432]{1,0:T(8,128)(2,1)S(1)}, bf16[24,2432]{1,0:T(8,128)(2,1)S(1)}, u32[]{:S(2)}, u32[]{:S(2)}) %collective-permute-start.2) | collective-permute-done | bytes 116768 | tf_op jit(solution)/shard_map/ppermute | solution.py:673
  30.5 10.9 %collective-permute-done.5 = bf16[4,24,2432]{2,1,0:T(8,128)(2,1)S(1)} collective-permute-done((bf16[4,24,2432]{2,1,0:T(8,128)(2,1)}, bf16[4,24,2432]{2,1,0:T(8,128)(2,1)S(1)}, u32[]{:S(2)}, u32[]{:S(2)}) %collective-permute-start.5) | collective-permute-done | bytes 466976 | tf_op jit(solution)/shard_map/ppermute | solution.py:673
  41.4 7.6 %collective-permute-done.4 = bf16[4,24,2432]{2,1,0:T(8,128)(2,1)S(1)} collective-permute-done((bf16[4,24,2432]{2,1,0:T(8,128)(2,1)}, bf16[4,24,2432]{2,1,0:T(8,128)(2,1)S(1)}, u32[]{:S(2)}, u32[]{:S(2)}) %collective-permute-start.4) | collective-permute-done | bytes 466976 | tf_op jit(solution)/shard_map/ppermute | solution.py:673
  49.1 5.3 %collective-permute-done.6 = bf16[4,24,2432]{2,1,0:T(8,128)(2,1)S(1)} collective-permute-done((bf16[4,24,2432]{2,1,0:T(8,128)(2,1)}, bf16[4,24,2432]{2,1,0:T(8,128)(2,1)S(1)}, u32[]{:S(2)}, u32[]{:S(2)}) %collective-permute-start.6) | collective-permute-done | bytes 466976 | tf_op jit(solution)/shard_map/ppermute | solution.py:673
  58.4 14.8 %collective-permute-done = bf16[544,768]{1,0:T(8,128)(2,1)} collective-permute-done((bf16[544,768]{1,0:T(8,128)(2,1)S(1)}, bf16[544,768]{1,0:T(8,128)(2,1)}, u32[]{:S(2)}, u32[]{:S(2)}) %collective-permute-start) | collective-permute-done | bytes 835616 | tf_op jit(solution)/shard_map/ppermute | solution.py:781
  82.3 10.1 %fusion.9.q_ref.k_ref.v_ref = bf16[1088,2304]{1,0:T(8,128)(2,1)} fusion(f32[2304]{0:T(1024)S(1)} %pad_maximum_fusion.14, bf16[768,2432]{1,0:T(8,128)(2,1)} %bitcast.237, f32[768]{0:T(1024)S(1)} %reshape.443, f32[768]{0:T(1024)S(1)} %reshape.442, f32[1088]{0:T(1024)S(1)} %add_rsqrt_fusion.1, f32[1088]{0:T(1024)S(1)} %broadcast_multiply_fusion.5, ...), kind=kOutput, calls=%fused_computation.16 | convolution fusion | flops 3866247168 | bytes 10247680 | tf_op jit(solution)/shard_map/dot_general | solution.py:848
  94.7 39.5 %attend_forward.1 = (bf16[1088,768]{1,0:T(8,128)(2,1)}, f32[12,1,1088]{2,1,0:T(1,128)}, f32[256,256]{1,0:T(8,128)}, f32[512,256]{1,0:T(8,128)}, f32[768,256]{1,0...) custom-call(bf16[1088,2304]{1,0:T(8,128)(2,1)} %fusion.9.q_ref.k_ref.v_ref, ...), custom_call_target="tpu_custom_call" | custom-call | tf_op jit(solution)/shard_map/attend_forward/pallas_call | solution.py:603
  141.3 3.1 fusion.65
  144.5 6.8 %slice.320 = bf16[32,96,768]{2,1,0:T(8,128)(2,1)} slice(bf16[32,216,768]{2,1,0:T(8,128)(2,1)} %bitcast.228), slice={[0:32], [120:216], [0:768]} | slice | bytes 9437184 | tf_op jit(solution)/shard_map/slice | solution.py:843
  153.8 17.5 %fusion.8 = (bf16[1088,3072]{1,0:T(8,128)(2,1)}, bf16[1088,3072]{1,0:T(8,128)(2,1)}) fusion(f32[3072]{0:T(1024)S(1)} %copy-done.45, bf16[768,768]{1,0:T(8,128)(2,1)S(1)} %bitcast.244, bf16[768,768]{1,0:T(8,128)(2,1)S(1)} %bitcast.246, bf16[768,768]{1,0:T(8,128)(2,1)S(1)} %bitcast.248, bf16[768,768]{1,0:T(8,128)(2,1)S(1)} %bitcast.242, ...), kind=kOutput, calls=%fused_computation.13 | convolution fusion | flops 5223727104 | bytes 21457408 | tf_op jit(solution)/shard_map/dot_general | solution.py:855
  171.2 11.2 %fusion.10 = bf16[1088,3072]{1,0:T(8,128)(2,1)S(1)} fusion(bf16[1088,3072]{1,0:T(8,128)(2,1)} %get-tuple-element.49, bf16[3072,768]{1,0:T(8,128)(2,1)} %bitcast.233, bf16[64,768]{1,0:T(8,128)(2,1)S(1)} %get-tuple-element.168, bf16[64,768]{1,0:T(8,128)(2,1)S(1)} %get-tuple-element.127, bf16[480,768]{1,0:T(8,128)(2,1)S(1)} %copy-done.15, ...), kind=kOutput, calls=%fused_computation.17 | convolution fusion | flops 5150539776 | bytes 19759104 | tf_op jit(solution)/shard_map/re,de->rd/dot_general | solution.py:862
  182.4 8.0 %convolution_convert_fusion.2 = bf16[768,3072]{1,0:T(8,128)(2,1)S(1)} fusion(bf16[1088,3072]{1,0:T(8,128)(2,1)S(1)} %fusion.10, f32[1088,768]{1,0:T(8,128)S(1)} %get-tuple-element.209, f32[768]{0:T(1024)S(1)} %copy-done.50, f32[768]{0:T(1024)S(1)} %copy-done.44, f32[1088]{0:T(1024)S(1)} %add_rsqrt_fusion, f32[1088]{0:T(1024)S(1)} %broadcast_multiply_fusion.4), kind=kOutput, calls=%fused_computation.20 | convolution fusion | flops 5140365312 | bytes 14760448 | tf_op jit(solution)/shard_map/rd,re->de/dot_general | solution.py:859
  193.8 6.7 %convolution_convert_fusion.1 = bf16[3072,768]{1,0:T(8,128)(2,1)S(1)} fusion(bf16[1088,3072]{1,0:T(8,128)(2,1)S(1)} %copy-done.56, bf16[64,768]{1,0:T(8,128)(2,1)S(1)} %get-tuple-element.168, bf16[64,768]{1,0:T(8,128)(2,1)S(1)} %get-tuple-element.127, bf16[480,768]{1,0:T(8,128)(2,1)S(1)} %copy-done.15, bf16[480,768]{1,0:T(8,128)(2,1)S(1)} %copy-done.14), kind=kOutput, calls=%fused_computation.19 | convolution fusion | flops 5142872064 | bytes 13074432 | tf_op jit(solution)/shard_map/rd,re->de/dot_general | solution.py:859
  206.4 9.7 %fusion.18 = bf16[1088,768]{1,0:T(8,128)(2,1)S(1)} fusion(f32[1088,768]{1,0:T(8,128)} %copy-done.5, bf16[1088,3072]{1,0:T(8,128)(2,1)} %get-tuple-element.51, bf16[3072,768]{1,0:T(8,128)(2,1)} %bitcast.234, f32[768]{0:T(1024)S(1)} %copy-done.49), kind=kOutput, calls=%fused_computation.35 | convolution fusion | flops 5136334848 | bytes 16419840 | tf_op jit(solution)/shard_map/dot_general | solution.py:885
  219.9 9.8 %multiply_reduce_fusion = (bf16[768]{0:T(1024)(128)(2,1)}, f32[1088]{0:T(1024)S(1)}, f32[1088]{0:T(1024)S(1)}, bf16[768]{0:T(1024)(128)(2,1)}, f32[1088,768]{1,0:T(8,128)S(1)}) fusion(f32[1088,768]{1,0:T(8,128)S(1)} %copy-done.6, f32[1088]{0:T(1024)S(1)} %add_rsqrt_fusion, f32[1088]{0:T(1024)S(1)} %broadcast_multiply_fusion.4, f32[768]{0:T(1024)S(1)} %copy-done.44, ...), kind=kOutput, calls=%fused_computation.45 | convolution fusion | flops 5160218624 | bytes 18111488 | tf_op jit(solution)/shard_map/re,de->rd/dot_general | solution.py:862
  229.7 3.4 convert_reduce_fusion.1
  237.7 48.8 %attend_backward.1 = bf16[1088,2304]{1,0:T(8,128)(2,1)} custom-call(bf16[1088,2304]{1,0:T(8,128)(2,1)} %fusion.9.q_ref.k_ref.v_ref, bf16[1088,2304]{1,0:T(8,128)(2,1)} %fusion.9.q_ref.k_ref.v_ref, bf16[1088,2304]{1,0:T(8,128)(2,1)} %fusion.9.q_ref.k_ref.v_ref, bf16[1088,768]{1,0:T(8,128)(2,1)} %convolution_convert_fusion.3.g_ref, ...), custom_call_target="tpu_custom_call" | custom-call | tf_op jit(solution)/shard_map/attend_backward/pallas_call | solution.py:628
  286.5 8.0 %convolution_convert_fusion = bf16[768,2304]{1,0:T(8,128)(2,1)S(1)} fusion(bf16[1088,2304]{1,0:T(8,128)(2,1)} %attend_backward.1, f32[768]{0:T(1024)S(1)} %copy-done.48, f32[768]{0:T(1024)S(1)} %copy-done.36, f32[1088]{0:T(1024)S(1)} %add_rsqrt_fusion.1, f32[1088]{0:T(1024)S(1)} %broadcast_multiply_fusion.5, bf16[64,768]{1,0:T(8,128)(2,1)S(1)} %get-tuple-element.170, ...), kind=kOutput, calls=%fused_computation.18 | convolution fusion | flops 3863003136 | bytes 10238464 | tf_op jit(solution)/shard_map/rd,re->de/dot_general | solution.py:859
  300.5 5.8 %fusion.27 = f32[1088,768]{1,0:T(8,128)} fusion(bf16[1088,2304]{1,0:T(8,128)(2,1)S(1)} %bitcast.226, bf16[768,2432]{1,0:T(8,128)(2,1)S(1)} %bitcast.238), kind=kOutput, calls=%fused_computation.51 | convolution fusion | flops 3850371072 | bytes 11894784 | tf_op jit(solution)/shard_map/re,de->rd/dot_general | solution.py:862
  312.1 3.8 collective-permute-done.28
  316.0 3.6 collective-permute-done.27
  325.4 3.0 collective-permute-start.30
  331.7 3.9 reduce.3
  342.6 3.0 bitcast_add_fusion
  345.7 4.0 fusion.25
  350.4 5.0 %fusion.24 = f32[1088,768]{1,0:T(8,128)S(1)} fusion(f32[1088,768]{1,0:T(8,128)} %copy-done.2, f32[1088,768]{1,0:T(8,128)} %fusion.27, f32[1088]{0:T(1024)S(1)} %broadcast_multiply_fusion, f32[1088]{0:T(1024)S(1)} %broadcast_multiply_fusion.1, f32[768]{0:T(1024)} %copy-done.35, f32[1088]{0:T(1024)S(1)} %add_rsqrt_fusion.1, ...), kind=kLoop, calls=%fused_computation.42 | loop fusion | flops 13369344 | bytes 11718656 | tf_op jit(solution)/shard_map/add | solution.py:908
  355.6 3.3 collective-permute-start.15
  373.2 9.4 %collective-permute-done.21 = bf16[4,24,2304]{2,1,0:T(8,128)(2,1)} collective-permute-done((bf16[4,24,2304]{2,1,0:T(8,128)(2,1)}, bf16[4,24,2304]{2,1,0:T(8,128)(2,1)}, u32[]{:S(2)}, u32[]{:S(2)}) %collective-permute-start.21) | collective-permute-done | bytes 442400 | tf_op jit(solution)/shard_map/ppermute | solution.py:673
  382.6 5.9 %collective-permute-done.20 = bf16[4,24,2304]{2,1,0:T(8,128)(2,1)} collective-permute-done((bf16[4,24,2304]{2,1,0:T(8,128)(2,1)}, bf16[4,24,2304]{2,1,0:T(8,128)(2,1)}, u32[]{:S(2)}, u32[]{:S(2)}) %collective-permute-start.20) | collective-permute-done | bytes 442400 | tf_op jit(solution)/shard_map/ppermute | solution.py:673
  388.5 13.7 %collective-permute-done.19 = bf16[4,24,2304]{2,1,0:T(8,128)(2,1)} collective-permute-done((bf16[4,24,2304]{2,1,0:T(8,128)(2,1)}, bf16[4,24,2304]{2,1,0:T(8,128)(2,1)}, u32[]{:S(2)}, u32[]{:S(2)}) %collective-permute-start.19) | collective-permute-done | bytes 442400 | tf_op jit(solution)/shard_map/ppermute | solution.py:673
  411.7 4.5 %collective-permute-done.23 = bf16[24,2304]{1,0:T(8,128)(2,1)S(1)} collective-permute-done((bf16[24,2304]{1,0:T(8,128)(2,1)S(1)}, bf16[24,2304]{1,0:T(8,128)(2,1)S(1)}, u32[]{:S(2)}, u32[]{:S(2)}) %collective-permute-start.23) | collective-permute-done | bytes 110624 | tf_op jit(solution)/shard_map/ppermute | solution.py:673
  (298 shorter events, 118.2 us)
Async XLA Ops:
  7.2 134.1 %all-gather.3.cloned.1.call-start = ((), (), s32[]{:S(2)}) async-start(), calls=%async_computation.2 | async-start | bytes 10948608 | tf_op jit(solution)/shard_map/all_gather | solution.py:833
  9.3 10.5 %collective-permute-start.1 = (bf16[24,2432]{1,0:T(8,128)(2,1)S(1)}, bf16[24,2432]{1,0:T(8,128)(2,1)S(1)}, u32[]{:S(2)}, u32[]{:S(2)}) collective-permute-start(bf16[24,2432]{1,0:T(8,128)(2,1)S(1)} %pad_maximum_fusion.13), channel_id=1, source_target_pairs={{0,8},{1,9},{2,10},{3,11},{4,12},{5,13},{6,14},{7,15},{8,0},{9,1},... | collective-permute-start | bytes 350216 | tf_op jit(solution)/shard_map/ppermute | solution.py:673
  12.4 11.9 %collective-permute-start.2 = (bf16[24,2432]{1,0:T(8,128)(2,1)S(1)}, bf16[24,2432]{1,0:T(8,128)(2,1)S(1)}, u32[]{:S(2)}, u32[]{:S(2)}) collective-permute-start(bf16[24,2432]{1,0:T(8,128)(2,1)S(1)} %pad_maximum_fusion.13), channel_id=1, source_target_pairs={{0,16},{1,17},{2,18},{3,19},{4,20},{5,21},{6,22},{7,23},{8,24},{9,... | collective-permute-start | bytes 350216 | tf_op jit(solution)/shard_map/ppermute | solution.py:673
  15.0 9.3 %collective-permute-start.3 = (bf16[24,2432]{1,0:T(8,128)(2,1)S(1)}, bf16[24,2432]{1,0:T(8,128)(2,1)S(1)}, u32[]{:S(2)}, u32[]{:S(2)}) collective-permute-start(bf16[24,2432]{1,0:T(8,128)(2,1)S(1)} %pad_maximum_fusion.13), channel_id=1, source_target_pairs={{0,24},{1,25},{2,26},{3,27},{4,28},{5,29},{6,30},{7,31},{8,16},{9,... | collective-permute-start | bytes 350216 | tf_op jit(solution)/shard_map/ppermute | solution.py:673
  24.3 397.6 %reduce-scatter.2.cloned.1.call-start = ((), (), s32[]{:S(2)}) async-start(), calls=%async_computation.1 | async-start | bytes 9732096 | tf_op jit(solution)/shard_map/reduce_scatter | solution.py:880
  25.3 16.1 %collective-permute-start.5 = (bf16[4,24,2432]{2,1,0:T(8,128)(2,1)}, bf16[4,24,2432]{2,1,0:T(8,128)(2,1)S(1)}, u32[]{:S(2)}, u32[]{:S(2)}) collective-permute-start(bf16[4,24,2432]{2,1,0:T(8,128)(2,1)} %pad_maximum_fusion.11), channel_id=1, source_target_pairs={{0,4},{1,5},{2,6},{3,7},{4,0},{5,1},{6,2},{7,3},{8,12},{9,13},{10,... | collective-permute-start | bytes 1400840 | tf_op jit(solution)/shard_map/ppermute | solution.py:673
  26.8 22.3 %collective-permute-start.4 = (bf16[4,24,2432]{2,1,0:T(8,128)(2,1)}, bf16[4,24,2432]{2,1,0:T(8,128)(2,1)S(1)}, u32[]{:S(2)}, u32[]{:S(2)}) collective-permute-start(bf16[4,24,2432]{2,1,0:T(8,128)(2,1)} %pad_maximum_fusion.11), channel_id=1, source_target_pairs={{0,5},{1,4},{2,7},{3,6},{4,1},{5,0},{6,3},{7,2},{8,13},{9,12},{10,... | collective-permute-start | bytes 1400840 | tf_op jit(solution)/shard_map/ppermute | solution.py:673
  28.3 26.2 %collective-permute-start.6 = (bf16[4,24,2432]{2,1,0:T(8,128)(2,1)}, bf16[4,24,2432]{2,1,0:T(8,128)(2,1)S(1)}, u32[]{:S(2)}, u32[]{:S(2)}) collective-permute-start(bf16[4,24,2432]{2,1,0:T(8,128)(2,1)} %pad_maximum_fusion.11), channel_id=1, source_target_pairs={{0,1},{1,0},{2,3},{3,2},{4,5},{5,4},{6,7},{7,6},{8,9},{9,8},{10,11... | collective-permute-start | bytes 1400840 | tf_op jit(solution)/shard_map/ppermute | solution.py:673
  28.9 44.2 %collective-permute-start = (bf16[544,768]{1,0:T(8,128)(2,1)S(1)}, bf16[544,768]{1,0:T(8,128)(2,1)}, u32[]{:S(2)}, u32[]{:S(2)}) collective-permute-start(bf16[544,768]{1,0:T(8,128)(2,1)S(1)} %pad_maximum_fusion.5), channel_id=1, source_target_pairs={{0,1},{1,0},{2,3},{3,2},{4,5},{5,4},{6,7},{7,6},{8,9},{9,8},{10,11... | collective-permute-start | bytes 2506760 | tf_op jit(solution)/shard_map/ppermute | solution.py:781
  58.4 18.4 %collective-permute-start.7 = (bf16[4,2,2,24,2432]{4,3,2,1,0:T(8,128)(2,1)}, bf16[4,2,2,24,2432]{4,3,2,1,0:T(8,128)(2,1)}, u32[]{:S(2)}, u32[]{:S(2)}) collective-permute-start(bf16[4,2,2,24,2432]{4,3,2,1,0:T(8,128)(2,1)} %pad_maximum_fusion.2), channel_id=1, source_target_pairs={{0,2},{1,3},{2,0},{3,1},{4,6},{5,7},{6,4},{7,5},{8,10},{9,11},{10,... | collective-permute-start | bytes 5603336 | tf_op jit(solution)/shard_map/ppermute | solution.py:673
  93.5 43.4 %collective-permute-start.8 = (bf16[544,768]{1,0:T(8,128)(2,1)}, bf16[544,768]{1,0:T(8,128)(2,1)}, u32[]{:S(2)}, u32[]{:S(2)}) collective-permute-start(bf16[544,768]{1,0:T(8,128)(2,1)} %pad_maximum_fusion.6), channel_id=1, source_target_pairs={{0,1},{1,0},{2,3},{3,2},{4,5},{5,4},{6,7},{7,6},{8,9},{9,8},{10,11... | collective-permute-start | bytes 2506760 | tf_op jit(solution)/shard_map/ppermute | solution.py:781
  218.4 119.4 %collective-permute-start.9 = (bf16[544,768]{1,0:T(8,128)(2,1)}, bf16[544,768]{1,0:T(8,128)(2,1)}, u32[]{:S(2)}, u32[]{:S(2)}) collective-permute-start(bf16[544,768]{1,0:T(8,128)(2,1)} %pad_maximum_fusion.7), channel_id=1, source_target_pairs={{0,1},{1,0},{2,3},{3,2},{4,5},{5,4},{6,7},{7,6},{8,9},{9,8},{10,11... | collective-permute-start | bytes 2506760 | tf_op jit(solution)/shard_map/ppermute | solution.py:805
  296.2 46.4 %collective-permute-start.10 = (bf16[4,2,2,24,2304]{4,3,0,2,1:T(8,128)(2,1)}, bf16[4,2,2,24,2304]{4,3,0,2,1:T(8,128)(2,1)}, u32[]{:S(2)}, u32[]{:S(2)}) collective-permute-start(bf16[4,2,2,24,2304]{4,3,0,2,1:T(8,128)(2,1)} %bitcast.223), channel_id=1, source_target_pairs={{0,2},{1,3},{2,0},{3,1},{4,6},{5,7},{6,4},{7,5},{8,10},{9,11},{10,... | collective-permute-start | bytes 5308424 | tf_op jit(solution)/shard_map/ppermute | solution.py:673
  299.6 6.6 %collective-permute-start.25 = (bf16[4,2,2,24,768]{4,3,0,2,1:T(8,128)(2,1)S(1)}, bf16[4,2,2,24,768]{4,3,0,2,1:T(8,128)(2,1)S(1)}, u32[]{:S(2)}, u32[]{:S(2)}) collective-permute-start(bf16[4,2,2,24,768]{4,3,0,2,1:T(8,128)(2,1)S(1)} %bitcast.253), channel_id=1, source_target_pairs={{0,2},{1,3},{2,0},{3,1},{4,6},{5,7},{6,4},{7,5},{8,10},{9,11},{10,... | collective-permute-start | bytes 1769480 | tf_op jit(solution)/shard_map/ppermute | solution.py:673
  307.9 8.0 %collective-permute-start.28 = (bf16[4,24,768]{2,1,0:T(8,128)(2,1)}, bf16[4,24,768]{2,1,0:T(8,128)(2,1)}, u32[]{:S(2)}, u32[]{:S(2)}) collective-permute-start(bf16[4,24,768]{2,1,0:T(8,128)(2,1)} %get-tuple-element.176), channel_id=1, source_target_pairs={{0,5},{1,4},{2,7},{3,6},{4,1},{5,0},{6,3},{7,2},{8,13},{9,12},{10,... | collective-permute-start | bytes 442376 | tf_op jit(solution)/shard_map/ppermute | solution.py:673
  309.4 10.1 %collective-permute-start.27 = (bf16[4,24,768]{2,1,0:T(8,128)(2,1)}, bf16[4,24,768]{2,1,0:T(8,128)(2,1)}, u32[]{:S(2)}, u32[]{:S(2)}) collective-permute-start(bf16[4,24,768]{2,1,0:T(8,128)(2,1)} %get-tuple-element.177), channel_id=1, source_target_pairs={{0,4},{1,5},{2,6},{3,7},{4,0},{5,1},{6,2},{7,3},{8,12},{9,13},{10,... | collective-permute-start | bytes 442376 | tf_op jit(solution)/shard_map/ppermute | solution.py:673
  310.0 10.0 %collective-permute-start.26 = (bf16[4,24,768]{2,1,0:T(8,128)(2,1)}, bf16[4,24,768]{2,1,0:T(8,128)(2,1)}, u32[]{:S(2)}, u32[]{:S(2)}) collective-permute-start(bf16[4,24,768]{2,1,0:T(8,128)(2,1)} %get-tuple-element.175), channel_id=1, source_target_pairs={{0,1},{1,0},{2,3},{3,2},{4,5},{5,4},{6,7},{7,6},{8,9},{9,8},{10,11... | collective-permute-start | bytes 442376 | tf_op jit(solution)/shard_map/ppermute | solution.py:673
  322.6 13.7 %collective-permute-start.31 = (bf16[24,768]{1,0:T(8,128)(2,1)}, bf16[24,768]{1,0:T(8,128)(2,1)S(1)}, u32[]{:S(2)}, u32[]{:S(2)}) collective-permute-start(bf16[24,768]{1,0:T(8,128)(2,1)} %get-tuple-element.186), channel_id=1, source_target_pairs={{0,24},{1,25},{2,26},{3,27},{4,28},{5,29},{6,30},{7,31},{8,16},{9,... | collective-permute-start | bytes 110600 | tf_op jit(solution)/shard_map/ppermute | solution.py:673
  325.4 10.9 %collective-permute-start.30 = (bf16[24,768]{1,0:T(8,128)(2,1)}, bf16[24,768]{1,0:T(8,128)(2,1)}, u32[]{:S(2)}, u32[]{:S(2)}) collective-permute-start(bf16[24,768]{1,0:T(8,128)(2,1)} %get-tuple-element.187), channel_id=1, source_target_pairs={{0,16},{1,17},{2,18},{3,19},{4,20},{5,21},{6,22},{7,23},{8,24},{9,... | collective-permute-start | bytes 110600 | tf_op jit(solution)/shard_map/ppermute | solution.py:673
  328.5 7.8 %collective-permute-start.29 = (bf16[24,768]{1,0:T(8,128)(2,1)S(1)}, bf16[24,768]{1,0:T(8,128)(2,1)}, u32[]{:S(2)}, u32[]{:S(2)}) collective-permute-start(bf16[24,768]{1,0:T(8,128)(2,1)S(1)} %get-tuple-element.185), channel_id=1, source_target_pairs={{0,8},{1,9},{2,10},{3,11},{4,12},{5,13},{6,14},{7,15},{8,0},{9,1},... | collective-permute-start | bytes 110600 | tf_op jit(solution)/shard_map/ppermute | solution.py:673
  350.2 5.3 %collective-permute-start.12 = (bf16[4,2,2,24,128]{4,3,2,1,0:T(8,128)(2,1)S(1)}, bf16[4,2,2,24,128]{4,3,2,1,0:T(8,128)(2,1)S(1)}, u32[]{:S(2)}, u32[]{:S(2)}) collective-permute-start(bf16[4,2,2,24,128]{4,3,2,1,0:T(8,128)(2,1)S(1)} %dynamic-slice_bitcast_fusion.9), channel_id=1, source_target_pairs={{0,2},{1,3},{2,0},{3,1},{4,6},{5,7},{6,4},{7,5},{8,10},{9,11},{10,... | collective-permute-start | bytes 294920 | tf_op jit(solution)/shard_map/ppermute | solution.py:673
  355.6 6.3 %collective-permute-start.15 = (bf16[4,24,128]{2,1,0:T(8,128)(2,1)S(1)}, bf16[4,24,128]{2,1,0:T(8,128)(2,1)S(1)}, u32[]{:S(2)}, u32[]{:S(2)}) collective-permute-start(bf16[4,24,128]{2,1,0:T(8,128)(2,1)S(1)} %get-tuple-element.189), channel_id=1, source_target_pairs={{0,5},{1,4},{2,7},{3,6},{4,1},{5,0},{6,3},{7,2},{8,13},{9,12},{10,... | collective-permute-start | bytes 73736 | tf_op jit(solution)/shard_map/ppermute | solution.py:673
  360.4 56.5 %collective-permute-start.11 = (bf16[544,768]{1,0:T(8,128)(2,1)}, bf16[544,768]{1,0:T(8,128)(2,1)}, u32[]{:S(2)}, u32[]{:S(2)}) collective-permute-start(bf16[544,768]{1,0:T(8,128)(2,1)} %pad_maximum_fusion.8), channel_id=1, source_target_pairs={{0,1},{1,0},{2,3},{3,2},{4,5},{5,4},{6,7},{7,6},{8,9},{9,8},{10,11... | collective-permute-start | bytes 2506760 | tf_op jit(solution)/shard_map/ppermute | solution.py:805
  362.7 7.6 %collective-permute-start.18 = (bf16[24,128]{1,0:T(8,128)(2,1)S(1)}, bf16[24,128]{1,0:T(8,128)(2,1)S(1)}, u32[]{:S(2)}, u32[]{:S(2)}) collective-permute-start(bf16[24,128]{1,0:T(8,128)(2,1)S(1)} %get-tuple-element.192), channel_id=1, source_target_pairs={{0,24},{1,25},{2,26},{3,27},{4,28},{5,29},{6,30},{7,31},{8,16},{9,... | collective-permute-start | bytes 18440 | tf_op jit(solution)/shard_map/ppermute | solution.py:673
  365.6 4.8 %collective-permute-start.17 = (bf16[24,128]{1,0:T(8,128)(2,1)S(1)}, bf16[24,128]{1,0:T(8,128)(2,1)S(1)}, u32[]{:S(2)}, u32[]{:S(2)}) collective-permute-start(bf16[24,128]{1,0:T(8,128)(2,1)S(1)} %get-tuple-element.193), channel_id=1, source_target_pairs={{0,16},{1,17},{2,18},{3,19},{4,20},{5,21},{6,22},{7,23},{8,24},{9,... | collective-permute-start | bytes 18440 | tf_op jit(solution)/shard_map/ppermute | solution.py:673
  365.8 6.1 %collective-permute-start.16 = (bf16[24,128]{1,0:T(8,128)(2,1)S(1)}, bf16[24,128]{1,0:T(8,128)(2,1)S(1)}, u32[]{:S(2)}, u32[]{:S(2)}) collective-permute-start(bf16[24,128]{1,0:T(8,128)(2,1)S(1)} %get-tuple-element.191), channel_id=1, source_target_pairs={{0,8},{1,9},{2,10},{3,11},{4,12},{5,13},{6,14},{7,15},{8,0},{9,1},... | collective-permute-start | bytes 18440 | tf_op jit(solution)/shard_map/ppermute | solution.py:673
  368.3 14.3 %collective-permute-start.21 = (bf16[4,24,2304]{2,1,0:T(8,128)(2,1)}, bf16[4,24,2304]{2,1,0:T(8,128)(2,1)}, u32[]{:S(2)}, u32[]{:S(2)}) collective-permute-start(bf16[4,24,2304]{2,1,0:T(8,128)(2,1)} %get-tuple-element.163), channel_id=1, source_target_pairs={{0,5},{1,4},{2,7},{3,6},{4,1},{5,0},{6,3},{7,2},{8,13},{9,12},{10,... | collective-permute-start | bytes 1327112 | tf_op jit(solution)/shard_map/ppermute | solution.py:673
  370.3 18.1 %collective-permute-start.20 = (bf16[4,24,2304]{2,1,0:T(8,128)(2,1)}, bf16[4,24,2304]{2,1,0:T(8,128)(2,1)}, u32[]{:S(2)}, u32[]{:S(2)}) collective-permute-start(bf16[4,24,2304]{2,1,0:T(8,128)(2,1)} %get-tuple-element.164), channel_id=1, source_target_pairs={{0,4},{1,5},{2,6},{3,7},{4,0},{5,1},{6,2},{7,3},{8,12},{9,13},{10,... | collective-permute-start | bytes 1327112 | tf_op jit(solution)/shard_map/ppermute | solution.py:673
  370.4 31.8 %collective-permute-start.19 = (bf16[4,24,2304]{2,1,0:T(8,128)(2,1)}, bf16[4,24,2304]{2,1,0:T(8,128)(2,1)}, u32[]{:S(2)}, u32[]{:S(2)}) collective-permute-start(bf16[4,24,2304]{2,1,0:T(8,128)(2,1)} %get-tuple-element.162), channel_id=1, source_target_pairs={{0,1},{1,0},{2,3},{3,2},{4,5},{5,4},{6,7},{7,6},{8,9},{9,8},{10,11... | collective-permute-start | bytes 1327112 | tf_op jit(solution)/shard_map/ppermute | solution.py:673
  403.9 7.8 %collective-permute-start.24 = (bf16[24,2304]{1,0:T(8,128)(2,1)S(1)}, bf16[24,2304]{1,0:T(8,128)(2,1)S(1)}, u32[]{:S(2)}, u32[]{:S(2)}) collective-permute-start(bf16[24,2304]{1,0:T(8,128)(2,1)S(1)} %get-tuple-element.183), channel_id=1, source_target_pairs={{0,24},{1,25},{2,26},{3,27},{4,28},{5,29},{6,30},{7,31},{8,16},{9,... | collective-permute-start | bytes 331784 | tf_op jit(solution)/shard_map/ppermute | solution.py:673
  406.8 9.4 %collective-permute-start.23 = (bf16[24,2304]{1,0:T(8,128)(2,1)S(1)}, bf16[24,2304]{1,0:T(8,128)(2,1)S(1)}, u32[]{:S(2)}, u32[]{:S(2)}) collective-permute-start(bf16[24,2304]{1,0:T(8,128)(2,1)S(1)} %get-tuple-element.184), channel_id=1, source_target_pairs={{0,16},{1,17},{2,18},{3,19},{4,20},{5,21},{6,22},{7,23},{8,24},{9,... | collective-permute-start | bytes 331784 | tf_op jit(solution)/shard_map/ppermute | solution.py:673
  406.9 9.3 %collective-permute-start.22 = (bf16[24,2304]{1,0:T(8,128)(2,1)S(1)}, bf16[24,2304]{1,0:T(8,128)(2,1)S(1)}, u32[]{:S(2)}, u32[]{:S(2)}) collective-permute-start(bf16[24,2304]{1,0:T(8,128)(2,1)S(1)} %get-tuple-element.182), channel_id=1, source_target_pairs={{0,8},{1,9},{2,10},{3,11},{4,12},{5,13},{6,14},{7,15},{8,0},{9,1},... | collective-permute-start | bytes 331784 | tf_op jit(solution)/shard_map/ppermute | solution.py:673
  (61 other events, 1098.1 us)
Sparse Core Ops, SparseCore 0:
  24.4 110.5 all-gather.2
  237.8 150.1 reduce-scatter.1

commit v2 on v1

--- a/solution.py
+++ b/solution.py
@@ -752,9 +752,11 @@
 def gelu_pair(upward):
     rate = (2.0 / jnp.pi) ** 0.5
     square = upward * upward
-    bend = jnp.tanh(rate * (upward + 0.044715 * (square * upward)))
-    gate = 0.5 * (1.0 + bend)
-    slope = gate + 0.5 * upward * (1.0 - bend * bend) * (rate * (1.0 + 3 * 0.044715 * square))
+    bend = jnp.tanh(upward * (rate + (rate * 0.044715) * square))
+    gate = 0.5 + 0.5 * bend
+    slope = gate + upward * (1.0 - bend * bend) * (
+        0.5 * rate + (1.5 * 0.044715 * rate) * square
+    )
     return (upward * gate).astype(B16), slope.astype(B16)
 
 
@@ -896,24 +898,25 @@
     grad_b_out = column_sum(grad_branch)
     grad_mixed = through(grad_branch, full_out).astype(B16)
     grad_joined = attend_backward(joined, grad_mixed, lse, biases)
-    grad_qkv = weight_grad(normed_one, grad_joined)
-    grad_qkv, grad_joined = lax.optimization_barrier((grad_qkv, grad_joined))
     grad_b_qv = jnp.concatenate(
         [column_sum(grad_joined[:, :D]), column_sum(grad_joined[:, 2 * D :])]
     )
-    first = scatter_core(grad_qkv)
-    back_one = through(grad_joined, full_qkv)
-    first, back_one = lax.optimization_barrier((first, back_one))
-    grad_input, grad_gain_one, grad_shift_one = normalize_back(flat_x, gain_one, back_one)
-    dx_prompt, dx_cont = return_rows(grad_resid + grad_input, F32)
-
+    grad_input, grad_gain_one, grad_shift_one = normalize_back(
+        flat_x, gain_one, through(grad_joined, full_qkv)
+    )
+    grad_x = grad_resid + grad_input
+    dx_prompt, dx_cont = return_rows(grad_x, F32)
     small = (
         grad_gain_one, grad_shift_one, grad_b_qv, grad_b_out,
         grad_gain_two, grad_shift_two, grad_b_up, grad_b_down,
     )
-    own_first = scatter_chips(first)
-    own_vectors = scatter_steps(pack_vectors(small, B16))
-    grad_w_qkv = own_first
+    small, grad_x, grad_joined = lax.optimization_barrier(
+        (pack_vectors(small, B16), grad_x, grad_joined)
+    )
+    grad_qkv = weight_grad(normed_one, grad_joined)
+    own_first = scatter_steps(jnp.concatenate([grad_qkv, small], 1))
+    grad_w_qkv = own_first[:, : 3 * D]
+    own_vectors = own_first[:, 3 * D :]
     pieces = unpack_vectors(own_vectors, sizes)
     return (
         y_prompt, y_cont, dx_prompt, dx_cont,

time: 437 us -> 414 us (0.947)
  other arithmetic: 55.9 us -> 48.6 us
  local copies, waits for them, and re-layouts: 49.9 us -> 44.4 us
  starting transfers between devices: 40.7 us -> 35.3 us
    ppermute x28 -> x21, waiting for transfers between devices: 73.4 us -> 64.1 us  [swap(): lax.ppermute(value, EVERY, [(i, i ^ mask) for i in range(device_count())])]
    ppermute x2, waiting for transfers between devices: 0.01 us -> 7.72 us  [return_rows(): lax.ppermute(jnp.concatenate(away, 0).astype(B16), 'fsdp', [(0, 1), (1, 0)])]
    ppermute x28 -> x21, starting transfers between devices: 35.6 us -> 31.1 us  [swap(): lax.ppermute(value, EVERY, [(i, i ^ mask) for i in range(device_count())])]
    unnamed x127 -> x143, local copies, waits for them, and re-layouts: 20.3 us -> 18.6 us
  transfers between devices with their start and end apart: 34 -> 27, of which waited for: 14 -> 17; matrix products, arithmetic and copies ran while one was open for 25% -> 25% of each run, Pallas kernels for 20% -> 22%
where the time goes in v2:
time: 414 us; the launch traced here: 409 us
  matrix products  90.6 us (22%)
  Pallas kernels  88.5 us (21%)
  waiting for transfers between devices  86.6 us (21%)
  other arithmetic  48.6 us (12%)
  local copies, waits for them, and re-layouts  44.4 us (11%)
  starting transfers between devices  35.3 us (9%)
  between operations  15.4 us (4%)
    ppermute x21, waiting for transfers between devices, swap(): lax.ppermute(value, EVERY, [(i, i ^ mask) for i in range(device_count())])  64.1 us
    pallas_call x1, Pallas kernels, attend_backward(): pl.pallas_call(backward_kernel, grid=(HEADS,), in_specs=[pair_spec(lambda...  49 us
    pallas_call x1, Pallas kernels, attend_forward(): pl.pallas_call(forward_kernel, grid=(HEADS,), in_specs=[pair_spec(lambda...  39.5 us
    ppermute x21, starting transfers between devices, swap(): lax.ppermute(value, EVERY, [(i, i ^ mask) for i in range(device_count())])  31.1 us
    dot_general x4, matrix products, through(): return jnp.einsum('re,de->rd', grad, weight, preferred_element_type=F32)  30 us
    dot_general x4, matrix products, weight_grad(): jnp.einsum('rd,re->de', left, right, preferred_element_type=F32).astype(B16)  22.2 us
    unnamed x143, local copies, waits for them, and re-layouts  18.6 us
    dot_general x1, matrix products, whole_steps(): upward = jnp.dot(normed_two, full_up, preferred_element_type=F32) + bias_up  17.5 us
  transfers between devices with their start and end apart: 27, of which 17 were waited for; matrix products, arithmetic and copies ran while one was open for 25% of the time, Pallas kernels for 22%

profile of v2, /device:TPU:0, one launch (start us, length us, event | category | flops | bytes accessed | tf_op | source)
XLA Modules:
  0.0 409.4 jit_solution(180810704805077721)
XLA Ops:
  9.3 3.1 collective-permute-start.1
  12.4 2.6 collective-permute-start.2
  19.8 4.5 %collective-permute-done.2 = bf16[24,2432]{1,0:T(8,128)(2,1)S(1)} collective-permute-done((bf16[24,2432]{1,0:T(8,128)(2,1)S(1)}, bf16[24,2432]{1,0:T(8,128)(2,1)S(1)}, u32[]{:S(2)}, u32[]{:S(2)}) %collective-permute-start.2) | collective-permute-done | bytes 116768 | tf_op jit(solution)/shard_map/ppermute | solution.py:673
  30.5 10.9 %collective-permute-done.5 = bf16[4,24,2432]{2,1,0:T(8,128)(2,1)S(1)} collective-permute-done((bf16[4,24,2432]{2,1,0:T(8,128)(2,1)}, bf16[4,24,2432]{2,1,0:T(8,128)(2,1)S(1)}, u32[]{:S(2)}, u32[]{:S(2)}) %collective-permute-start.5) | collective-permute-done | bytes 466976 | tf_op jit(solution)/shard_map/ppermute | solution.py:673
  41.4 7.6 %collective-permute-done.4 = bf16[4,24,2432]{2,1,0:T(8,128)(2,1)S(1)} collective-permute-done((bf16[4,24,2432]{2,1,0:T(8,128)(2,1)}, bf16[4,24,2432]{2,1,0:T(8,128)(2,1)S(1)}, u32[]{:S(2)}, u32[]{:S(2)}) %collective-permute-start.4) | collective-permute-done | bytes 466976 | tf_op jit(solution)/shard_map/ppermute | solution.py:673
  49.1 5.3 %collective-permute-done.6 = bf16[4,24,2432]{2,1,0:T(8,128)(2,1)S(1)} collective-permute-done((bf16[4,24,2432]{2,1,0:T(8,128)(2,1)}, bf16[4,24,2432]{2,1,0:T(8,128)(2,1)S(1)}, u32[]{:S(2)}, u32[]{:S(2)}) %collective-permute-start.6) | collective-permute-done | bytes 466976 | tf_op jit(solution)/shard_map/ppermute | solution.py:673
  58.4 14.8 %collective-permute-done = bf16[544,768]{1,0:T(8,128)(2,1)} collective-permute-done((bf16[544,768]{1,0:T(8,128)(2,1)S(1)}, bf16[544,768]{1,0:T(8,128)(2,1)}, u32[]{:S(2)}, u32[]{:S(2)}) %collective-permute-start) | collective-permute-done | bytes 835616 | tf_op jit(solution)/shard_map/ppermute | solution.py:783
  82.9 10.3 %fusion.q_ref.k_ref.v_ref = bf16[1088,2304]{1,0:T(8,128)(2,1)} fusion(f32[2304]{0:T(1024)S(1)} %pad_maximum_fusion.15, bf16[768,2432]{1,0:T(8,128)(2,1)} %bitcast.214, f32[768]{0:T(1024)S(1)} %reshape.435, f32[768]{0:T(1024)S(1)} %reshape.434, f32[1088]{0:T(1024)S(1)} %copy-done.46, f32[1088]{0:T(1024)S(1)} %broadcast_multiply_fusion.5, ...), kind=kOutput, calls=%fused_computation.8 | convolution fusion | flops 3866247168 | bytes 10247680 | tf_op jit(solution)/shard_map/dot_general | solution.py:850
  95.5 39.5 %attend_forward.1 = (bf16[1088,768]{1,0:T(8,128)(2,1)}, f32[12,1,1088]{2,1,0:T(1,128)}, f32[256,256]{1,0:T(8,128)}, f32[512,256]{1,0:T(8,128)}, f32[768,256]{1,0...) custom-call(bf16[1088,2304]{1,0:T(8,128)(2,1)} %fusion.q_ref.k_ref.v_ref, bf16[1088,2304]{1,0:T(8,128)(2,1)} %fusion.q_ref.k_ref.v_ref, ...), custom_call_target="tpu_custom_call" | custom-call | tf_op jit(solution)/shard_map/attend_forward/pallas_call | solution.py:603
  140.8 4.1 %fusion.46 = (bf16[32,24,768]{2,1,0:T(8,128)(2,1)S(1)}, bf16[32,24,768]{2,1,0:T(8,128)(2,1)S(1)}, bf16[32,24,768]{2,1,0:T(8,128)(2,1)S(1)}, bf16[32,24,768]{2,1,0:T(8,128)(2,1)}, bf16[32,24,768]{2,1,0:T(8,128)(2,1)S(1)}) fusion(bf16[32,216,768]{2,1,0:T(8,128)(2,1)} %bitcast.204), kind=kLoop, calls=%fused_computation.211 | loop fusion | bytes 11796480 | tf_op jit(solution)/shard_map/slice | solution.py:843
  145.0 4.4 %slice.328 = bf16[32,96,768]{2,1,0:T(8,128)(2,1)S(1)} slice(bf16[32,216,768]{2,1,0:T(8,128)(2,1)} %bitcast.205), slice={[0:32], [120:216], [0:768]} | slice | bytes 9437184 | tf_op jit(solution)/shard_map/slice | solution.py:845
  152.3 17.5 %add_convert_fusion = (bf16[1088,3072]{1,0:T(8,128)(2,1)}, bf16[1088,3072]{1,0:T(8,128)(2,1)}) fusion(f32[3072]{0:T(1024)S(1)} %copy-done.54, bf16[768,768]{1,0:T(8,128)(2,1)S(1)} %bitcast.220, bf16[768,768]{1,0:T(8,128)(2,1)S(1)} %bitcast.222, bf16[768,768]{1,0:T(8,128)(2,1)} %bitcast.224, bf16[768,768]{1,0:T(8,128)(2,1)S(1)} %bitcast.218, ...), kind=kOutput, calls=%fused_computation.3 | convolution fusion | flops 5213700096 | bytes 21457408 | tf_op jit(solution)/shard_map/dot_general | solution.py:857
  169.8 7.7 %fusion.1 = bf16[1088,3072]{1,0:T(8,128)(2,1)S(1)} fusion(bf16[1088,3072]{1,0:T(8,128)(2,1)} %get-tuple-element.47, bf16[3072,768]{1,0:T(8,128)(2,1)S(1)} %bitcast.210, bf16[64,768]{1,0:T(8,128)(2,1)S(1)} %copy-done.40, bf16[64,768]{1,0:T(8,128)(2,1)S(1)} %copy-done.38, bf16[480,768]{1,0:T(8,128)(2,1)S(1)} %copy-done.19, bf16[480,768]{1,0:T(8,128)(2,1)S(1)} %copy-done.17), kind=kOutput, calls=%fused_computation.9 | convolution fusion | flops 5150539776 | bytes 19759104 | tf_op jit(solution)/shard_map/re,de->rd/dot_general | solution.py:864
  177.5 7.8 %convolution_convert_fusion.2 = bf16[768,3072]{1,0:T(8,128)(2,1)S(1)} fusion(bf16[1088,3072]{1,0:T(8,128)(2,1)S(1)} %fusion.1, f32[1088,768]{1,0:T(8,128)S(1)} %get-tuple-element.183, f32[768]{0:T(1024)S(1)} %copy-done.58, f32[768]{0:T(1024)S(1)} %copy-done.52, f32[1088]{0:T(1024)S(1)} %add_rsqrt_fusion, f32[1088]{0:T(1024)S(1)} %broadcast_multiply_fusion.4), kind=kOutput, calls=%fused_computation.12 | convolution fusion | flops 5140365312 | bytes 14760448 | tf_op jit(solution)/shard_map/rd,re->de/dot_general | solution.py:861
  189.0 6.8 %convolution_convert_fusion.1 = bf16[3072,768]{1,0:T(8,128)(2,1)S(1)} fusion(bf16[1088,3072]{1,0:T(8,128)(2,1)S(1)} %copy-done.64, bf16[64,768]{1,0:T(8,128)(2,1)S(1)} %copy-done.41, bf16[64,768]{1,0:T(8,128)(2,1)S(1)} %copy-done.38, bf16[480,768]{1,0:T(8,128)(2,1)S(1)} %copy-done.20, bf16[480,768]{1,0:T(8,128)(2,1)S(1)} %copy-done.17), kind=kOutput, calls=%fused_computation.11 | convolution fusion | flops 5142872064 | bytes 13074432 | tf_op jit(solution)/shard_map/rd,re->de/dot_general | solution.py:861
  201.6 9.0 %fusion.9 = bf16[1088,768]{1,0:T(8,128)(2,1)S(1)} fusion(f32[1088,768]{1,0:T(8,128)S(1)} %get-tuple-element.183, bf16[1088,3072]{1,0:T(8,128)(2,1)} %get-tuple-element.49, bf16[3072,768]{1,0:T(8,128)(2,1)} %bitcast.211, f32[768]{0:T(1024)} %reshape.440), kind=kOutput, calls=%fused_computation.28 | convolution fusion | flops 5136334848 | bytes 16419840 | tf_op jit(solution)/shard_map/dot_general | solution.py:887
  214.4 9.8 %multiply_reduce_fusion = (bf16[768]{0:T(1024)(128)(2,1)}, f32[1088]{0:T(1024)S(1)}, f32[1088]{0:T(1024)S(1)}, bf16[768]{0:T(1024)(128)(2,1)}, f32[1088,768]{1,0:T(8,128)S(1)}) fusion(f32[1088,768]{1,0:T(8,128)S(1)} %get-tuple-element.183, f32[1088]{0:T(1024)S(1)} %copy-done.44, f32[1088]{0:T(1024)S(1)} %broadcast_multiply_fusion.4, ...), kind=kOutput, calls=%fused_computation.38 | convolution fusion | flops 5160218624 | bytes 18111488 | tf_op jit(solution)/shard_map/re,de->rd/dot_general | solution.py:864
  224.2 3.7 convert_reduce_fusion.1
  229.7 2.7 convolution_convert_fusion.3.g_ref
  232.4 49.0 %attend_backward.1 = bf16[1088,2304]{1,0:T(8,128)(2,1)} custom-call(bf16[1088,2304]{1,0:T(8,128)(2,1)} %fusion.q_ref.k_ref.v_ref, bf16[1088,2304]{1,0:T(8,128)(2,1)} %fusion.q_ref.k_ref.v_ref, bf16[1088,2304]{1,0:T(8,128)(2,1)} %fusion.q_ref.k_ref.v_ref, bf16[1088,768]{1,0:T(8,128)(2,1)} %convolution_convert_fusion.3.g_ref, ...), custom_call_target="tpu_custom_call" | custom-call | tf_op jit(solution)/shard_map/attend_backward/pallas_call | solution.py:628
  281.5 9.9 %fusion.16 = (bf16[768]{0:T(1024)(128)(2,1)S(1)}, f32[1088]{0:T(1024)S(1)}, f32[1088]{0:T(1024)S(1)}, bf16[768]{0:T(1024)(128)(2,1)S(1)}, f32[1088,768]{1,0:T(8,128)}) fusion(f32[1088]{0:T(1024)S(1)} %copy-done.47, f32[1088]{0:T(1024)S(1)} %broadcast_multiply_fusion.5, bf16[64,768]{1,0:T(8,128)(2,1)S(1)} %get-tuple-element.150, ...), kind=kOutput, calls=%fused_computation.36 | convolution fusion | flops 3864572416 | bytes 13589504 | tf_op jit(solution)/shard_map/re,de->rd/dot_general | solution.py:864
  294.6 3.9 reduce.3
  298.9 5.1 %fusion.15 = f32[1088,768]{1,0:T(8,128)S(1)} fusion(f32[1088,768]{1,0:T(8,128)} %copy-done, f32[1088,768]{1,0:T(8,128)} %get-tuple-element.185, f32[1088]{0:T(1024)S(1)} %broadcast_multiply_fusion, f32[1088]{0:T(1024)S(1)} %broadcast_multiply_fusion.1, f32[768]{0:T(1024)} %copy-done.49, f32[1088]{0:T(1024)} %add_rsqrt_fusion.1, ...), kind=kLoop, calls=%fused_computation.35 | loop fusion | flops 13369344 | bytes 11718656 | tf_op jit(solution)/shard_map/add | solution.py:907
  307.1 5.8 %convolution_convert_fusion = bf16[768,2304]{1,0:T(8,128)(2,1)S(1)} fusion(bf16[1088,2304]{1,0:T(8,128)(2,1)S(1)} %bitcast.203, f32[768]{0:T(1024)S(1)} %copy-done.57, f32[768]{0:T(1024)S(1)} %copy-done.51, f32[1088]{0:T(1024)S(1)} %copy-done.48, f32[1088]{0:T(1024)S(1)} %broadcast_multiply_fusion.5, bf16[64,768]{1,0:T(8,128)(2,1)S(1)} %get-tuple-element.150, ...), kind=kOutput, calls=%fused_computation.10 | convolution fusion | flops 3863003136 | bytes 10238464 | tf_op jit(solution)/shard_map/rd,re->de/dot_general | solution.py:861
  320.9 3.2 collective-permute-done.21
  327.5 2.6 collective-permute-start.24
  333.4 4.2 %collective-permute-start.22 = (bf16[24,768]{1,0:T(8,128)(2,1)}, bf16[24,768]{1,0:T(8,128)(2,1)}, u32[]{:S(2)}, u32[]{:S(2)}) collective-permute-start(bf16[24,768]{1,0:T(8,128)(2,1)} %get-tuple-element.165), channel_id=1, source_target_pairs={{0,8},{1,9},{2,10},{3,11},{4,12},{5,13},{6,14},{7,15},{8,0},{9,1},... | collective-permute-start | bytes 110600 | tf_op jit(solution)/shard_map/ppermute | solution.py:673
  345.4 7.7 %collective-permute-done.10 = bf16[544,768]{1,0:T(8,128)(2,1)} collective-permute-done((bf16[544,768]{1,0:T(8,128)(2,1)}, bf16[544,768]{1,0:T(8,128)(2,1)}, u32[]{:S(2)}, u32[]{:S(2)}) %collective-permute-start.10) | collective-permute-done | bytes 835616 | tf_op jit(solution)/shard_map/ppermute | solution.py:807
  364.8 9.6 %collective-permute-done.14 = bf16[4,24,2432]{2,1,0:T(8,128)(2,1)S(1)} collective-permute-done((bf16[4,24,2432]{2,1,0:T(8,128)(2,1)S(1)}, bf16[4,24,2432]{2,1,0:T(8,128)(2,1)S(1)}, u32[]{:S(2)}, u32[]{:S(2)}) %collective-permute-start.14) | collective-permute-done | bytes 466976 | tf_op jit(solution)/shard_map/ppermute | solution.py:673
  374.4 7.2 %collective-permute-done.13 = bf16[4,24,2432]{2,1,0:T(8,128)(2,1)S(1)} collective-permute-done((bf16[4,24,2432]{2,1,0:T(8,128)(2,1)S(1)}, bf16[4,24,2432]{2,1,0:T(8,128)(2,1)S(1)}, u32[]{:S(2)}, u32[]{:S(2)}) %collective-permute-start.13) | collective-permute-done | bytes 466976 | tf_op jit(solution)/shard_map/ppermute | solution.py:673
  382.7 2.7 collective-permute-start.17
  389.9 7.4 %collective-permute-done.16 = bf16[24,2432]{1,0:T(8,128)(2,1)S(1)} collective-permute-done((bf16[24,2432]{1,0:T(8,128)(2,1)S(1)}, bf16[24,2432]{1,0:T(8,128)(2,1)S(1)}, u32[]{:S(2)}, u32[]{:S(2)}) %collective-permute-start.16) | collective-permute-done | bytes 116768 | tf_op jit(solution)/shard_map/ppermute | solution.py:673
  (296 shorter events, 104.0 us)
Async XLA Ops:
  7.2 133.6 %all-gather.3.cloned.1.call-start = ((), (), s32[]{:S(2)}) async-start(), calls=%async_computation.2 | async-start | bytes 10948608 | tf_op jit(solution)/shard_map/all_gather | solution.py:835
  9.3 10.5 %collective-permute-start.1 = (bf16[24,2432]{1,0:T(8,128)(2,1)S(1)}, bf16[24,2432]{1,0:T(8,128)(2,1)S(1)}, u32[]{:S(2)}, u32[]{:S(2)}) collective-permute-start(bf16[24,2432]{1,0:T(8,128)(2,1)S(1)} %pad_maximum_fusion.14), channel_id=1, source_target_pairs={{0,8},{1,9},{2,10},{3,11},{4,12},{5,13},{6,14},{7,15},{8,0},{9,1},... | collective-permute-start | bytes 350216 | tf_op jit(solution)/shard_map/ppermute | solution.py:673
  12.4 11.9 %collective-permute-start.2 = (bf16[24,2432]{1,0:T(8,128)(2,1)S(1)}, bf16[24,2432]{1,0:T(8,128)(2,1)S(1)}, u32[]{:S(2)}, u32[]{:S(2)}) collective-permute-start(bf16[24,2432]{1,0:T(8,128)(2,1)S(1)} %pad_maximum_fusion.14), channel_id=1, source_target_pairs={{0,16},{1,17},{2,18},{3,19},{4,20},{5,21},{6,22},{7,23},{8,24},{9,... | collective-permute-start | bytes 350216 | tf_op jit(solution)/shard_map/ppermute | solution.py:673
  15.0 9.3 %collective-permute-start.3 = (bf16[24,2432]{1,0:T(8,128)(2,1)S(1)}, bf16[24,2432]{1,0:T(8,128)(2,1)S(1)}, u32[]{:S(2)}, u32[]{:S(2)}) collective-permute-start(bf16[24,2432]{1,0:T(8,128)(2,1)S(1)} %pad_maximum_fusion.14), channel_id=1, source_target_pairs={{0,24},{1,25},{2,26},{3,27},{4,28},{5,29},{6,30},{7,31},{8,16},{9,... | collective-permute-start | bytes 350216 | tf_op jit(solution)/shard_map/ppermute | solution.py:673
  24.3 375.7 %reduce-scatter.2.cloned.1.call-start = ((), (), s32[]{:S(2)}) async-start(), calls=%async_computation.1 | async-start | bytes 9732096 | tf_op jit(solution)/shard_map/reduce_scatter | solution.py:882
  25.3 16.1 %collective-permute-start.5 = (bf16[4,24,2432]{2,1,0:T(8,128)(2,1)}, bf16[4,24,2432]{2,1,0:T(8,128)(2,1)S(1)}, u32[]{:S(2)}, u32[]{:S(2)}) collective-permute-start(bf16[4,24,2432]{2,1,0:T(8,128)(2,1)} %pad_maximum_fusion.12), channel_id=1, source_target_pairs={{0,4},{1,5},{2,6},{3,7},{4,0},{5,1},{6,2},{7,3},{8,12},{9,13},{10,... | collective-permute-start | bytes 1400840 | tf_op jit(solution)/shard_map/ppermute | solution.py:673
  26.8 22.3 %collective-permute-start.4 = (bf16[4,24,2432]{2,1,0:T(8,128)(2,1)}, bf16[4,24,2432]{2,1,0:T(8,128)(2,1)S(1)}, u32[]{:S(2)}, u32[]{:S(2)}) collective-permute-start(bf16[4,24,2432]{2,1,0:T(8,128)(2,1)} %pad_maximum_fusion.12), channel_id=1, source_target_pairs={{0,5},{1,4},{2,7},{3,6},{4,1},{5,0},{6,3},{7,2},{8,13},{9,12},{10,... | collective-permute-start | bytes 1400840 | tf_op jit(solution)/shard_map/ppermute | solution.py:673
  28.3 26.2 %collective-permute-start.6 = (bf16[4,24,2432]{2,1,0:T(8,128)(2,1)}, bf16[4,24,2432]{2,1,0:T(8,128)(2,1)S(1)}, u32[]{:S(2)}, u32[]{:S(2)}) collective-permute-start(bf16[4,24,2432]{2,1,0:T(8,128)(2,1)} %pad_maximum_fusion.12), channel_id=1, source_target_pairs={{0,1},{1,0},{2,3},{3,2},{4,5},{5,4},{6,7},{7,6},{8,9},{9,8},{10,11... | collective-permute-start | bytes 1400840 | tf_op jit(solution)/shard_map/ppermute | solution.py:673
  28.9 44.2 %collective-permute-start = (bf16[544,768]{1,0:T(8,128)(2,1)S(1)}, bf16[544,768]{1,0:T(8,128)(2,1)}, u32[]{:S(2)}, u32[]{:S(2)}) collective-permute-start(bf16[544,768]{1,0:T(8,128)(2,1)S(1)} %pad_maximum_fusion.6), channel_id=1, source_target_pairs={{0,1},{1,0},{2,3},{3,2},{4,5},{5,4},{6,7},{7,6},{8,9},{9,8},{10,11... | collective-permute-start | bytes 2506760 | tf_op jit(solution)/shard_map/ppermute | solution.py:783
  58.4 19.0 %collective-permute-start.7 = (bf16[4,2,2,24,2432]{4,3,2,1,0:T(8,128)(2,1)}, bf16[4,2,2,24,2432]{4,3,2,1,0:T(8,128)(2,1)}, u32[]{:S(2)}, u32[]{:S(2)}) collective-permute-start(bf16[4,2,2,24,2432]{4,3,2,1,0:T(8,128)(2,1)} %pad_maximum_fusion.3), channel_id=1, source_target_pairs={{0,2},{1,3},{2,0},{3,1},{4,6},{5,7},{6,4},{7,5},{8,10},{9,11},{10,... | collective-permute-start | bytes 5603336 | tf_op jit(solution)/shard_map/ppermute | solution.py:673
  94.3 43.4 %collective-permute-start.8 = (bf16[544,768]{1,0:T(8,128)(2,1)}, bf16[544,768]{1,0:T(8,128)(2,1)S(1)}, u32[]{:S(2)}, u32[]{:S(2)}) collective-permute-start(bf16[544,768]{1,0:T(8,128)(2,1)} %pad_maximum_fusion.7), channel_id=1, source_target_pairs={{0,1},{1,0},{2,3},{3,2},{4,5},{5,4},{6,7},{7,6},{8,9},{9,8},{10,11... | collective-permute-start | bytes 2506760 | tf_op jit(solution)/shard_map/ppermute | solution.py:783
  152.1 25.4 %copy-start.43 = (f32[1088]{0:T(1024)}, f32[1088]{0:T(1024)S(1)}, u32[]{:S(2)}) copy-start(f32[1088]{0:T(1024)S(1)} %add_rsqrt_fusion) | copy-start | bytes 13060
  212.8 129.7 %collective-permute-start.9 = (bf16[544,768]{1,0:T(8,128)(2,1)}, bf16[544,768]{1,0:T(8,128)(2,1)}, u32[]{:S(2)}, u32[]{:S(2)}) collective-permute-start(bf16[544,768]{1,0:T(8,128)(2,1)} %pad_maximum_fusion.8), channel_id=1, source_target_pairs={{0,1},{1,0},{2,3},{3,2},{4,5},{5,4},{6,7},{7,6},{8,9},{9,8},{10,11... | collective-permute-start | bytes 2506760 | tf_op jit(solution)/shard_map/ppermute | solution.py:807
  232.4 49.0 %copy-start.4 = (bf16[480,768]{1,0:T(8,128)(2,1)S(1)}, bf16[480,768]{1,0:T(8,128)(2,1)}, u32[]{:S(2)}) copy-start(bf16[480,768]{1,0:T(8,128)(2,1)} %copy-done.2) | copy-start | bytes 2211844
  232.4 49.0 %copy-start.8 = (bf16[480,768]{1,0:T(8,128)(2,1)S(1)}, bf16[480,768]{1,0:T(8,128)(2,1)}, u32[]{:S(2)}) copy-start(bf16[480,768]{1,0:T(8,128)(2,1)} %copy-done.6) | copy-start | bytes 2211844
  232.4 49.0 %copy-start.47 = (f32[1088]{0:T(1024)S(1)}, f32[1088]{0:T(1024)}, u32[]{:S(2)}) copy-start(f32[1088]{0:T(1024)} %add_rsqrt_fusion.1) | copy-start | bytes 13060
  232.4 49.0 %copy-start.50 = (f32[768]{0:T(1024)S(1)}, f32[768]{0:T(1024)}, u32[]{:S(2)}) copy-start(f32[768]{0:T(1024)} %copy-done.49) | copy-start | bytes 9220
  305.9 10.2 %collective-permute-start.18 = (bf16[4,2,2,24,768]{4,3,0,2,1:T(8,128)(2,1)S(1)}, bf16[4,2,2,24,768]{4,3,0,2,1:T(8,128)(2,1)S(1)}, u32[]{:S(2)}, u32[]{:S(2)}) collective-permute-start(bf16[4,2,2,24,768]{4,3,0,2,1:T(8,128)(2,1)S(1)} %bitcast.228), channel_id=1, source_target_pairs={{0,2},{1,3},{2,0},{3,1},{4,6},{5,7},{6,4},{7,5},{8,10},{9,11},{10,... | collective-permute-start | bytes 1769480 | tf_op jit(solution)/shard_map/ppermute | solution.py:673
  316.1 39.5 %collective-permute-start.11 = (bf16[4,2,2,24,2432]{4,3,0,2,1:T(8,128)(2,1)}, bf16[4,2,2,24,2432]{4,3,0,2,1:T(8,128)(2,1)}, u32[]{:S(2)}, u32[]{:S(2)}) collective-permute-start(bf16[4,2,2,24,2432]{4,3,0,2,1:T(8,128)(2,1)} %bitcast.199), channel_id=1, source_target_pairs={{0,2},{1,3},{2,0},{3,1},{4,6},{5,7},{6,4},{7,5},{8,10},{9,11},{10,... | collective-permute-start | bytes 5603336 | tf_op jit(solution)/shard_map/ppermute | solution.py:673
  316.3 7.7 %collective-permute-start.21 = (bf16[4,24,768]{2,1,0:T(8,128)(2,1)S(1)}, bf16[4,24,768]{2,1,0:T(8,128)(2,1)S(1)}, u32[]{:S(2)}, u32[]{:S(2)}) collective-permute-start(bf16[4,24,768]{2,1,0:T(8,128)(2,1)S(1)} %get-tuple-element.156), channel_id=1, source_target_pairs={{0,5},{1,4},{2,7},{3,6},{4,1},{5,0},{6,3},{7,2},{8,13},{9,12},{10,... | collective-permute-start | bytes 442376 | tf_op jit(solution)/shard_map/ppermute | solution.py:673
  317.9 7.9 %collective-permute-start.20 = (bf16[4,24,768]{2,1,0:T(8,128)(2,1)S(1)}, bf16[4,24,768]{2,1,0:T(8,128)(2,1)S(1)}, u32[]{:S(2)}, u32[]{:S(2)}) collective-permute-start(bf16[4,24,768]{2,1,0:T(8,128)(2,1)S(1)} %get-tuple-element.157), channel_id=1, source_target_pairs={{0,4},{1,5},{2,6},{3,7},{4,0},{5,1},{6,2},{7,3},{8,12},{9,13},{10,... | collective-permute-start | bytes 442376 | tf_op jit(solution)/shard_map/ppermute | solution.py:673
  318.4 8.4 %collective-permute-start.19 = (bf16[4,24,768]{2,1,0:T(8,128)(2,1)S(1)}, bf16[4,24,768]{2,1,0:T(8,128)(2,1)S(1)}, u32[]{:S(2)}, u32[]{:S(2)}) collective-permute-start(bf16[4,24,768]{2,1,0:T(8,128)(2,1)S(1)} %get-tuple-element.155), channel_id=1, source_target_pairs={{0,1},{1,0},{2,3},{3,2},{4,5},{5,4},{6,7},{7,6},{8,9},{9,8},{10,11... | collective-permute-start | bytes 442376 | tf_op jit(solution)/shard_map/ppermute | solution.py:673
  324.1 29.1 %collective-permute-start.10 = (bf16[544,768]{1,0:T(8,128)(2,1)}, bf16[544,768]{1,0:T(8,128)(2,1)}, u32[]{:S(2)}, u32[]{:S(2)}) collective-permute-start(bf16[544,768]{1,0:T(8,128)(2,1)} %pad_maximum_fusion.9), channel_id=1, source_target_pairs={{0,1},{1,0},{2,3},{3,2},{4,5},{5,4},{6,7},{7,6},{8,9},{9,8},{10,11... | collective-permute-start | bytes 2506760 | tf_op jit(solution)/shard_map/ppermute | solution.py:807
  327.5 5.9 %collective-permute-start.24 = (bf16[24,768]{1,0:T(8,128)(2,1)S(1)}, bf16[24,768]{1,0:T(8,128)(2,1)S(1)}, u32[]{:S(2)}, u32[]{:S(2)}) collective-permute-start(bf16[24,768]{1,0:T(8,128)(2,1)S(1)} %get-tuple-element.166), channel_id=1, source_target_pairs={{0,24},{1,25},{2,26},{3,27},{4,28},{5,29},{6,30},{7,31},{8,16},{9,... | collective-permute-start | bytes 110600 | tf_op jit(solution)/shard_map/ppermute | solution.py:673
  330.1 9.6 %collective-permute-start.23 = (bf16[24,768]{1,0:T(8,128)(2,1)}, bf16[24,768]{1,0:T(8,128)(2,1)}, u32[]{:S(2)}, u32[]{:S(2)}) collective-permute-start(bf16[24,768]{1,0:T(8,128)(2,1)} %get-tuple-element.167), channel_id=1, source_target_pairs={{0,16},{1,17},{2,18},{3,19},{4,20},{5,21},{6,22},{7,23},{8,24},{9,... | collective-permute-start | bytes 110600 | tf_op jit(solution)/shard_map/ppermute | solution.py:673
  333.4 7.7 %collective-permute-start.22 = (bf16[24,768]{1,0:T(8,128)(2,1)}, bf16[24,768]{1,0:T(8,128)(2,1)}, u32[]{:S(2)}, u32[]{:S(2)}) collective-permute-start(bf16[24,768]{1,0:T(8,128)(2,1)} %get-tuple-element.165), channel_id=1, source_target_pairs={{0,8},{1,9},{2,10},{3,11},{4,12},{5,13},{6,14},{7,15},{8,0},{9,1},... | collective-permute-start | bytes 110600 | tf_op jit(solution)/shard_map/ppermute | solution.py:673
  357.7 16.7 %collective-permute-start.14 = (bf16[4,24,2432]{2,1,0:T(8,128)(2,1)S(1)}, bf16[4,24,2432]{2,1,0:T(8,128)(2,1)S(1)}, u32[]{:S(2)}, u32[]{:S(2)}) collective-permute-start(bf16[4,24,2432]{2,1,0:T(8,128)(2,1)S(1)} %get-tuple-element.140), channel_id=1, source_target_pairs={{0,5},{1,4},{2,7},{3,6},{4,1},{5,0},{6,3},{7,2},{8,13},{9,12},{10,... | collective-permute-start | bytes 1400840 | tf_op jit(solution)/shard_map/ppermute | solution.py:673
  359.3 22.3 %collective-permute-start.13 = (bf16[4,24,2432]{2,1,0:T(8,128)(2,1)S(1)}, bf16[4,24,2432]{2,1,0:T(8,128)(2,1)S(1)}, u32[]{:S(2)}, u32[]{:S(2)}) collective-permute-start(bf16[4,24,2432]{2,1,0:T(8,128)(2,1)S(1)} %get-tuple-element.141), channel_id=1, source_target_pairs={{0,4},{1,5},{2,6},{3,7},{4,0},{5,1},{6,2},{7,3},{8,12},{9,13},{10,... | collective-permute-start | bytes 1400840 | tf_op jit(solution)/shard_map/ppermute | solution.py:673
  359.8 22.7 %collective-permute-start.12 = (bf16[4,24,2432]{2,1,0:T(8,128)(2,1)S(1)}, bf16[4,24,2432]{2,1,0:T(8,128)(2,1)S(1)}, u32[]{:S(2)}, u32[]{:S(2)}) collective-permute-start(bf16[4,24,2432]{2,1,0:T(8,128)(2,1)S(1)} %get-tuple-element.139), channel_id=1, source_target_pairs={{0,1},{1,0},{2,3},{3,2},{4,5},{5,4},{6,7},{7,6},{8,9},{9,8},{10,11... | collective-permute-start | bytes 1400840 | tf_op jit(solution)/shard_map/ppermute | solution.py:673
  382.7 7.2 %collective-permute-start.17 = (bf16[24,2432]{1,0:T(8,128)(2,1)S(1)}, bf16[24,2432]{1,0:T(8,128)(2,1)S(1)}, u32[]{:S(2)}, u32[]{:S(2)}) collective-permute-start(bf16[24,2432]{1,0:T(8,128)(2,1)S(1)} %get-tuple-element.159), channel_id=1, source_target_pairs={{0,24},{1,25},{2,26},{3,27},{4,28},{5,29},{6,30},{7,31},{8,16},{9,... | collective-permute-start | bytes 350216 | tf_op jit(solution)/shard_map/ppermute | solution.py:673
  385.4 11.9 %collective-permute-start.16 = (bf16[24,2432]{1,0:T(8,128)(2,1)S(1)}, bf16[24,2432]{1,0:T(8,128)(2,1)S(1)}, u32[]{:S(2)}, u32[]{:S(2)}) collective-permute-start(bf16[24,2432]{1,0:T(8,128)(2,1)S(1)} %get-tuple-element.160), channel_id=1, source_target_pairs={{0,16},{1,17},{2,18},{3,19},{4,20},{5,21},{6,22},{7,23},{8,24},{9,... | collective-permute-start | bytes 350216 | tf_op jit(solution)/shard_map/ppermute | solution.py:673
  387.8 9.5 %collective-permute-start.15 = (bf16[24,2432]{1,0:T(8,128)(2,1)S(1)}, bf16[24,2432]{1,0:T(8,128)(2,1)S(1)}, u32[]{:S(2)}, u32[]{:S(2)}) collective-permute-start(bf16[24,2432]{1,0:T(8,128)(2,1)S(1)} %get-tuple-element.158), channel_id=1, source_target_pairs={{0,8},{1,9},{2,10},{3,11},{4,12},{5,13},{6,14},{7,15},{8,0},{9,1},... | collective-permute-start | bytes 350216 | tf_op jit(solution)/shard_map/ppermute | solution.py:673
  (62 other events, 411.6 us)
Sparse Core Ops, SparseCore 0:
  24.4 109.5 all-gather.2
  232.5 152.9 reduce-scatter.1

commit v3 on v2

--- a/solution.py
+++ b/solution.py
@@ -423,10 +423,11 @@
     return jnp.where(lane // HEAD_DIM == half, values, 0.0).astype(B16)
 
 
-def block_masks(place):
+def block_masks(place, low=0, high=None):
     first, rows, keys = BLOCKS[place]
-    key_id = lax.broadcasted_iota(jnp.int32, (keys, rows), 0)
-    row_id = first + lax.broadcasted_iota(jnp.int32, (keys, rows), 1)
+    shape = ((high or keys) - low, rows)
+    key_id = low + lax.broadcasted_iota(jnp.int32, shape, 0)
+    row_id = first + lax.broadcasted_iota(jnp.int32, shape, 1)
     visible = key_id <= row_id
     if first >= SEQ:
         visible = visible & ((key_id < PROMPT) | (key_id >= SEQ))
@@ -446,7 +447,11 @@
     return jnp.where((a > b) if later else (a < b), 1.0, 0.0).astype(B16)
 
 
-def forward_kernel(q_ref, k_ref, v_ref, o_ref, lse_ref, b0, b1, b2, b3, b4, vt_ref, ot_ref):
+def chunks_of(keys):
+    return [(low, min(low + 256, keys)) for low in range(0, keys, 256)]
+
+
+def forward_kernel(q_ref, k_ref, v_ref, o_ref, lse_ref, b0, b1, b2, b3, b4, vt_ref, ot_ref, logit_ref, share_ref):
     bias_refs = (b0, b1, b2, b3, b4)
     head = pl.program_id(0)
     half = head % 2
@@ -479,11 +484,19 @@
 
     own = pl.ds(pl.multiple_of(half * HEAD_DIM, HEAD_DIM), HEAD_DIM)
     for place, (first, rows, keys) in enumerate(BLOCKS):
-        logits = mm_nt(k_ref[:keys], queries[first : first + rows]) + bias_refs[place][...]
-        highest = jnp.max(logits, 0, keepdims=True)
-        raised = jnp.exp(logits - highest)
-        total = jnp.sum(raised, 0, keepdims=True)
-        mixed = mm(vt_ref[own, :keys], raised.astype(B16))
+        asked = queries[first : first + rows]
+        highest = None
+        for low, high in chunks_of(keys):
+            logits = mm_nt(k_ref[low:high], asked) + bias_refs[place][low:high]
+            logit_ref[low:high, first : first + rows] = logits
+            top = jnp.max(logits, 0, keepdims=True)
+            highest = top if highest is None else jnp.maximum(highest, top)
+        total = 0.0
+        for low, high in chunks_of(keys):
+            raised = jnp.exp(logit_ref[low:high, first : first + rows] - highest)
+            total = total + jnp.sum(raised, 0, keepdims=True)
+            share_ref[low:high, first : first + rows] = raised.astype(B16)
+        mixed = mm(vt_ref[own, :keys], share_ref[:keys, first : first + rows])
         ot_ref[own, first : first + rows] = mixed * (1.0 / total)
         lse_ref[0, :, first : first + rows] = highest + jnp.log(total)
 
@@ -493,9 +506,9 @@
 
 
 def backward_kernel(
-    q_ref, k_ref, v_ref, g_ref, lse_ref, b0, b1, b2, b3, b4,
+    q_ref, k_ref, v_ref, g_ref, o_ref, lse_ref, b0, b1, b2, b3, b4,
     joined_ref,
-    kt_ref, dqt_ref, dk_acc, dv_acc, p0, p1, p2, p3, p4, stage_ref, sems,
+    kt_ref, dqt_ref, dk_acc, dv_acc, p0, p1, p2, p3, p4, stage_ref, share_ref, grad_ref, inner_ref, sems,
 ):
     bias_refs = (b0, b1, b2, b3, b4)
     pen_refs = (p0, p1, p2, p3, p4)
@@ -513,51 +526,68 @@
     @pl.when(half == 1)
     def _():
         kt_ref[...] = k_ref[...].astype(F32).T.astype(B16)
+        both = (o_ref[...].astype(F32) * g_ref[...].astype(F32)).T
+        inner_ref[0] = jnp.sum(both[:HEAD_DIM], 0, keepdims=True)
+        inner_ref[1] = jnp.sum(both[HEAD_DIM:], 0, keepdims=True)
         dk_acc[...] = jnp.zeros_like(dk_acc)
         dv_acc[...] = jnp.zeros_like(dv_acc)
 
-    def softmax_grad(place):
+    def tile(place, low, high):
+        first, rows, _ = BLOCKS[place]
+        scores = mm_nt(k_ref[low:high], queries[first : first + rows])
+        shares = jnp.exp(
+            scores + bias_refs[place][low:high] - lse_ref[0, :, first : first + rows]
+        )
+        back = mm_nt(v_ref[low:high], grads[first : first + rows])
+        share_ref[low:high, first : first + rows] = shares.astype(B16)
+        return scores, shares * (back - inner_ref[half, :, first : first + rows])
+
+    def finish(low, high):
+        dv_acc[low:high] += mm(share_ref[low:high, low:], grads[low:])
+        dk_acc[low:high] += mm(grad_ref[low:high, low:], queries[low:])
+
+    def finish_queries(place):
         first, rows, keys = BLOCKS[place]
-        scores = mm_nt(k_ref[:keys], queries[first : first + rows])
-        shares = jnp.exp(scores + bias_refs[place][...] - lse_ref[0, :, first : first + rows])
-        back = mm_nt(v_ref[:keys], grads[first : first + rows])
-        inner = jnp.sum(shares * back, 0, keepdims=True)
-        dv_acc[:keys] += mm(shares.astype(B16), grads[first : first + rows])
-        return scores, shares * (back - inner)
-
-    def score_grad(place, grad):
-        first, rows, keys = BLOCKS[place]
-        grad = grad.astype(B16)
-        dqt_ref[own, first : first + rows] = mm(kt_ref[own, :keys], grad)
-        dk_acc[:keys] += mm(grad, queries[first : first + rows])
+        dqt_ref[own, first : first + rows] = mm(
+            kt_ref[own, :keys], grad_ref[:keys, first : first + rows]
+        )
 
     @pl.when(head != 0)
     def _():
-        for place in range(len(BLOCKS)):
-            _, grad = softmax_grad(place)
-            pen_refs[place][...] += grad
-            score_grad(place, grad)
+        for low, high in chunks_of(ROWS):
+            for place, (first, rows, keys) in enumerate(BLOCKS):
+                if low < keys:
+                    _, grad = tile(place, low, high)
+                    pen_refs[place][low:high] += grad
+                    grad_ref[low:high, first : first + rows] = grad.astype(B16)
+            finish(low, high)
+            finish_queries(low // 256)
 
     @pl.when(head == 0)
     def _():
-        carry = None
-        for place in reversed(range(len(BLOCKS))):
-            first, rows, keys = BLOCKS[place]
-            scores, grad = softmax_grad(place)
-            whole = pen_refs[place][...] + grad
-            later = split_mm(whole, triangle(rows, True))
-            total = jnp.sum(whole, 1, keepdims=True)
-            if carry is not None:
-                if first + rows == SEQ:
-                    lane = lax.broadcasted_iota(jnp.int32, (keys, rows), 1)
-                    later = later + jnp.where(lane < TAIL, carry[:keys], 0.0)
-                else:
-                    later = later + carry[:keys]
-                total = total + carry[:keys]
-            carry = total
-            _, chosen = block_masks(place)
-            grad = grad + jnp.where(chosen & (scores > 0.0), -SELECT_GAIN * later, 0.0)
-            score_grad(place, grad)
+        for low, high in chunks_of(ROWS):
+            carry = None
+            for place in reversed(range(len(BLOCKS))):
+                first, rows, keys = BLOCKS[place]
+                if low >= keys:
+                    continue
+                scores, grad = tile(place, low, high)
+                whole = pen_refs[place][low:high] + grad
+                later = split_mm(whole, triangle(rows, True))
+                total = jnp.sum(whole, 1, keepdims=True)
+                if carry is not None:
+                    if first + rows == SEQ:
+                        lane = lax.broadcasted_iota(jnp.int32, later.shape, 1)
+                        later = later + jnp.where(lane < TAIL, carry, 0.0)
+                    else:
+                        later = later + carry
+                    total = total + carry
+                carry = total
+                chosen = block_masks(place, low, high)[1]
+                grad = grad + jnp.where(chosen & (scores > 0.0), -SELECT_GAIN * later, 0.0)
+                grad_ref[low:high, first : first + rows] = grad.astype(B16)
+            finish(low, high)
+            finish_queries(low // 256)
 
     def copies(pair):
         return [
@@ -618,12 +648,17 @@
             jax.ShapeDtypeStruct((HEADS, 1, ROWS), F32),
             *(jax.ShapeDtypeStruct((keys, rows), F32) for _, rows, keys in BLOCKS),
         ],
-        scratch_shapes=[pltpu.VMEM((PAIR, ROWS), B16), pltpu.VMEM((PAIR, ROWS), F32)],
+        scratch_shapes=[
+            pltpu.VMEM((PAIR, ROWS), B16),
+            pltpu.VMEM((PAIR, ROWS), F32),
+            pltpu.VMEM((ROWS, ROWS), F32),
+            pltpu.VMEM((ROWS, ROWS), B16),
+        ],
         name="attend_forward",
     )(joined, joined, joined)
 
 
-def attend_backward(joined, grad_mixed, lse, biases):
+def attend_backward(joined, grad_mixed, mixed, lse, biases):
     last = PAIRS - 1
     return pl.pallas_call(
         backward_kernel,
@@ -632,6 +667,7 @@
             pair_spec(lambda i: (0, last - i // 2)),
             pair_spec(lambda i: (0, PAIRS + last - i // 2)),
             pair_spec(lambda i: (0, 2 * PAIRS + last - i // 2)),
+            pair_spec(lambda i: (0, last - i // 2)),
             pair_spec(lambda i: (0, last - i // 2)),
             pl.BlockSpec((1, 1, ROWS), lambda i: (HEADS - 1 - i, 0, 0)),
             *whole_specs(),
@@ -645,10 +681,13 @@
             pltpu.VMEM((ROWS, PAIR), F32),
             *(pltpu.VMEM((keys, rows), F32) for _, rows, keys in BLOCKS),
             pltpu.VMEM((3, ROWS, PAIR), B16),
+            pltpu.VMEM((ROWS, ROWS), B16),
+            pltpu.VMEM((ROWS, ROWS), B16),
+            pltpu.VMEM((2, 1, ROWS), F32),
             pltpu.SemaphoreType.DMA((3,)),
         ],
         name="attend_backward",
-    )(joined, joined, joined, grad_mixed, lse, *biases)
+    )(joined, joined, joined, grad_mixed, mixed, lse, *biases)
 
 
 EVERY = ("dp", "fsdp")
@@ -706,10 +745,6 @@
     return total
 
 
-def scatter_steps(grad):
-    return scatter_chips(scatter_core(grad))
-
-
 def scatter_core(grad):
     core = place_of()[2]
     rows = grad.shape[0] // device_count()
@@ -718,35 +753,53 @@
     return take(value, core, 2) + other
 
 
-def scatter_chips(value):
-    z, x, _, y = place_of()
+def scatter_plane(value):
+    _, x, _, y = place_of()
     plane = [
         take(take(value, x ^ (mask // 4), 1), y ^ (mask % 2), 1) for mask in PLANE
     ]
     others = [swap(piece, mask) for piece, mask in zip(plane[1:], PLANE[1:])]
-    value = add_up(plane[:1] + others).astype(B16)
+    return plane[:1] + others
+
+
+def scatter_column(plane):
+    z = place_of()[0]
+    value = add_up(plane).astype(B16)
     column = [take(value, z ^ k, 0) for k in range(depth())]
     others = [swap(column[k], 8 * k) for k in range(1, depth())]
     return add_up(column[:1] + others)
 
 
-def pack_vectors(vectors, kind):
+def pack_vectors(vectors):
     rows = D // device_count()
-    flat = jnp.concatenate([v.reshape(-1, v.shape[0] // vectors[0].shape[0] * rows) for v in vectors], 1)
-    flat = flat.astype(kind).reshape(-1, 3, flat.shape[1] // 3)
-    flat = jnp.pad(flat, ((0, 0), (0, rows - 3), (0, 128 - flat.shape[2])))
-    return flat.reshape(-1, 128)
+    padded = [jnp.pad(v, (0, 128 - v.shape[0]))[None] for v in vectors]
+    return jnp.pad(jnp.concatenate(padded, 0), ((0, rows - len(vectors)), (0, 0)))
 
 
 def unpack_vectors(columns, sizes):
-    rows = D // device_count()
-    width = sum(sizes) // 3
-    flat = columns.reshape(-1, rows, 128)[:, :3, :width].reshape(-1, 3 * width)
-    out, start = [], 0
-    for size in sizes:
-        out.append(flat[:, start : start + size].reshape(-1).astype(F32))
-        start += size
-    return out
+    rows = columns.reshape(-1, D // device_count(), 128)
+    return [rows[:, i, :size].reshape(-1).astype(F32) for i, size in enumerate(sizes)]
+
+
+def pack_kernel(*refs):
+    out_ref = refs[-1]
+    devices = out_ref.shape[0]
+    out_ref[...] = jnp.zeros_like(out_ref)
+    for i, ref in enumerate(refs[:-1]):
+        count = ref.shape[1]
+        piece = count // devices
+        values = ref[...]
+        for j in range(devices):
+            out_ref[j, i : i + 1, :piece] = values[:, j * piece : (j + 1) * piece]
+
+
+def pack_grads(vectors):
+    devices = device_count()
+    return pl.pallas_call(
+        pack_kernel,
+        out_shape=jax.ShapeDtypeStruct((devices, D // devices, 128), F32),
+        name="pack_grads",
+    )(*(v.astype(F32)[None] for v in vectors))
 
 
 def gelu_pair(upward):
@@ -794,7 +847,7 @@
     )
 
 
-def return_rows(whole, kind):
+def trade_back(whole):
     place = lax.axis_index("fsdp")
     low = place == 0
     half = PROMPT // 2
@@ -805,7 +858,12 @@
     mine = [pick(parts[0][i], parts[1][i], low) for i in range(2)]
     away = [pick(parts[1][i], parts[0][i], low) for i in range(2)]
     came = lax.ppermute(jnp.concatenate(away, 0).astype(B16), "fsdp", [(0, 1), (1, 0)])
-    came = (came[:half], came[half:])
+    return mine, came
+
+
+def join_rows(mine, came, kind):
+    low = lax.axis_index("fsdp") == 0
+    came = (came[: PROMPT // 2], came[PROMPT // 2 :])
     out = []
     for i in range(2):
         own, other = mine[i].astype(kind), came[i].astype(kind)
@@ -831,7 +889,9 @@
     rest = jnp.concatenate(
         [w_out, *(w_up[:, i * D : (i + 1) * D] for i in range(chunks)), w_down], 0
     )
-    full_first, rest = gather_steps(jnp.concatenate([w_qkv, pack_vectors(vectors, B16)], 1), rest)
+    full_first, rest = gather_steps(
+        jnp.concatenate([w_qkv, pack_vectors(vectors)], 1), rest
+    )
     full_rest = lax.all_gather(rest, EVERY, axis=0)
     full_qkv = full_first[:, : 3 * D]
     (
@@ -885,7 +945,7 @@
     )
     grad_w_down = own_hidden[chunks * rows :]
     output = residual + (jnp.dot(active, full_down, preferred_element_type=F32) + bias_down)
-    y_prompt, y_cont = return_rows(output.astype(B16), B16)
+    came_y = trade_back(output.astype(B16))
 
     grad_b_down = column_sum(grad_y)
     grad_b_up = column_sum(grad_upward)
@@ -894,10 +954,10 @@
     )
     grad_resid = grad_y.astype(F32) + grad_resid
     grad_branch = grad_resid.astype(B16)
-    grad_w_out = scatter_steps(weight_grad(mixed, grad_branch))
+    out_plane = scatter_plane(scatter_core(weight_grad(mixed, grad_branch)))
     grad_b_out = column_sum(grad_branch)
     grad_mixed = through(grad_branch, full_out).astype(B16)
-    grad_joined = attend_backward(joined, grad_mixed, lse, biases)
+    grad_joined = attend_backward(joined, grad_mixed, mixed, lse, biases)
     grad_b_qv = jnp.concatenate(
         [column_sum(grad_joined[:, :D]), column_sum(grad_joined[:, 2 * D :])]
     )
@@ -905,19 +965,28 @@
         flat_x, gain_one, through(grad_joined, full_qkv)
     )
     grad_x = grad_resid + grad_input
-    dx_prompt, dx_cont = return_rows(grad_x, F32)
+    came_x = trade_back(grad_x)
     small = (
         grad_gain_one, grad_shift_one, grad_b_qv, grad_b_out,
         grad_gain_two, grad_shift_two, grad_b_up, grad_b_down,
     )
     small, grad_x, grad_joined = lax.optimization_barrier(
-        (pack_vectors(small, B16), grad_x, grad_joined)
+        (pack_grads(small), grad_x, grad_joined)
     )
     grad_qkv = weight_grad(normed_one, grad_joined)
-    own_first = scatter_steps(jnp.concatenate([grad_qkv, small], 1))
+    first = scatter_core(
+        jnp.concatenate([grad_qkv, small.reshape(D, 128).astype(B16)], 1)
+    )
+    first, came_y, out_plane = lax.optimization_barrier((first, came_y, out_plane))
+    plane = scatter_plane(first)
+    plane, came_x = lax.optimization_barrier((plane, came_x))
+    own_first = scatter_column(plane)
+    dx_prompt, dx_cont = join_rows(*came_x, F32)
+    grad_w_out = scatter_column(out_plane)
+    y_prompt, y_cont = join_rows(*came_y, B16)
     grad_w_qkv = own_first[:, : 3 * D]
     own_vectors = own_first[:, 3 * D :]
-    pieces = unpack_vectors(own_vectors, sizes)
+    pieces = [own_vectors[i, :size] for i, size in enumerate(sizes)]
     return (
         y_prompt, y_cont, dx_prompt, dx_cont,
         pieces[0], pieces[1], grad_w_qkv, pieces[2], grad_w_out, pieces[3],

time: 414 us -> 457 us (1.10)
  waiting for transfers between devices: 86.6 us -> 139 us
  Pallas kernels: 88.5 us -> 77.5 us
    ppermute x21, waiting for transfers between devices: 64.1 us -> 95.6 us  [swap(): lax.ppermute(value, EVERY, [(i, i ^ mask) for i in range(device_count())])]
    reduce_scatter x1, waiting for transfers between devices: 0.01 us -> 28.5 us  [whole_steps(): lax.psum_scatter(packed_grads, EVERY, scatter_dimension=0).astype(F32)]
    pallas_call x1, Pallas kernels: 49 us -> 39.5 us  [attend_backward(): pl.pallas_call(backward_kernel, grid=(HEADS,), in_specs=[pair_spec(lambda...]
    ppermute x2, waiting for transfers between devices: 7.72 us -> 0.01 us  [trade_back(): lax.ppermute(jnp.concatenate(away, 0).astype(B16), 'fsdp', [(0, 1), (1, 0)])]
    convert_element_type x5 -> x11, other arithmetic: 0.56 us -> 7.52 us  [the longest x8 5.5 us: unpack_vectors(): rows[:, i, :size].reshape(-1).astype(F32)]
    broadcast_in_dim x0 -> x11, local copies, waits for them, and re-layouts: none -> 6.92 us  [the longest x7 4.1 us: pack_grads(): v.astype(F32)[None]]
    another operation x6, other arithmetic: 5.26 us -> 0.53 us  [the longest x4 0.38 us: join_rows(): out.append(jnp.stack([pick(own, other, low), pick(other, own, low)]))]
    reduce_sum x6 -> x3, other arithmetic: 12.4 us -> 8.73 us  [column_sum(): return jnp.sum(values.astype(F32), 0)]
  transfers between devices with their start and end apart: 27 -> 27, of which waited for: 17 -> 16; matrix products, arithmetic and copies ran while one was open for 25% -> 16% of each run, Pallas kernels for 22% -> 8%
where the time goes in v3:
time: 457 us; the launch traced here: 451 us
  waiting for transfers between devices  139 us (30%)
  matrix products  94.1 us (21%)
  Pallas kernels  77.5 us (17%)
  local copies, waits for them, and re-layouts  46.9 us (10%)
  other arithmetic  44.6 us (10%)
  starting transfers between devices  34.2 us (7%)
  between operations  15.4 us (3%)
    ppermute x21, waiting for transfers between devices, swap(): lax.ppermute(value, EVERY, [(i, i ^ mask) for i in range(device_count())])  95.6 us
    pallas_call x1, Pallas kernels, attend_backward(): pl.pallas_call(backward_kernel, grid=(HEADS,), in_specs=[pair_spec(lambda...  39.5 us
    pallas_call x1, Pallas kernels, attend_forward(): pl.pallas_call(forward_kernel, grid=(HEADS,), in_specs=[pair_spec(lambda...  36.2 us
    dot_general x4, matrix products, through(): return jnp.einsum('re,de->rd', grad, weight, preferred_element_type=F32)  30 us
    ppermute x21, starting transfers between devices, swap(): lax.ppermute(value, EVERY, [(i, i ^ mask) for i in range(device_count())])  29.9 us
    reduce_scatter x1, waiting for transfers between devices, whole_steps(): lax.psum_scatter(packed_grads, EVERY, scatter_dimension=0).astype(F32)  28.5 us
    dot_general x4, matrix products, weight_grad(): jnp.einsum('rd,re->de', left, right, preferred_element_type=F32).astype(B16)  24.4 us
    unnamed x139, local copies, waits for them, and re-layouts  17.9 us
  transfers between devices with their start and end apart: 27, of which 16 were waited for; matrix products, arithmetic and copies ran while one was open for 16% of the time, Pallas kernels for 8%

profile of v3, /device:TPU:0, one launch (start us, length us, event | category | flops | bytes accessed | tf_op | source)
XLA Modules:
  0.0 451.3 jit_solution(18136167925547287281)
XLA Ops:
  11.0 3.1 collective-permute-start.1
  14.1 2.6 collective-permute-start.2
  21.5 4.5 collective-permute-done.2
  33.1 10.1 %collective-permute-done.5 = bf16[4,24,2432]{2,1,0:T(8,128)(2,1)S(1)} collective-permute-done((bf16[4,24,2432]{2,1,0:T(8,128)(2,1)}, bf16[4,24,2432]{2,1,0:T(8,128)(2,1)S(1)}, u32[]{:S(2)}, u32[]{:S(2)}) %collective-permute-start.5) | collective-permute-done | bytes 466976 | tf_op jit(solution)/shard_map/ppermute | solution.py:712
  43.2 7.6 %collective-permute-done.4 = bf16[4,24,2432]{2,1,0:T(8,128)(2,1)S(1)} collective-permute-done((bf16[4,24,2432]{2,1,0:T(8,128)(2,1)}, bf16[4,24,2432]{2,1,0:T(8,128)(2,1)S(1)}, u32[]{:S(2)}, u32[]{:S(2)}) %collective-permute-start.4) | collective-permute-done | bytes 466976 | tf_op jit(solution)/shard_map/ppermute | solution.py:712
  50.8 5.4 %collective-permute-done.6 = bf16[4,24,2432]{2,1,0:T(8,128)(2,1)} collective-permute-done((bf16[4,24,2432]{2,1,0:T(8,128)(2,1)}, bf16[4,24,2432]{2,1,0:T(8,128)(2,1)}, u32[]{:S(2)}, u32[]{:S(2)}) %collective-permute-start.6) | collective-permute-done | bytes 466976 | tf_op jit(solution)/shard_map/ppermute | solution.py:712
  60.5 14.4 %collective-permute-done = bf16[544,768]{1,0:T(8,128)(2,1)} collective-permute-done((bf16[544,768]{1,0:T(8,128)(2,1)}, bf16[544,768]{1,0:T(8,128)(2,1)}, u32[]{:S(2)}, u32[]{:S(2)}) %collective-permute-start) | collective-permute-done | bytes 835616 | tf_op jit(solution)/shard_map/ppermute | solution.py:836
  84.8 10.4 %fusion.q_ref.k_ref.v_ref = bf16[1088,2304]{1,0:T(8,128)(2,1)} fusion(f32[2304]{0:T(1024)S(1)} %pad_maximum_fusion.14, bf16[768,2432]{1,0:T(8,128)(2,1)} %bitcast.230, f32[768]{0:T(1024)S(1)} %reshape.294, f32[768]{0:T(1024)S(1)} %reshape.293, f32[1088]{0:T(1024)S(1)} %copy-done.47, f32[1088]{0:T(1024)S(1)} %broadcast_multiply_fusion.5, ...), kind=kOutput, calls=%fused_computation.9 | convolution fusion | flops 3866247168 | bytes 10247680 | tf_op jit(solution)/shard_map/dot_general | solution.py:910
  96.1 36.2 %attend_forward.1 = (bf16[1088,768]{1,0:T(8,128)(2,1)}, f32[12,1,1088]{2,1,0:T(1,128)}, f32[256,256]{1,0:T(8,128)}, f32[512,256]{1,0:T(8,128)}, f32[768,256]{1,0...) custom-call(bf16[1088,2304]{1,0:T(8,128)(2,1)} %fusion.q_ref.k_ref.v_ref, bf16[1088,2304]{1,0:T(8,128)(2,1)} %fusion.q_ref.k_ref.v_ref, ...), custom_call_target="tpu_custom_call" | custom-call | tf_op jit(solution)/shard_map/attend_forward/pallas_call | solution.py:633
  145.3 4.6 %fusion.39 = (bf16[32,24,768]{2,1,0:T(8,128)(2,1)S(1)}, bf16[32,24,768]{2,1,0:T(8,128)(2,1)}, bf16[32,24,768]{2,1,0:T(8,128)(2,1)}, bf16[32,24,768]{2,1,0:T(8,128)(2,1)}, bf16[32,24,768]{2,1,0:T(8,128)(2,1)S(1)}) fusion(bf16[32,216,768]{2,1,0:T(8,128)(2,1)} %bitcast.220), kind=kLoop, calls=%fused_computation.211 | loop fusion | bytes 11796480 | tf_op jit(solution)/shard_map/slice | solution.py:903
  149.9 3.5 slice.324
  158.6 17.5 %add_convert_fusion = (bf16[1088,3072]{1,0:T(8,128)(2,1)}, bf16[1088,3072]{1,0:T(8,128)(2,1)}) fusion(f32[3072]{0:T(1024)S(1)} %copy-done.58, bf16[768,768]{1,0:T(8,128)(2,1)S(1)} %bitcast.237, bf16[768,768]{1,0:T(8,128)(2,1)S(1)} %bitcast.239, bf16[768,768]{1,0:T(8,128)(2,1)} %bitcast.240, bf16[768,768]{1,0:T(8,128)(2,1)S(1)} %bitcast.234, ...), kind=kOutput, calls=%fused_computation.4 | convolution fusion | flops 5213700096 | bytes 21457408 | tf_op jit(solution)/shard_map/dot_general | solution.py:917
  176.1 7.7 %fusion.1 = bf16[1088,3072]{1,0:T(8,128)(2,1)S(1)} fusion(bf16[1088,3072]{1,0:T(8,128)(2,1)} %get-tuple-element.62, bf16[3072,768]{1,0:T(8,128)(2,1)S(1)} %bitcast.226, bf16[64,768]{1,0:T(8,128)(2,1)S(1)} %copy-done.42, bf16[64,768]{1,0:T(8,128)(2,1)S(1)} %copy-done.40, bf16[480,768]{1,0:T(8,128)(2,1)S(1)} %copy-done.22, bf16[480,768]{1,0:T(8,128)(2,1)S(1)} %copy-done.20), kind=kOutput, calls=%fused_computation.10 | convolution fusion | flops 5150539776 | bytes 19759104 | tf_op jit(solution)/shard_map/re,de->rd/dot_general | solution.py:924
  183.9 7.8 %convolution_convert_fusion.2 = bf16[768,3072]{1,0:T(8,128)(2,1)S(1)} fusion(bf16[1088,3072]{1,0:T(8,128)(2,1)S(1)} %fusion.1, f32[1088,768]{1,0:T(8,128)S(1)} %get-tuple-element.208, f32[768]{0:T(1024)S(1)} %copy-done.61, f32[768]{0:T(1024)S(1)} %copy-done.54, f32[1088]{0:T(1024)S(1)} %add_rsqrt_fusion, f32[1088]{0:T(1024)S(1)} %broadcast_multiply_fusion.4), kind=kOutput, calls=%fused_computation.13 | convolution fusion | flops 5140365312 | bytes 14760448 | tf_op jit(solution)/shard_map/rd,re->de/dot_general | solution.py:921
  195.3 6.8 %convolution_convert_fusion.1 = bf16[3072,768]{1,0:T(8,128)(2,1)S(1)} fusion(bf16[1088,3072]{1,0:T(8,128)(2,1)S(1)} %copy-done.64, bf16[64,768]{1,0:T(8,128)(2,1)S(1)} %copy-done.43, bf16[64,768]{1,0:T(8,128)(2,1)S(1)} %copy-done.40, bf16[480,768]{1,0:T(8,128)(2,1)S(1)} %copy-done.23, bf16[480,768]{1,0:T(8,128)(2,1)S(1)} %copy-done.20), kind=kOutput, calls=%fused_computation.12 | convolution fusion | flops 5142872064 | bytes 13074432 | tf_op jit(solution)/shard_map/rd,re->de/dot_general | solution.py:921
  208.0 11.1 %multiply_reduce_fusion = (f32[768]{0:T(1024)}, f32[1088]{0:T(1024)S(1)}, f32[1088]{0:T(1024)S(1)}, f32[768]{0:T(1024)}, f32[1088,768]{1,0:T(8,128)S(1)}) fusion(f32[1088,768]{1,0:T(8,128)S(1)} %get-tuple-element.208, f32[1088]{0:T(1024)} %copy-done.45, f32[1088]{0:T(1024)S(1)} %broadcast_multiply_fusion.4, f32[768]{0:T(1024)} %reshape.296, ...), kind=kOutput, calls=%fused_computation.41 | convolution fusion | flops 5160218624 | bytes 18114560 | tf_op jit(solution)/shard_map/re,de->rd/dot_general | solution.py:924
  219.2 3.6 convert_reduce_fusion.3
  222.8 2.7 convolution_convert_fusion.3.g_ref
  225.5 39.5 %attend_backward.1 = bf16[1088,2304]{1,0:T(8,128)(2,1)} custom-call(bf16[1088,2304]{1,0:T(8,128)(2,1)} %fusion.q_ref.k_ref.v_ref, bf16[1088,2304]{1,0:T(8,128)(2,1)} %fusion.q_ref.k_ref.v_ref, bf16[1088,2304]{1,0:T(8,128)(2,1)} %fusion.q_ref.k_ref.v_ref, bf16[1088,768]{1,0:T(8,128)(2,1)} %convolution_convert_fusion.3.g_ref, ...), custom_call_target="tpu_custom_call" | custom-call | tf_op jit(solution)/shard_map/attend_backward/pallas_call | solution.py:663
  265.1 8.5 %fusion.13 = (f32[1088]{0:T(1024)S(1)}, f32[768]{0:T(1024)S(1)}, f32[1088]{0:T(1024)S(1)}, f32[768]{0:T(1024)S(1)}, f32[1088,768]{1,0:T(8,128)S(1)}) fusion(f32[768]{0:T(1024)S(1)} %copy-done.52, f32[1088]{0:T(1024)S(1)} %copy-done.48, f32[1088]{0:T(1024)S(1)} %broadcast_multiply_fusion.5, bf16[64,768]{1,0:T(8,128)(2,1)S(1)} %get-tuple-element.174, ...), kind=kOutput, calls=%fused_computation.36 | convolution fusion | flops 3864572416 | bytes 13592576 | tf_op jit(solution)/shard_map/re,de->rd/dot_general | solution.py:924
  274.2 4.6 %convert_reduce_fusion = f32[3072]{0:T(1024)} fusion(bf16[1088,3072]{1,0:T(8,128)(2,1)} %copy-done.14), kind=kLoop, calls=%fused_computation.3 | loop fusion | flops 6681600 | bytes 6696960 | tf_op jit(solution)/shard_map/reduce_sum | solution.py:927
  283.0 3.4 fusion.16
  290.6 8.0 %convolution_convert_fusion = bf16[768,2304]{1,0:T(8,128)(2,1)S(1)} fusion(bf16[1088,2304]{1,0:T(8,128)(2,1)} %attend_backward.1, f32[768]{0:T(1024)} %copy-done.59, f32[768]{0:T(1024)} %copy-done.51, f32[1088]{0:T(1024)S(1)} %copy-done.50, f32[1088]{0:T(1024)S(1)} %broadcast_multiply_fusion.5, bf16[64,768]{1,0:T(8,128)(2,1)S(1)} %get-tuple-element.174, ...), kind=kOutput, calls=%fused_computation.11 | convolution fusion | flops 3863003136 | bytes 10238464 | tf_op jit(solution)/shard_map/rd,re->de/dot_general | solution.py:921
  301.0 10.1 %fusion.9 = bf16[1088,768]{1,0:T(8,128)(2,1)S(1)} fusion(f32[1088,768]{1,0:T(8,128)S(1)} %copy-done.5, bf16[1088,3072]{1,0:T(8,128)(2,1)} %get-tuple-element.73, bf16[3072,768]{1,0:T(8,128)(2,1)} %bitcast.227, f32[768]{0:T(1024)S(1)} %copy-done.60), kind=kOutput, calls=%fused_computation.31 | convolution fusion | flops 5136334848 | bytes 16419840 | tf_op jit(solution)/shard_map/dot_general | solution.py:947
  320.9 43.4 %collective-permute-done.12 = bf16[4,24,768]{2,1,0:T(8,128)(2,1)S(1)} collective-permute-done((bf16[4,24,768]{2,1,0:T(8,128)(2,1)S(1)}, bf16[4,24,768]{2,1,0:T(8,128)(2,1)S(1)}, u32[]{:S(2)}, u32[]{:S(2)}) %collective-permute-start.12) | collective-permute-done | bytes 147488 | tf_op jit(solution)/shard_map/ppermute | solution.py:712
  364.4 2.7 collective-permute-start.24
  371.2 5.3 %collective-permute-start.23 = (bf16[24,768]{1,0:T(8,128)(2,1)S(1)}, bf16[24,768]{1,0:T(8,128)(2,1)S(1)}, u32[]{:S(2)}, u32[]{:S(2)}) collective-permute-start(bf16[24,768]{1,0:T(8,128)(2,1)S(1)} %get-tuple-element.206), channel_id=1, source_target_pairs={{0,16},{1,17},{2,18},{3,19},{4,20},{5,21},{6,22},{7,23},{8,24},{9,... | collective-permute-start | bytes 110600 | tf_op jit(solution)/shard_map/ppermute | solution.py:712
  380.7 3.0 collective-permute-done.22
  386.7 8.5 %collective-permute-done.17 = bf16[4,24,2432]{2,1,0:T(8,128)(2,1)S(1)} collective-permute-done((bf16[4,24,2432]{2,1,0:T(8,128)(2,1)S(1)}, bf16[4,24,2432]{2,1,0:T(8,128)(2,1)S(1)}, u32[]{:S(2)}, u32[]{:S(2)}) %collective-permute-start.17) | collective-permute-done | bytes 466976 | tf_op jit(solution)/shard_map/ppermute | solution.py:712
  397.6 3.0 collective-permute-start.20
  403.4 5.9 %collective-permute-done.20 = bf16[24,2432]{1,0:T(8,128)(2,1)S(1)} collective-permute-done((bf16[24,2432]{1,0:T(8,128)(2,1)S(1)}, bf16[24,2432]{1,0:T(8,128)(2,1)S(1)}, u32[]{:S(2)}, u32[]{:S(2)}) %collective-permute-start.20) | collective-permute-done | bytes 116768 | tf_op jit(solution)/shard_map/ppermute | solution.py:712
  413.2 28.5 %reduce-scatter.2.cloned.1.call-done = bf16[1,192,768]{2,1,0:T(8,128)(2,1)} async-done(((bf16[32,192,768]{2,1,0:T(8,128)(2,1)}), bf16[1,192,768]{2,1,0:T(8,128)(2,1)}) %reduce-scatter.2.cloned.1.call-update) | async-done | bytes 294928 | tf_op jit(solution)/shard_map/reduce_scatter | solution.py:942
  (290 shorter events, 101.7 us)
Async XLA Ops:
  7.2 138.1 %all-gather.3.cloned.1.call-start = ((), (), s32[]{:S(2)}) async-start(), calls=%async_computation.2 | async-start | bytes 10948608 | tf_op jit(solution)/shard_map/all_gather | solution.py:895
  11.0 10.5 %collective-permute-start.1 = (bf16[24,2432]{1,0:T(8,128)(2,1)S(1)}, bf16[24,2432]{1,0:T(8,128)(2,1)S(1)}, u32[]{:S(2)}, u32[]{:S(2)}) collective-permute-start(bf16[24,2432]{1,0:T(8,128)(2,1)S(1)} %fusion.29), channel_id=1, source_target_pairs={{0,8},{1,9},{2,10},{3,11},{4,12},{5,13},{6,14},{7,15},{8,0},{9,1},... | collective-permute-start | bytes 350216 | tf_op jit(solution)/shard_map/ppermute | solution.py:712
  14.1 11.9 %collective-permute-start.2 = (bf16[24,2432]{1,0:T(8,128)(2,1)S(1)}, bf16[24,2432]{1,0:T(8,128)(2,1)S(1)}, u32[]{:S(2)}, u32[]{:S(2)}) collective-permute-start(bf16[24,2432]{1,0:T(8,128)(2,1)S(1)} %fusion.29), channel_id=1, source_target_pairs={{0,16},{1,17},{2,18},{3,19},{4,20},{5,21},{6,22},{7,23},{8,24},{9,... | collective-permute-start | bytes 350216 | tf_op jit(solution)/shard_map/ppermute | solution.py:712
  16.7 9.3 %collective-permute-start.3 = (bf16[24,2432]{1,0:T(8,128)(2,1)S(1)}, bf16[24,2432]{1,0:T(8,128)(2,1)S(1)}, u32[]{:S(2)}, u32[]{:S(2)}) collective-permute-start(bf16[24,2432]{1,0:T(8,128)(2,1)S(1)} %fusion.29), channel_id=1, source_target_pairs={{0,24},{1,25},{2,26},{3,27},{4,28},{5,29},{6,30},{7,31},{8,16},{9,... | collective-permute-start | bytes 350216 | tf_op jit(solution)/shard_map/ppermute | solution.py:712
  26.0 415.7 %reduce-scatter.2.cloned.1.call-start = ((), (), s32[]{:S(2)}) async-start(), calls=%async_computation.1 | async-start | bytes 9732096 | tf_op jit(solution)/shard_map/reduce_scatter | solution.py:942
  27.0 16.1 %collective-permute-start.5 = (bf16[4,24,2432]{2,1,0:T(8,128)(2,1)}, bf16[4,24,2432]{2,1,0:T(8,128)(2,1)S(1)}, u32[]{:S(2)}, u32[]{:S(2)}) collective-permute-start(bf16[4,24,2432]{2,1,0:T(8,128)(2,1)} %pad_maximum_fusion.12), channel_id=1, source_target_pairs={{0,4},{1,5},{2,6},{3,7},{4,0},{5,1},{6,2},{7,3},{8,12},{9,13},{10,... | collective-permute-start | bytes 1400840 | tf_op jit(solution)/shard_map/ppermute | solution.py:712
  28.5 22.3 %collective-permute-start.4 = (bf16[4,24,2432]{2,1,0:T(8,128)(2,1)}, bf16[4,24,2432]{2,1,0:T(8,128)(2,1)S(1)}, u32[]{:S(2)}, u32[]{:S(2)}) collective-permute-start(bf16[4,24,2432]{2,1,0:T(8,128)(2,1)} %pad_maximum_fusion.12), channel_id=1, source_target_pairs={{0,5},{1,4},{2,7},{3,6},{4,1},{5,0},{6,3},{7,2},{8,13},{9,12},{10,... | collective-permute-start | bytes 1400840 | tf_op jit(solution)/shard_map/ppermute | solution.py:712
  30.0 26.3 %collective-permute-start.6 = (bf16[4,24,2432]{2,1,0:T(8,128)(2,1)}, bf16[4,24,2432]{2,1,0:T(8,128)(2,1)}, u32[]{:S(2)}, u32[]{:S(2)}) collective-permute-start(bf16[4,24,2432]{2,1,0:T(8,128)(2,1)} %pad_maximum_fusion.12), channel_id=1, source_target_pairs={{0,1},{1,0},{2,3},{3,2},{4,5},{5,4},{6,7},{7,6},{8,9},{9,8},{10,11... | collective-permute-start | bytes 1400840 | tf_op jit(solution)/shard_map/ppermute | solution.py:712
  31.6 43.4 %collective-permute-start = (bf16[544,768]{1,0:T(8,128)(2,1)}, bf16[544,768]{1,0:T(8,128)(2,1)}, u32[]{:S(2)}, u32[]{:S(2)}) collective-permute-start(bf16[544,768]{1,0:T(8,128)(2,1)} %pad_maximum_fusion.6), channel_id=1, source_target_pairs={{0,1},{1,0},{2,3},{3,2},{4,5},{5,4},{6,7},{7,6},{8,9},{9,8},{10,11... | collective-permute-start | bytes 2506760 | tf_op jit(solution)/shard_map/ppermute | solution.py:836
  60.5 18.7 %collective-permute-start.7 = (bf16[4,2,2,24,2432]{4,3,2,1,0:T(8,128)(2,1)}, bf16[4,2,2,24,2432]{4,3,2,1,0:T(8,128)(2,1)}, u32[]{:S(2)}, u32[]{:S(2)}) collective-permute-start(bf16[4,2,2,24,2432]{4,3,2,1,0:T(8,128)(2,1)} %pad_maximum_fusion.3), channel_id=1, source_target_pairs={{0,2},{1,3},{2,0},{3,1},{4,6},{5,7},{6,4},{7,5},{8,10},{9,11},{10,... | collective-permute-start | bytes 5603336 | tf_op jit(solution)/shard_map/ppermute | solution.py:712
  95.4 48.0 %collective-permute-start.8 = (bf16[544,768]{1,0:T(8,128)(2,1)S(1)}, bf16[544,768]{1,0:T(8,128)(2,1)S(1)}, u32[]{:S(2)}, u32[]{:S(2)}) collective-permute-start(bf16[544,768]{1,0:T(8,128)(2,1)S(1)} %pad_maximum_fusion.7), channel_id=1, source_target_pairs={{0,1},{1,0},{2,3},{3,2},{4,5},{5,4},{6,7},{7,6},{8,9},{9,8},{10,11... | collective-permute-start | bytes 2506760 | tf_op jit(solution)/shard_map/ppermute | solution.py:836
  96.1 48.0 %copy-start.17 = (bf16[2,1,480,768]{3,2,1,0:T(8,128)(2,1)S(1)}, bf16[2,1,480,768]{3,2,1,0:T(8,128)(2,1)}, u32[]{:S(2)}) copy-start(bf16[2,1,480,768]{3,2,1,0:T(8,128)(2,1)} %param.18) | copy-start | bytes 4423684
  155.7 63.4 %copy-start.4 = (f32[1088,768]{1,0:T(8,128)}, f32[1088,768]{1,0:T(8,128)S(1)}, u32[]{:S(2)}) copy-start(f32[1088,768]{1,0:T(8,128)S(1)} %get-tuple-element.208) | copy-start | bytes 10027012
  225.5 39.5 %copy-start.12 = (bf16[480,768]{1,0:T(8,128)(2,1)S(1)}, bf16[480,768]{1,0:T(8,128)(2,1)}, u32[]{:S(2)}) copy-start(bf16[480,768]{1,0:T(8,128)(2,1)} %copy-done.10) | copy-start | bytes 2211844
  225.5 39.6 %copy-start.48 = (f32[1088]{0:T(1024)S(1)}, f32[1088]{0:T(1024)}, u32[]{:S(2)}) copy-start(f32[1088]{0:T(1024)} %add_rsqrt_fusion.1) | copy-start | bytes 13060
  225.5 39.6 %copy-start.52 = (f32[768]{0:T(1024)S(1)}, f32[768]{0:T(1024)}, u32[]{:S(2)}) copy-start(f32[768]{0:T(1024)} %copy-done.51) | copy-start | bytes 9220
  299.0 20.2 %collective-permute-start.9 = (bf16[4,2,2,24,2432]{4,3,2,1,0:T(8,128)(2,1)S(1)}, bf16[4,2,2,24,2432]{4,3,2,1,0:T(8,128)(2,1)S(1)}, u32[]{:S(2)}, u32[]{:S(2)}) collective-permute-start(bf16[4,2,2,24,2432]{4,3,2,1,0:T(8,128)(2,1)S(1)} %dynamic-slice_bitcast_fusion), channel_id=1, source_target_pairs={{0,2},{1,3},{2,0},{3,1},{4,6},{5,7},{6,4},{7,5},{8,10},{9,11},{10,... | collective-permute-start | bytes 5603336 | tf_op jit(solution)/shard_map/ppermute | solution.py:712
  313.1 51.2 %collective-permute-start.10 = (bf16[544,768]{1,0:T(8,128)(2,1)S(1)}, bf16[544,768]{1,0:T(8,128)(2,1)S(1)}, u32[]{:S(2)}, u32[]{:S(2)}) collective-permute-start(bf16[544,768]{1,0:T(8,128)(2,1)S(1)} %pad_maximum_fusion.8), channel_id=1, source_target_pairs={{0,1},{1,0},{2,3},{3,2},{4,5},{5,4},{6,7},{7,6},{8,9},{9,8},{10,11... | collective-permute-start | bytes 2506760 | tf_op jit(solution)/shard_map/ppermute | solution.py:860
  314.8 2.2 collective-permute-start.11
  315.1 69.2 %collective-permute-start.18 = (bf16[544,768]{1,0:T(8,128)(2,1)S(1)}, bf16[544,768]{1,0:T(8,128)(2,1)S(1)}, u32[]{:S(2)}, u32[]{:S(2)}) collective-permute-start(bf16[544,768]{1,0:T(8,128)(2,1)S(1)} %pad_maximum_fusion.9), channel_id=1, source_target_pairs={{0,1},{1,0},{2,3},{3,2},{4,5},{5,4},{6,7},{7,6},{8,9},{9,8},{10,11... | collective-permute-start | bytes 2506760 | tf_op jit(solution)/shard_map/ppermute | solution.py:860
  317.1 47.2 %collective-permute-start.12 = (bf16[4,24,768]{2,1,0:T(8,128)(2,1)S(1)}, bf16[4,24,768]{2,1,0:T(8,128)(2,1)S(1)}, u32[]{:S(2)}, u32[]{:S(2)}) collective-permute-start(bf16[4,24,768]{2,1,0:T(8,128)(2,1)S(1)} %get-tuple-element.183), channel_id=1, source_target_pairs={{0,1},{1,0},{2,3},{3,2},{4,5},{5,4},{6,7},{7,6},{8,9},{9,8},{10,11... | collective-permute-start | bytes 442376 | tf_op jit(solution)/shard_map/ppermute | solution.py:712
  317.8 46.5 %collective-permute-start.13 = (bf16[4,24,768]{2,1,0:T(8,128)(2,1)S(1)}, bf16[4,24,768]{2,1,0:T(8,128)(2,1)S(1)}, u32[]{:S(2)}, u32[]{:S(2)}) collective-permute-start(bf16[4,24,768]{2,1,0:T(8,128)(2,1)S(1)} %get-tuple-element.182), channel_id=1, source_target_pairs={{0,4},{1,5},{2,6},{3,7},{4,0},{5,1},{6,2},{7,3},{8,12},{9,13},{10,... | collective-permute-start | bytes 442376 | tf_op jit(solution)/shard_map/ppermute | solution.py:712
  319.2 45.1 %collective-permute-start.14 = (bf16[4,24,768]{2,1,0:T(8,128)(2,1)S(1)}, bf16[4,24,768]{2,1,0:T(8,128)(2,1)S(1)}, u32[]{:S(2)}, u32[]{:S(2)}) collective-permute-start(bf16[4,24,768]{2,1,0:T(8,128)(2,1)S(1)} %get-tuple-element.181), channel_id=1, source_target_pairs={{0,5},{1,4},{2,7},{3,6},{4,1},{5,0},{6,3},{7,2},{8,13},{9,12},{10,... | collective-permute-start | bytes 442376 | tf_op jit(solution)/shard_map/ppermute | solution.py:712
  364.4 6.7 %collective-permute-start.24 = (bf16[24,768]{1,0:T(8,128)(2,1)S(1)}, bf16[24,768]{1,0:T(8,128)(2,1)S(1)}, u32[]{:S(2)}, u32[]{:S(2)}) collective-permute-start(bf16[24,768]{1,0:T(8,128)(2,1)S(1)} %get-tuple-element.205), channel_id=1, source_target_pairs={{0,24},{1,25},{2,26},{3,27},{4,28},{5,29},{6,30},{7,31},{8,16},{9,... | collective-permute-start | bytes 110600 | tf_op jit(solution)/shard_map/ppermute | solution.py:712
  367.4 19.0 %collective-permute-start.15 = (bf16[4,24,2432]{2,1,0:T(8,128)(2,1)S(1)}, bf16[4,24,2432]{2,1,0:T(8,128)(2,1)S(1)}, u32[]{:S(2)}, u32[]{:S(2)}) collective-permute-start(bf16[4,24,2432]{2,1,0:T(8,128)(2,1)S(1)} %get-tuple-element.157), channel_id=1, source_target_pairs={{0,1},{1,0},{2,3},{3,2},{4,5},{5,4},{6,7},{7,6},{8,9},{9,8},{10,11... | collective-permute-start | bytes 1400840 | tf_op jit(solution)/shard_map/ppermute | solution.py:712
  369.0 17.6 %collective-permute-start.16 = (bf16[4,24,2432]{2,1,0:T(8,128)(2,1)S(1)}, bf16[4,24,2432]{2,1,0:T(8,128)(2,1)S(1)}, u32[]{:S(2)}, u32[]{:S(2)}) collective-permute-start(bf16[4,24,2432]{2,1,0:T(8,128)(2,1)S(1)} %get-tuple-element.156), channel_id=1, source_target_pairs={{0,4},{1,5},{2,6},{3,7},{4,0},{5,1},{6,2},{7,3},{8,12},{9,13},{10,... | collective-permute-start | bytes 1400840 | tf_op jit(solution)/shard_map/ppermute | solution.py:712
  370.5 24.6 %collective-permute-start.17 = (bf16[4,24,2432]{2,1,0:T(8,128)(2,1)S(1)}, bf16[4,24,2432]{2,1,0:T(8,128)(2,1)S(1)}, u32[]{:S(2)}, u32[]{:S(2)}) collective-permute-start(bf16[4,24,2432]{2,1,0:T(8,128)(2,1)S(1)} %get-tuple-element.155), channel_id=1, source_target_pairs={{0,5},{1,4},{2,7},{3,6},{4,1},{5,0},{6,3},{7,2},{8,13},{9,12},{10,... | collective-permute-start | bytes 1400840 | tf_op jit(solution)/shard_map/ppermute | solution.py:712
  371.2 8.5 %collective-permute-start.23 = (bf16[24,768]{1,0:T(8,128)(2,1)S(1)}, bf16[24,768]{1,0:T(8,128)(2,1)S(1)}, u32[]{:S(2)}, u32[]{:S(2)}) collective-permute-start(bf16[24,768]{1,0:T(8,128)(2,1)S(1)} %get-tuple-element.206), channel_id=1, source_target_pairs={{0,16},{1,17},{2,18},{3,19},{4,20},{5,21},{6,22},{7,23},{8,24},{9,... | collective-permute-start | bytes 110600 | tf_op jit(solution)/shard_map/ppermute | solution.py:712
  379.7 4.0 collective-permute-start.22
  395.4 8.0 %collective-permute-start.21 = (bf16[24,2432]{1,0:T(8,128)(2,1)S(1)}, bf16[24,2432]{1,0:T(8,128)(2,1)S(1)}, u32[]{:S(2)}, u32[]{:S(2)}) collective-permute-start(bf16[24,2432]{1,0:T(8,128)(2,1)S(1)} %get-tuple-element.186), channel_id=1, source_target_pairs={{0,24},{1,25},{2,26},{3,27},{4,28},{5,29},{6,30},{7,31},{8,16},{9,... | collective-permute-start | bytes 350216 | tf_op jit(solution)/shard_map/ppermute | solution.py:712
  397.6 11.8 %collective-permute-start.20 = (bf16[24,2432]{1,0:T(8,128)(2,1)S(1)}, bf16[24,2432]{1,0:T(8,128)(2,1)S(1)}, u32[]{:S(2)}, u32[]{:S(2)}) collective-permute-start(bf16[24,2432]{1,0:T(8,128)(2,1)S(1)} %get-tuple-element.187), channel_id=1, source_target_pairs={{0,16},{1,17},{2,18},{3,19},{4,20},{5,21},{6,22},{7,23},{8,24},{9,... | collective-permute-start | bytes 350216 | tf_op jit(solution)/shard_map/ppermute | solution.py:712
  400.6 10.3 %collective-permute-start.19 = (bf16[24,2432]{1,0:T(8,128)(2,1)S(1)}, bf16[24,2432]{1,0:T(8,128)(2,1)S(1)}, u32[]{:S(2)}, u32[]{:S(2)}) collective-permute-start(bf16[24,2432]{1,0:T(8,128)(2,1)S(1)} %get-tuple-element.185), channel_id=1, source_target_pairs={{0,8},{1,9},{2,10},{3,11},{4,12},{5,13},{6,14},{7,15},{8,0},{9,1},... | collective-permute-start | bytes 350216 | tf_op jit(solution)/shard_map/ppermute | solution.py:712
  (60 other events, 560.7 us)
Sparse Core Ops, SparseCore 0:
  26.1 110.4 all-gather.2
  290.0 151.6 reduce-scatter.1

commit v4 on v3

--- a/solution.py
+++ b/solution.py
@@ -722,16 +722,15 @@
     return pieces
 
 
-def gather_steps(shard, held):
+def gather_steps(shard):
     z, x, core, y = place_of()
     column = [shard] + [swap(shard, 8 * k) for k in range(1, depth())]
-    *column, held = lax.optimization_barrier((*column, held))
     value = jnp.stack(arrange(column, z))
     plane = [value] + [swap(value, mask) for mask in PLANE[1:]]
     plane = arrange(plane, 2 * x + y)
     value = jnp.stack([jnp.stack(plane[:2], 1), jnp.stack(plane[2:], 1)], 1)
     value = jnp.stack(arrange([value, swap(value, CORE)], core), 2)
-    return value.reshape(-1, shard.shape[1]), held
+    return value.reshape(-1, shard.shape[1])
 
 
 def take(value, index, axis):
@@ -827,13 +826,16 @@
     return jnp.where(when, first, second)
 
 
-def trade_rows(prompt, cont):
-    place = lax.axis_index("fsdp")
-    low = place == 0
-    swap_pairs = [(0, 1), (1, 0)]
+def split_rows(prompt, cont):
+    low = lax.axis_index("fsdp") == 0
     mine = [pick(t[0], t[1], low).reshape(-1, D) for t in (prompt, cont)]
     away = [pick(t[1], t[0], low).reshape(-1, D) for t in (prompt, cont)]
-    came = lax.ppermute(jnp.concatenate(away, 0), "fsdp", swap_pairs)
+    return mine, jnp.concatenate(away, 0)
+
+
+def trade_rows(mine, away):
+    low = lax.axis_index("fsdp") == 0
+    came = lax.ppermute(away, "fsdp", [(0, 1), (1, 0)])
     half = mine[0].shape[0]
     parts = (came[:half], came[half:])
     return jnp.concatenate(
@@ -885,13 +887,11 @@
     sizes = [v.shape[0] for v in vectors]
     chunks = w_down.shape[0] // w_qkv.shape[0]
     rows = w_qkv.shape[0]
-    flat_x = trade_rows(x_prompt, x_cont).astype(F32)
+    flat_x = trade_rows(*split_rows(x_prompt, x_cont)).astype(F32)
     rest = jnp.concatenate(
         [w_out, *(w_up[:, i * D : (i + 1) * D] for i in range(chunks)), w_down], 0
     )
-    full_first, rest = gather_steps(
-        jnp.concatenate([w_qkv, pack_vectors(vectors)], 1), rest
-    )
+    full_first = gather_steps(jnp.concatenate([w_qkv, pack_vectors(vectors)], 1))
     full_rest = lax.all_gather(rest, EVERY, axis=0)
     full_qkv = full_first[:, : 3 * D]
     (
@@ -904,16 +904,19 @@
     )
     full_down = full_rest[:, rows * (chunks + 1) :].reshape(hidden, D)
 
-    normed_one = normalize(flat_x, gain_one, shift_one).astype(B16)
+    center = flat_x - jnp.mean(flat_x, -1, keepdims=True)
+    rate = lax.rsqrt(jnp.mean(center * center, -1, keepdims=True) + EPS)
+    normed_one = (center * rate * gain_one + shift_one).astype(B16)
     bias_joined = jnp.concatenate([bias_qv[:D], jnp.zeros((D,), F32), bias_qv[D:]])
     joined = (
         jnp.dot(normed_one, full_qkv, preferred_element_type=F32) + bias_joined
     ).astype(B16)
-    joined, dy_prompt, dy_cont = lax.optimization_barrier((joined, dy_prompt, dy_cont))
-    grad_y = trade_rows(dy_prompt, dy_cont)
+    dy_mine, dy_away = split_rows(dy_prompt, dy_cont)
+    joined, dy_away = lax.optimization_barrier((joined, dy_away))
+    grad_y = trade_rows(dy_mine, dy_away)
     mixed, lse, *biases = attend_forward(joined)
     residual = flat_x + (jnp.dot(mixed, full_out, preferred_element_type=F32) + bias_out)
-    normed_two = normalize(residual, gain_two, shift_two).astype(B16)
+    normed_two = lax.optimization_barrier(normalize(residual, gain_two, shift_two).astype(B16))
     upward = jnp.dot(normed_two, full_up, preferred_element_type=F32) + bias_up
     active, slope = lax.optimization_barrier(gelu_pair(upward))
 

time: 457 us -> 462 us (1.011)
  waiting for transfers between devices: 139 us -> 163 us
  starting transfers between devices: 34.2 us -> 26.3 us
  local copies, waits for them, and re-layouts: 46.9 us -> 41.5 us
    ppermute x21, waiting for transfers between devices: 95.6 us -> 123 us  [swap(): lax.ppermute(value, EVERY, [(i, i ^ mask) for i in range(device_count())])]
    ppermute x21, starting transfers between devices: 29.9 us -> 21.8 us  [swap(): lax.ppermute(value, EVERY, [(i, i ^ mask) for i in range(device_count())])]
    reduce_scatter x1, waiting for transfers between devices: 28.5 us -> 22.8 us  [whole_steps(): lax.psum_scatter(packed_grads, EVERY, scatter_dimension=0).astype(F32)]
    unnamed x139 -> x131, local copies, waits for them, and re-layouts: 17.9 us -> 16.5 us
  transfers between devices with their start and end apart: 27 -> 27, of which waited for: 16 -> 18; matrix products, arithmetic and copies ran while one was open for 16% -> 14% of each run, Pallas kernels for 8% -> 8%
where the time goes in v4:
time: 462 us; the launch traced here: 457 us
  waiting for transfers between devices  163 us (35%)
  matrix products  90.6 us (20%)
  Pallas kernels  77.4 us (17%)
  other arithmetic  42.7 us (9%)
  local copies, waits for them, and re-layouts  41.5 us (9%)
  starting transfers between devices  26.3 us (6%)
  between operations  15.5 us (3%)
    ppermute x21, waiting for transfers between devices, swap(): lax.ppermute(value, EVERY, [(i, i ^ mask) for i in range(device_count())])  123 us
    pallas_call x1, Pallas kernels, attend_backward(): pl.pallas_call(backward_kernel, grid=(HEADS,), in_specs=[pair_spec(lambda...  39.4 us
    pallas_call x1, Pallas kernels, attend_forward(): pl.pallas_call(forward_kernel, grid=(HEADS,), in_specs=[pair_spec(lambda...  36.2 us
    dot_general x4, matrix products, through(): return jnp.einsum('re,de->rd', grad, weight, preferred_element_type=F32)  30.4 us
    dot_general x4, matrix products, weight_grad(): jnp.einsum('rd,re->de', left, right, preferred_element_type=F32).astype(B16)  23.7 us
    reduce_scatter x1, waiting for transfers between devices, whole_steps(): lax.psum_scatter(packed_grads, EVERY, scatter_dimension=0).astype(F32)  22.8 us
    ppermute x21, starting transfers between devices, swap(): lax.ppermute(value, EVERY, [(i, i ^ mask) for i in range(device_count())])  21.8 us
    ppermute x2, waiting for transfers between devices, trade_rows(): came = lax.ppermute(away, 'fsdp', [(0, 1), (1, 0)])  17 us
  transfers between devices with their start and end apart: 27, of which 18 were waited for; matrix products, arithmetic and copies ran while one was open for 14% of the time, Pallas kernels for 8%

profile of v4, /device:TPU:0, one launch (start us, length us, event | category | flops | bytes accessed | tf_op | source)
XLA Modules:
  0.0 457.0 jit_solution(2937121490863238359)
XLA Ops:
  16.6 5.1 %collective-permute-start.1 = (bf16[24,2432]{1,0:T(8,128)(2,1)S(1)}, bf16[24,2432]{1,0:T(8,128)(2,1)S(1)}, u32[]{:S(2)}, u32[]{:S(2)}) collective-permute-start(bf16[24,2432]{1,0:T(8,128)(2,1)S(1)} %fusion.29), channel_id=1, source_target_pairs={{0,24},{1,25},{2,26},{3,27},{4,28},{5,29},{6,30},{7,31},{8,16},{9,... | collective-permute-start | bytes 350216 | tf_op jit(solution)/shard_map/ppermute | solution.py:712
  22.4 3.5 collective-permute-done.1
  25.9 11.2 %collective-permute-done.2 = bf16[24,2432]{1,0:T(8,128)(2,1)S(1)} collective-permute-done((bf16[24,2432]{1,0:T(8,128)(2,1)S(1)}, bf16[24,2432]{1,0:T(8,128)(2,1)S(1)}, u32[]{:S(2)}, u32[]{:S(2)}) %collective-permute-start.2) | collective-permute-done | bytes 116768 | tf_op jit(solution)/shard_map/ppermute | solution.py:712
  44.9 13.8 %collective-permute-done.5 = bf16[4,24,2432]{2,1,0:T(8,128)(2,1)S(1)} collective-permute-done((bf16[4,24,2432]{2,1,0:T(8,128)(2,1)}, bf16[4,24,2432]{2,1,0:T(8,128)(2,1)S(1)}, u32[]{:S(2)}, u32[]{:S(2)}) %collective-permute-start.5) | collective-permute-done | bytes 466976 | tf_op jit(solution)/shard_map/ppermute | solution.py:712
  58.7 11.5 %collective-permute-done.4 = bf16[4,24,2432]{2,1,0:T(8,128)(2,1)S(1)} collective-permute-done((bf16[4,24,2432]{2,1,0:T(8,128)(2,1)}, bf16[4,24,2432]{2,1,0:T(8,128)(2,1)S(1)}, u32[]{:S(2)}, u32[]{:S(2)}) %collective-permute-start.4) | collective-permute-done | bytes 466976 | tf_op jit(solution)/shard_map/ppermute | solution.py:712
  76.5 17.0 %collective-permute-done = bf16[544,768]{1,0:T(8,128)(2,1)} collective-permute-done((bf16[544,768]{1,0:T(8,128)(2,1)}, bf16[544,768]{1,0:T(8,128)(2,1)}, u32[]{:S(2)}, u32[]{:S(2)}) %collective-permute-start) | collective-permute-done | bytes 835616 | tf_op jit(solution)/shard_map/ppermute | solution.py:838
  102.4 10.1 %fusion.q_ref.k_ref.v_ref = bf16[1088,2304]{1,0:T(8,128)(2,1)} fusion(f32[2304]{0:T(1024)S(1)} %pad_maximum_fusion.14, bf16[768,2432]{1,0:T(8,128)(2,1)} %bitcast.232, f32[768]{0:T(1024)S(1)} %reshape.294, f32[768]{0:T(1024)S(1)} %reshape.293, f32[1088]{0:T(1024)S(1)} %add_rsqrt_fusion.1, f32[1088]{0:T(1024)S(1)} %broadcast_multiply_fusion.5, ...), kind=kOutput, calls=%fused_computation.9 | convolution fusion | flops 3866247168 | bytes 10247680 | tf_op jit(solution)/shard_map/dot_general | solution.py:912
  113.5 36.2 %attend_forward.1 = (bf16[1088,768]{1,0:T(8,128)(2,1)}, f32[12,1,1088]{2,1,0:T(1,128)}, f32[256,256]{1,0:T(8,128)}, f32[512,256]{1,0:T(8,128)}, f32[768,256]{1,0...) custom-call(bf16[1088,2304]{1,0:T(8,128)(2,1)} %fusion.q_ref.k_ref.v_ref, bf16[1088,2304]{1,0:T(8,128)(2,1)} %fusion.q_ref.k_ref.v_ref, ...), custom_call_target="tpu_custom_call" | custom-call | tf_op jit(solution)/shard_map/attend_forward/pallas_call | solution.py:633
  156.3 3.1 fusion.39
  159.4 4.7 %slice.324 = bf16[32,96,768]{2,1,0:T(8,128)(2,1)S(1)} slice(bf16[32,216,768]{2,1,0:T(8,128)(2,1)} %bitcast.223), slice={[0:32], [120:216], [0:768]} | slice | bytes 9437184 | tf_op jit(solution)/shard_map/slice | solution.py:905
  167.8 14.9 %add_convert_fusion = (bf16[1088,3072]{1,0:T(8,128)(2,1)}, bf16[1088,3072]{1,0:T(8,128)(2,1)}) fusion(f32[3072]{0:T(1024)S(1)} %copy-done.55, bf16[1088,768]{1,0:T(8,128)(2,1)S(1)} %add_convert_fusion.1, bf16[768,768]{1,0:T(8,128)(2,1)S(1)} %bitcast.238, bf16[768,768]{1,0:T(8,128)(2,1)S(1)} %bitcast.240, bf16[768,768]{1,0:T(8,128)(2,1)S(1)} %bitcast.242, ...), kind=kOutput, calls=%fused_computation.4 | convolution fusion | flops 5209522176 | bytes 19771392 | tf_op jit(solution)/shard_map/dot_general | solution.py:920
  182.7 7.7 %fusion.1 = bf16[1088,3072]{1,0:T(8,128)(2,1)S(1)} fusion(bf16[1088,3072]{1,0:T(8,128)(2,1)} %get-tuple-element.50, bf16[3072,768]{1,0:T(8,128)(2,1)S(1)} %bitcast.228, bf16[64,768]{1,0:T(8,128)(2,1)S(1)} %copy-done.41, bf16[64,768]{1,0:T(8,128)(2,1)S(1)} %copy-done.39, bf16[480,768]{1,0:T(8,128)(2,1)S(1)} %copy-done.19, bf16[480,768]{1,0:T(8,128)(2,1)S(1)} %copy-done.17), kind=kOutput, calls=%fused_computation.10 | convolution fusion | flops 5150539776 | bytes 19759104 | tf_op jit(solution)/shard_map/re,de->rd/dot_general | solution.py:927
  190.4 6.7 %convolution_convert_fusion.2 = bf16[768,3072]{1,0:T(8,128)(2,1)S(1)} fusion(bf16[1088,768]{1,0:T(8,128)(2,1)S(1)} %add_convert_fusion.1, bf16[1088,3072]{1,0:T(8,128)(2,1)S(1)} %fusion.1), kind=kOutput, calls=%fused_computation.13 | convolution fusion | flops 5136187392 | bytes 13074432 | tf_op jit(solution)/shard_map/rd,re->de/dot_general | solution.py:924
  200.7 7.3 %convolution_convert_fusion.1 = bf16[3072,768]{1,0:T(8,128)(2,1)S(1)} fusion(bf16[1088,3072]{1,0:T(8,128)(2,1)S(1)} %copy-done.60, bf16[64,768]{1,0:T(8,128)(2,1)S(1)} %copy-done.42, bf16[64,768]{1,0:T(8,128)(2,1)S(1)} %copy-done.39, bf16[480,768]{1,0:T(8,128)(2,1)S(1)} %copy-done.20, bf16[480,768]{1,0:T(8,128)(2,1)S(1)} %copy-done.17), kind=kOutput, calls=%fused_computation.12 | convolution fusion | flops 5142872064 | bytes 13074432 | tf_op jit(solution)/shard_map/rd,re->de/dot_general | solution.py:924
  211.4 2.5 constant_dynamic-update-slice_fusion.2
  213.9 11.2 %multiply_reduce_fusion = (f32[768]{0:T(1024)}, f32[1088]{0:T(1024)S(1)}, f32[1088]{0:T(1024)S(1)}, f32[768]{0:T(1024)}, f32[1088,768]{1,0:T(8,128)S(1)}) fusion(f32[1088,768]{1,0:T(8,128)S(1)} %get-tuple-element.196, f32[1088]{0:T(1024)S(1)} %add_rsqrt_fusion, f32[1088]{0:T(1024)S(1)} %broadcast_multiply_fusion.4, f32[768]{0:T(1024)} %reshape.296, ...), kind=kOutput, calls=%fused_computation.41 | convolution fusion | flops 5160218624 | bytes 18114560 | tf_op jit(solution)/shard_map/re,de->rd/dot_general | solution.py:927
  225.2 3.6 convert_reduce_fusion.3
  228.7 2.7 convolution_convert_fusion.3.g_ref
  231.5 39.4 %attend_backward.1 = bf16[1088,2304]{1,0:T(8,128)(2,1)} custom-call(bf16[1088,2304]{1,0:T(8,128)(2,1)} %fusion.q_ref.k_ref.v_ref, bf16[1088,2304]{1,0:T(8,128)(2,1)} %fusion.q_ref.k_ref.v_ref, bf16[1088,2304]{1,0:T(8,128)(2,1)} %fusion.q_ref.k_ref.v_ref, bf16[1088,768]{1,0:T(8,128)(2,1)} %convolution_convert_fusion.3.g_ref, ...), custom_call_target="tpu_custom_call" | custom-call | tf_op jit(solution)/shard_map/attend_backward/pallas_call | solution.py:663
  270.9 8.8 %fusion.13 = (f32[1088]{0:T(1024)S(1)}, f32[768]{0:T(1024)S(1)}, f32[1088]{0:T(1024)S(1)}, f32[768]{0:T(1024)S(1)}, f32[1088,768]{1,0:T(8,128)S(1)}) fusion(f32[768]{0:T(1024)} %copy-done.50, f32[1088]{0:T(1024)S(1)} %copy-done.49, f32[1088]{0:T(1024)S(1)} %copy-done.45, bf16[64,768]{1,0:T(8,128)(2,1)S(1)} %get-tuple-element.162, ...), kind=kOutput, calls=%fused_computation.36 | convolution fusion | flops 3864572416 | bytes 13593600 | tf_op jit(solution)/shard_map/re,de->rd/dot_general | solution.py:927
  280.4 4.6 %convert_reduce_fusion = f32[3072]{0:T(1024)} fusion(bf16[1088,3072]{1,0:T(8,128)(2,1)} %copy-done.11), kind=kLoop, calls=%fused_computation.3 | loop fusion | flops 6681600 | bytes 6696960 | tf_op jit(solution)/shard_map/reduce_sum | solution.py:930
  289.1 4.2 fusion.16
  296.8 8.0 %convolution_convert_fusion = bf16[768,2304]{1,0:T(8,128)(2,1)S(1)} fusion(bf16[1088,2304]{1,0:T(8,128)(2,1)} %attend_backward.1, f32[768]{0:T(1024)} %copy-done.56, f32[768]{0:T(1024)} %copy-done.50, f32[1088]{0:T(1024)S(1)} %copy-done.49, f32[1088]{0:T(1024)S(1)} %copy-done.45, bf16[64,768]{1,0:T(8,128)(2,1)S(1)} %get-tuple-element.162, ...), kind=kOutput, calls=%fused_computation.11 | convolution fusion | flops 3863003136 | bytes 10238464 | tf_op jit(solution)/shard_map/rd,re->de/dot_general | solution.py:924
  305.8 9.9 %fusion.9 = bf16[1088,768]{1,0:T(8,128)(2,1)S(1)} fusion(f32[1088,768]{1,0:T(8,128)S(1)} %get-tuple-element.196, bf16[1088,3072]{1,0:T(8,128)(2,1)} %get-tuple-element.61, bf16[3072,768]{1,0:T(8,128)(2,1)} %bitcast.229, f32[768]{0:T(1024)S(1)} %copy-done.57), kind=kOutput, calls=%fused_computation.31 | convolution fusion | flops 5136334848 | bytes 16419840 | tf_op jit(solution)/shard_map/dot_general | solution.py:950
  325.2 45.4 %collective-permute-done.12 = bf16[4,24,768]{2,1,0:T(8,128)(2,1)S(1)} collective-permute-done((bf16[4,24,768]{2,1,0:T(8,128)(2,1)S(1)}, bf16[4,24,768]{2,1,0:T(8,128)(2,1)S(1)}, u32[]{:S(2)}, u32[]{:S(2)}) %collective-permute-start.12) | collective-permute-done | bytes 147488 | tf_op jit(solution)/shard_map/ppermute | solution.py:712
  378.8 4.1 collective-permute-done.23
  383.6 3.3 collective-permute-done.22
  387.6 4.5 collective-permute-done.15
  394.2 8.6 %collective-permute-done.17 = bf16[4,24,2432]{2,1,0:T(8,128)(2,1)S(1)} collective-permute-done((bf16[4,24,2432]{2,1,0:T(8,128)(2,1)S(1)}, bf16[4,24,2432]{2,1,0:T(8,128)(2,1)S(1)}, u32[]{:S(2)}, u32[]{:S(2)}) %collective-permute-start.17) | collective-permute-done | bytes 466976 | tf_op jit(solution)/shard_map/ppermute | solution.py:712
  403.1 3.2 collective-permute-start.21
  412.7 7.1 %collective-permute-done.20 = bf16[24,2432]{1,0:T(8,128)(2,1)S(1)} collective-permute-done((bf16[24,2432]{1,0:T(8,128)(2,1)S(1)}, bf16[24,2432]{1,0:T(8,128)(2,1)S(1)}, u32[]{:S(2)}, u32[]{:S(2)}) %collective-permute-start.20) | collective-permute-done | bytes 116768 | tf_op jit(solution)/shard_map/ppermute | solution.py:712
  424.6 22.8 %reduce-scatter.2.cloned.1.call-done = bf16[1,192,768]{2,1,0:T(8,128)(2,1)} async-done(((bf16[32,192,768]{2,1,0:T(8,128)(2,1)}), bf16[1,192,768]{2,1,0:T(8,128)(2,1)}) %reduce-scatter.2.cloned.1.call-update) | async-done | bytes 294928 | tf_op jit(solution)/shard_map/reduce_scatter | solution.py:945
  (283 shorter events, 94.8 us)
Async XLA Ops:
  7.2 35.3 %copy-start.34 = (bf16[2,1,1,64,768]{4,3,2,1,0:T(8,128)(2,1)S(1)}, bf16[2,1,1,64,768]{4,3,2,1,0:T(8,128)(2,1)}, u32[]{:S(2)}) copy-start(bf16[2,1,1,64,768]{4,3,2,1,0:T(8,128)(2,1)} %param.17) | copy-start | bytes 589828
  7.2 35.3 %copy-start.12 = (bf16[2,1,480,768]{3,2,1,0:T(8,128)(2,1)S(1)}, bf16[2,1,480,768]{3,2,1,0:T(8,128)(2,1)}, u32[]{:S(2)}) copy-start(bf16[2,1,480,768]{3,2,1,0:T(8,128)(2,1)} %param.16) | copy-start | bytes 4423684
  7.2 149.1 %all-gather.3.cloned.1.call-start = ((), (), s32[]{:S(2)}) async-start(), calls=%async_computation.2 | async-start | bytes 10948608 | tf_op jit(solution)/shard_map/all_gather | solution.py:895
  12.9 434.5 %reduce-scatter.2.cloned.1.call-start = ((), (), s32[]{:S(2)}) async-start(), calls=%async_computation.1 | async-start | bytes 9732096 | tf_op jit(solution)/shard_map/reduce_scatter | solution.py:945
  16.6 9.3 %collective-permute-start.1 = (bf16[24,2432]{1,0:T(8,128)(2,1)S(1)}, bf16[24,2432]{1,0:T(8,128)(2,1)S(1)}, u32[]{:S(2)}, u32[]{:S(2)}) collective-permute-start(bf16[24,2432]{1,0:T(8,128)(2,1)S(1)} %fusion.29), channel_id=1, source_target_pairs={{0,24},{1,25},{2,26},{3,27},{4,28},{5,29},{6,30},{7,31},{8,16},{9,... | collective-permute-start | bytes 350216 | tf_op jit(solution)/shard_map/ppermute | solution.py:712
  21.7 15.4 %collective-permute-start.2 = (bf16[24,2432]{1,0:T(8,128)(2,1)S(1)}, bf16[24,2432]{1,0:T(8,128)(2,1)S(1)}, u32[]{:S(2)}, u32[]{:S(2)}) collective-permute-start(bf16[24,2432]{1,0:T(8,128)(2,1)S(1)} %fusion.29), channel_id=1, source_target_pairs={{0,16},{1,17},{2,18},{3,19},{4,20},{5,21},{6,22},{7,23},{8,24},{9,... | collective-permute-start | bytes 350216 | tf_op jit(solution)/shard_map/ppermute | solution.py:712
  21.7 15.4 %collective-permute-start.3 = (bf16[24,2432]{1,0:T(8,128)(2,1)S(1)}, bf16[24,2432]{1,0:T(8,128)(2,1)S(1)}, u32[]{:S(2)}, u32[]{:S(2)}) collective-permute-start(bf16[24,2432]{1,0:T(8,128)(2,1)S(1)} %fusion.29), channel_id=1, source_target_pairs={{0,8},{1,9},{2,10},{3,11},{4,12},{5,13},{6,14},{7,15},{8,0},{9,1},... | collective-permute-start | bytes 350216 | tf_op jit(solution)/shard_map/ppermute | solution.py:712
  39.0 19.7 %collective-permute-start.5 = (bf16[4,24,2432]{2,1,0:T(8,128)(2,1)}, bf16[4,24,2432]{2,1,0:T(8,128)(2,1)S(1)}, u32[]{:S(2)}, u32[]{:S(2)}) collective-permute-start(bf16[4,24,2432]{2,1,0:T(8,128)(2,1)} %pad_maximum_fusion.12), channel_id=1, source_target_pairs={{0,4},{1,5},{2,6},{3,7},{4,0},{5,1},{6,2},{7,3},{8,12},{9,13},{10,... | collective-permute-start | bytes 1400840 | tf_op jit(solution)/shard_map/ppermute | solution.py:712
  40.3 29.9 %collective-permute-start.4 = (bf16[4,24,2432]{2,1,0:T(8,128)(2,1)}, bf16[4,24,2432]{2,1,0:T(8,128)(2,1)S(1)}, u32[]{:S(2)}, u32[]{:S(2)}) collective-permute-start(bf16[4,24,2432]{2,1,0:T(8,128)(2,1)} %pad_maximum_fusion.12), channel_id=1, source_target_pairs={{0,5},{1,4},{2,7},{3,6},{4,1},{5,0},{6,3},{7,2},{8,13},{9,12},{10,... | collective-permute-start | bytes 1400840 | tf_op jit(solution)/shard_map/ppermute | solution.py:712
  41.8 28.5 %collective-permute-start.6 = (bf16[4,24,2432]{2,1,0:T(8,128)(2,1)}, bf16[4,24,2432]{2,1,0:T(8,128)(2,1)S(1)}, u32[]{:S(2)}, u32[]{:S(2)}) collective-permute-start(bf16[4,24,2432]{2,1,0:T(8,128)(2,1)} %pad_maximum_fusion.12), channel_id=1, source_target_pairs={{0,1},{1,0},{2,3},{3,2},{4,5},{5,4},{6,7},{7,6},{8,9},{9,8},{10,11... | collective-permute-start | bytes 1400840 | tf_op jit(solution)/shard_map/ppermute | solution.py:712
  43.5 50.0 %collective-permute-start = (bf16[544,768]{1,0:T(8,128)(2,1)}, bf16[544,768]{1,0:T(8,128)(2,1)}, u32[]{:S(2)}, u32[]{:S(2)}) collective-permute-start(bf16[544,768]{1,0:T(8,128)(2,1)} %pad_maximum_fusion.6), channel_id=1, source_target_pairs={{0,1},{1,0},{2,3},{3,2},{4,5},{5,4},{6,7},{7,6},{8,9},{9,8},{10,11... | collective-permute-start | bytes 2506760 | tf_op jit(solution)/shard_map/ppermute | solution.py:838
  74.9 22.4 %collective-permute-start.7 = (bf16[4,2,2,24,2432]{4,3,2,1,0:T(8,128)(2,1)}, bf16[4,2,2,24,2432]{4,3,2,1,0:T(8,128)(2,1)}, u32[]{:S(2)}, u32[]{:S(2)}) collective-permute-start(bf16[4,2,2,24,2432]{4,3,2,1,0:T(8,128)(2,1)} %pad_maximum_fusion.3), channel_id=1, source_target_pairs={{0,2},{1,3},{2,0},{3,1},{4,6},{5,7},{6,4},{7,5},{8,10},{9,11},{10,... | collective-permute-start | bytes 5603336 | tf_op jit(solution)/shard_map/ppermute | solution.py:712
  112.5 40.9 %collective-permute-start.8 = (bf16[544,768]{1,0:T(8,128)(2,1)S(1)}, bf16[544,768]{1,0:T(8,128)(2,1)S(1)}, u32[]{:S(2)}, u32[]{:S(2)}) collective-permute-start(bf16[544,768]{1,0:T(8,128)(2,1)S(1)} %copy-done.33), channel_id=1, source_target_pairs={{0,1},{1,0},{2,3},{3,2},{4,5},{5,4},{6,7},{7,6},{8,9},{9,8},{10,11... | collective-permute-start | bytes 2506760 | tf_op jit(solution)/shard_map/ppermute | solution.py:838
  113.5 41.5 %copy-start.14 = (bf16[2,1,480,768]{3,2,1,0:T(8,128)(2,1)S(1)}, bf16[2,1,480,768]{3,2,1,0:T(8,128)(2,1)}, u32[]{:S(2)}) copy-start(bf16[2,1,480,768]{3,2,1,0:T(8,128)(2,1)} %param.18) | copy-start | bytes 4423684
  231.5 39.4 %copy-start.45 = (f32[1088]{0:T(1024)S(1)}, f32[1088]{0:T(1024)}, u32[]{:S(2)}) copy-start(f32[1088]{0:T(1024)} %copy-done.44) | copy-start | bytes 13060
  231.5 39.4 %copy-start.49 = (f32[1088]{0:T(1024)S(1)}, f32[1088]{0:T(1024)}, u32[]{:S(2)}) copy-start(f32[1088]{0:T(1024)} %copy-done.48) | copy-start | bytes 13060
  305.3 18.0 %collective-permute-start.9 = (bf16[4,2,2,24,2432]{4,3,2,1,0:T(8,128)(2,1)S(1)}, bf16[4,2,2,24,2432]{4,3,2,1,0:T(8,128)(2,1)S(1)}, u32[]{:S(2)}, u32[]{:S(2)}) collective-permute-start(bf16[4,2,2,24,2432]{4,3,2,1,0:T(8,128)(2,1)S(1)} %dynamic-slice_bitcast_fusion), channel_id=1, source_target_pairs={{0,2},{1,3},{2,0},{3,1},{4,6},{5,7},{6,4},{7,5},{8,10},{9,11},{10,... | collective-permute-start | bytes 5603336 | tf_op jit(solution)/shard_map/ppermute | solution.py:712
  317.7 53.0 %collective-permute-start.10 = (bf16[544,768]{1,0:T(8,128)(2,1)S(1)}, bf16[544,768]{1,0:T(8,128)(2,1)S(1)}, u32[]{:S(2)}, u32[]{:S(2)}) collective-permute-start(bf16[544,768]{1,0:T(8,128)(2,1)S(1)} %pad_maximum_fusion.8), channel_id=1, source_target_pairs={{0,1},{1,0},{2,3},{3,2},{4,5},{5,4},{6,7},{7,6},{8,9},{9,8},{10,11... | collective-permute-start | bytes 2506760 | tf_op jit(solution)/shard_map/ppermute | solution.py:862
  318.9 2.3 collective-permute-start.11
  319.2 68.3 %collective-permute-start.18 = (bf16[544,768]{1,0:T(8,128)(2,1)S(1)}, bf16[544,768]{1,0:T(8,128)(2,1)S(1)}, u32[]{:S(2)}, u32[]{:S(2)}) collective-permute-start(bf16[544,768]{1,0:T(8,128)(2,1)S(1)} %pad_maximum_fusion.9), channel_id=1, source_target_pairs={{0,1},{1,0},{2,3},{3,2},{4,5},{5,4},{6,7},{7,6},{8,9},{9,8},{10,11... | collective-permute-start | bytes 2506760 | tf_op jit(solution)/shard_map/ppermute | solution.py:862
  321.4 49.3 %collective-permute-start.12 = (bf16[4,24,768]{2,1,0:T(8,128)(2,1)S(1)}, bf16[4,24,768]{2,1,0:T(8,128)(2,1)S(1)}, u32[]{:S(2)}, u32[]{:S(2)}) collective-permute-start(bf16[4,24,768]{2,1,0:T(8,128)(2,1)S(1)} %get-tuple-element.171), channel_id=1, source_target_pairs={{0,1},{1,0},{2,3},{3,2},{4,5},{5,4},{6,7},{7,6},{8,9},{9,8},{10,11... | collective-permute-start | bytes 442376 | tf_op jit(solution)/shard_map/ppermute | solution.py:712
  322.3 48.4 %collective-permute-start.13 = (bf16[4,24,768]{2,1,0:T(8,128)(2,1)S(1)}, bf16[4,24,768]{2,1,0:T(8,128)(2,1)S(1)}, u32[]{:S(2)}, u32[]{:S(2)}) collective-permute-start(bf16[4,24,768]{2,1,0:T(8,128)(2,1)S(1)} %get-tuple-element.170), channel_id=1, source_target_pairs={{0,4},{1,5},{2,6},{3,7},{4,0},{5,1},{6,2},{7,3},{8,12},{9,13},{10,... | collective-permute-start | bytes 442376 | tf_op jit(solution)/shard_map/ppermute | solution.py:712
  323.3 47.3 %collective-permute-start.14 = (bf16[4,24,768]{2,1,0:T(8,128)(2,1)S(1)}, bf16[4,24,768]{2,1,0:T(8,128)(2,1)S(1)}, u32[]{:S(2)}, u32[]{:S(2)}) collective-permute-start(bf16[4,24,768]{2,1,0:T(8,128)(2,1)S(1)} %get-tuple-element.169), channel_id=1, source_target_pairs={{0,5},{1,4},{2,7},{3,6},{4,1},{5,0},{6,3},{7,2},{8,13},{9,12},{10,... | collective-permute-start | bytes 442376 | tf_op jit(solution)/shard_map/ppermute | solution.py:712
  370.8 6.8 %collective-permute-start.24 = (bf16[24,768]{1,0:T(8,128)(2,1)S(1)}, bf16[24,768]{1,0:T(8,128)(2,1)S(1)}, u32[]{:S(2)}, u32[]{:S(2)}) collective-permute-start(bf16[24,768]{1,0:T(8,128)(2,1)S(1)} %get-tuple-element.193), channel_id=1, source_target_pairs={{0,24},{1,25},{2,26},{3,27},{4,28},{5,29},{6,30},{7,31},{8,16},{9,... | collective-permute-start | bytes 110600 | tf_op jit(solution)/shard_map/ppermute | solution.py:712
  371.9 20.2 %collective-permute-start.15 = (bf16[4,24,2432]{2,1,0:T(8,128)(2,1)S(1)}, bf16[4,24,2432]{2,1,0:T(8,128)(2,1)S(1)}, u32[]{:S(2)}, u32[]{:S(2)}) collective-permute-start(bf16[4,24,2432]{2,1,0:T(8,128)(2,1)S(1)} %get-tuple-element.145), channel_id=1, source_target_pairs={{0,1},{1,0},{2,3},{3,2},{4,5},{5,4},{6,7},{7,6},{8,9},{9,8},{10,11... | collective-permute-start | bytes 1400840 | tf_op jit(solution)/shard_map/ppermute | solution.py:712
  373.6 20.7 %collective-permute-start.16 = (bf16[4,24,2432]{2,1,0:T(8,128)(2,1)S(1)}, bf16[4,24,2432]{2,1,0:T(8,128)(2,1)S(1)}, u32[]{:S(2)}, u32[]{:S(2)}) collective-permute-start(bf16[4,24,2432]{2,1,0:T(8,128)(2,1)S(1)} %get-tuple-element.144), channel_id=1, source_target_pairs={{0,4},{1,5},{2,6},{3,7},{4,0},{5,1},{6,2},{7,3},{8,12},{9,13},{10,... | collective-permute-start | bytes 1400840 | tf_op jit(solution)/shard_map/ppermute | solution.py:712
  375.0 27.8 %collective-permute-start.17 = (bf16[4,24,2432]{2,1,0:T(8,128)(2,1)S(1)}, bf16[4,24,2432]{2,1,0:T(8,128)(2,1)S(1)}, u32[]{:S(2)}, u32[]{:S(2)}) collective-permute-start(bf16[4,24,2432]{2,1,0:T(8,128)(2,1)S(1)} %get-tuple-element.143), channel_id=1, source_target_pairs={{0,5},{1,4},{2,7},{3,6},{4,1},{5,0},{6,3},{7,2},{8,13},{9,12},{10,... | collective-permute-start | bytes 1400840 | tf_op jit(solution)/shard_map/ppermute | solution.py:712
  377.6 5.3 %collective-permute-start.23 = (bf16[24,768]{1,0:T(8,128)(2,1)S(1)}, bf16[24,768]{1,0:T(8,128)(2,1)S(1)}, u32[]{:S(2)}, u32[]{:S(2)}) collective-permute-start(bf16[24,768]{1,0:T(8,128)(2,1)S(1)} %get-tuple-element.194), channel_id=1, source_target_pairs={{0,16},{1,17},{2,18},{3,19},{4,20},{5,21},{6,22},{7,23},{8,24},{9,... | collective-permute-start | bytes 110600 | tf_op jit(solution)/shard_map/ppermute | solution.py:712
  382.9 4.0 collective-permute-start.22
  403.1 9.6 %collective-permute-start.21 = (bf16[24,2432]{1,0:T(8,128)(2,1)S(1)}, bf16[24,2432]{1,0:T(8,128)(2,1)S(1)}, u32[]{:S(2)}, u32[]{:S(2)}) collective-permute-start(bf16[24,2432]{1,0:T(8,128)(2,1)S(1)} %get-tuple-element.174), channel_id=1, source_target_pairs={{0,24},{1,25},{2,26},{3,27},{4,28},{5,29},{6,30},{7,31},{8,16},{9,... | collective-permute-start | bytes 350216 | tf_op jit(solution)/shard_map/ppermute | solution.py:712
  406.3 13.5 %collective-permute-start.20 = (bf16[24,2432]{1,0:T(8,128)(2,1)S(1)}, bf16[24,2432]{1,0:T(8,128)(2,1)S(1)}, u32[]{:S(2)}, u32[]{:S(2)}) collective-permute-start(bf16[24,2432]{1,0:T(8,128)(2,1)S(1)} %get-tuple-element.175), channel_id=1, source_target_pairs={{0,16},{1,17},{2,18},{3,19},{4,20},{5,21},{6,22},{7,23},{8,24},{9,... | collective-permute-start | bytes 350216 | tf_op jit(solution)/shard_map/ppermute | solution.py:712
  406.3 16.0 %collective-permute-start.19 = (bf16[24,2432]{1,0:T(8,128)(2,1)S(1)}, bf16[24,2432]{1,0:T(8,128)(2,1)S(1)}, u32[]{:S(2)}, u32[]{:S(2)}) collective-permute-start(bf16[24,2432]{1,0:T(8,128)(2,1)S(1)} %get-tuple-element.173), channel_id=1, source_target_pairs={{0,8},{1,9},{2,10},{3,11},{4,12},{5,13},{6,14},{7,15},{8,0},{9,1},... | collective-permute-start | bytes 350216 | tf_op jit(solution)/shard_map/ppermute | solution.py:712
  (56 other events, 398.9 us)
Sparse Core Ops, SparseCore 0:
  13.0 102.6 all-gather.2
  297.0 150.4 reduce-scatter.1
